TPU v7x, 128 devices: a whole 4x4x4 slice. The times are simulated.
128 devices in a mesh: ty: 4 (over y), tx: 32 (over z, x, core).
Axes of the slice: x: 4, y: 4, z: 4, core: 2. Of those that a mesh axis runs over, the one named last changes fastest.
Arguments:
- block_sums: float32 [16384, 1, 1024], P(('ty', 'tx')), may hold values from -6 to 6
- block_weights: float32 [16384, 1, 1024], P(('ty', 'tx')), may hold values from 0.1 to 2
- block_tile: int32 [16384, 1], P(('ty', 'tx')), may hold values from 0 to 127; in each aligned block of 128 rows (0 to 127, 128 to 255, ...) at most 2 rows name the same one
- block_row: int32 [16384], P(('ty', 'tx')), may hold values from 0 to 127
- prior_weight: float32 [512, 32768], P('ty', 'tx'), may hold values from 0.1 to 1
Outputs:
- solution_field: float32 [512, 32768], P('ty', 'tx')
- residual: float32 [512, 32768], P('ty', 'tx')
Inputs may be any that keep to these rules, and one draw needn't show every extreme that they name: `block_tile`: among the 128 blocks of one log shard no tile is named more than 2 times, a bound that some block reaches.
All inputs are finite; a program needn't handle non-finite values.
Results may differ from a plain program's by a relative error of at most 0.0003.
Values sent between devices are 32-bit elements; how exact they have to be, the bound alone decides.
No kernel may reach another device: no remote copies, remote signals or barrier semaphores. Data moves between devices by JAX's collectives and lax.ppermute only.
A program may use at most 64 MiB of HBM per device.

v0:
```python
import functools

import jax
import jax.numpy as jnp
from jax import lax
from jax.sharding import Mesh
from jax.sharding import PartitionSpec as P

HALF = 32
ITERS = 2
TY_TX = ("ty", "tx_0", "tx_1", "tx_2")
TX = ("tx_0", "tx_1", "tx_2")


def over_axes(shard, axes):
    return functools.reduce(lax.psum, axes, shard)


def side_by_side(arrays, axis, split_dim, concat_dim, along):
    ends, at = ([], 0)
    for a in arrays[:-1]:
        at += a.shape[along]
        ends.append(at)
    both = jnp.concatenate(arrays, axis=along)
    return tuple(
        jnp.split(
            lax.all_to_all(both, axis, split_axis=split_dim, concat_axis=concat_dim, tiled=True),
            ends,
            axis=along,
        )
    )


def padded_2(block, sides, width):
    for axis, dim in sides:
        count = lax.axis_size(axis)
        forward = [(i, i + 1) for i in range(count - 1)]
        backward = [(target, source) for source, target in forward]
        low = lax.ppermute(
            lax.slice_in_dim(block, block.shape[dim] - width, None, axis=dim), axis, forward
        )
        high = lax.ppermute(lax.slice_in_dim(block, 0, width, axis=dim), axis, backward)
        block = jnp.concatenate([low, block, high], axis=dim)
    return block


def band_matrix(size, transpose):
    outer = jnp.arange(size + 2 * HALF)[:, None]
    inner = jnp.arange(size)[None, :]
    offset = (outer - inner - HALF).astype(jnp.float32)
    dist = jnp.abs(jnp.arange(-HALF, HALF + 1).astype(jnp.float32))
    scaled_all = dist / (HALF + 1.0)
    total = jnp.sum((1.0 - scaled_all) ** 4 * (1.0 + 4.0 * scaled_all))
    scaled = jnp.abs(offset) / (HALF + 1.0)
    values = (
        jnp.where(jnp.abs(offset) <= HALF, (1.0 - scaled) ** 4 * (1.0 + 4.0 * scaled), 0.0) / total
    )
    if transpose:
        return values.T
    return values


def paired(residual, image):
    return (
        over_axes(jnp.sum(residual * residual), TY_TX),
        over_axes(jnp.sum(residual * image), TY_TX),
    )


def shards(block_sums, block_weights, block_tile, block_row, prior_weight):
    devices = lax.axis_size(TY_TX)
    blocks, band, cols = block_sums.shape
    rows = prior_weight.shape[0]
    slots = 2 * blocks // devices
    target = block_tile[:, 0]
    owners = (target[:, None] == jnp.arange(devices, dtype=jnp.int32)[None, :]).astype(jnp.int32)
    rank = jnp.sum((jnp.cumsum(owners, axis=0) - 1) * owners, axis=1)
    position = target * slots + rank
    send_sums = jnp.zeros((devices * slots, band, cols), jnp.float32).at[position].set(block_sums)
    send_weights = (
        jnp.zeros((devices * slots, band, cols), jnp.float32).at[position].set(block_weights)
    )
    send_rows = jnp.zeros((devices * slots,), jnp.int32).at[position].set(block_row)
    got_sums, got_weights, got_rows = (
        *side_by_side(
            (
                send_sums.reshape(devices, slots, band, cols),
                send_weights.reshape(devices, slots, band, cols),
            ),
            TY_TX,
            0,
            0,
            1,
        ),
        lax.all_to_all(
            send_rows.reshape(devices, slots), TY_TX, split_axis=0, concat_axis=0, tiled=True
        ),
    )
    received = devices * slots
    got_rows = got_rows.reshape(received)
    select = (jnp.arange(rows // band, dtype=jnp.int32)[:, None] == got_rows[None, :]).astype(
        jnp.float32
    )
    cell_sums = jnp.dot(
        select, got_sums.reshape(received, band * cols), precision=lax.Precision.HIGHEST
    )
    cell_weights = jnp.dot(
        select, got_weights.reshape(received, band * cols), precision=lax.Precision.HIGHEST
    )
    root = jnp.sqrt(prior_weight + cell_weights)
    right_side = cell_sums / root
    col_band = band_matrix(cols, False)
    row_band = band_matrix(rows, True)

    def operate(field):
        padded = padded_2(root * field, (("ty", 0), (TX, 1)), HALF)
        across = jnp.dot(padded, col_band, precision=lax.Precision.HIGHEST)
        smoothed = jnp.dot(row_band, across, precision=lax.Precision.HIGHEST)
        return 0.5 * field + root * smoothed

    solution_field = jnp.zeros_like(right_side)
    residual = right_side
    image = operate(residual)
    norm_now, product = paired(residual, image)
    alpha = norm_now / product
    direction, along = (residual, image)
    for step in range(ITERS):
        solution_field = solution_field + alpha * direction
        residual = residual - alpha * along
        if step + 1 < ITERS:
            image = operate(residual)
            norm_next, product = paired(residual, image)
            ratio = norm_next / norm_now
            alpha = norm_next / (product - ratio * norm_next / alpha)
            direction = residual + ratio * direction
            along = image + ratio * along
            norm_now = norm_next
    return (solution_field, residual)


def solution(mesh):
    split = Mesh(mesh.devices.reshape(mesh.shape["ty"], 4, 4, 2), ("ty", "tx_0", "tx_1", "tx_2"))
    in_specs = (P(TY_TX, None, None), P(TY_TX, None, None), P(TY_TX, None), P(TY_TX), P("ty", TX))
    out_specs = (P("ty", TX), P("ty", TX))
    return jax.shard_map(
        shards, mesh=split, in_specs=in_specs, out_specs=out_specs, check_vma=False
    )
```

profile of v0, /device:TPU:1, one launch (start us, length us, event | category | flops | bytes accessed | tf_op | source)
XLA Modules:
  0.0 194.7 jit_solution(1892672509831383829)
XLA Ops:
  0.6 0.8 fusion.17
  1.6 0.8 select_reduce_fusion
  2.4 0.7 fusion.18
  3.1 1.1 scatter_custom_fusion
  4.2 0.8 all_to_all.9
  5.0 11.5 %all-to-all-start = ((s32[128,1,2]{2,1,0:T(1,128)}), s32[128,1,2]{2,1,0:T(1,128)S(1)}, u32[]{:S(2)}, u32[]{:S(2)}) async-start(s32[128,1,2]{2,1,0:T(1,128)} %bitcast.3), calls=%async_computation | async-start | bytes 131072 | tf_op jit(solution)/shard_map/all_to_all | solution.py:95
  16.5 1.9 scatter_custom_fusion.1
  18.4 0.6 reshape.23
  19.0 1.4 scatter_custom_fusion.2
  20.4 0.6 reshape.24
  21.0 2.3 %pad_maximum_fusion = f32[128,4,1,1024]{3,1,2,0:T(4,128)} fusion(f32[128,2,1,1024]{3,1,2,0:T(2,128)S(1)} %reshape.24, f32[128,2,1,1024]{3,1,2,0:T(2,128)S(1)} %reshape.23), kind=kLoop, calls=%fused_computation.8 | loop fusion | flops 524288 | bytes 4194304 | tf_op jit(solution)/shard_map/concatenate | solution.py:24
  23.3 2.6 %all-to-all-done = s32[128,1,2]{2,1,0:T(1,128)S(1)} async-done(((s32[128,1,2]{2,1,0:T(1,128)}), s32[128,1,2]{2,1,0:T(1,128)S(1)}, u32[]{:S(2)}, u32[]{:S(2)}) %all-to-all-start) | async-done | bytes 1056 | tf_op jit(solution)/shard_map/all_to_all | solution.py:95
  25.9 7.2 %all-to-all-start.1 = ((f32[128,4,1,1024]{3,1,2,0:T(4,128)}), f32[128,4,1,1024]{3,1,2,0:T(4,128)S(1)}, u32[]{:S(2)}, u32[]{:S(2)}) async-start(f32[128,4,1,1024]{3,1,2,0:T(4,128)} %pad_maximum_fusion), calls=%async_computation.1 | async-start | bytes 4194304 | tf_op jit(solution)/shard_map/all_to_all | solution.py:27
  33.6 0.8 reduce.3
  34.6 29.1 %all-to-all-done.1 = f32[128,4,1,1024]{3,1,2,0:T(4,128)S(1)} async-done(((f32[128,4,1,1024]{3,1,2,0:T(4,128)}), f32[128,4,1,1024]{3,1,2,0:T(4,128)S(1)}, u32[]{:S(2)}, u32[]{:S(2)}) %all-to-all-start.1) | async-done | bytes 2097184 | tf_op jit(solution)/shard_map/all_to_all | solution.py:27
  63.6 1.8 fusion.46
  65.4 0.7 reshape.26
  66.6 0.7 reshape.25
  67.4 1.7 fusion.5
  69.6 1.3 collective-permute-start
  70.9 1.3 collective-permute-start.1
  72.2 0.6 collective-permute-done
  72.9 3.8 %collective-permute-done.1 = f32[32,1024]{1,0:T(8,128)S(1)} collective-permute-done((f32[32,1024]{1,0:T(8,128)S(1)}, f32[32,1024]{1,0:T(8,128)S(1)}, u32[]{:S(2)}, u32[]{:S(2)}) %collective-permute-start.1) | collective-permute-done | bytes 131104 | tf_op jit(solution)/shard_map/ppermute | solution.py:42
  76.8 4.2 %collective-permute-start.2 = (f32[192,32]{1,0:T(8,128)S(1)}, f32[192,32]{1,0:T(8,128)S(1)}, u32[]{:S(2)}, u32[]{:S(2)}) collective-permute-start(f32[192,32]{1,0:T(8,128)S(1)} %get-tuple-element.29), channel_id=1, source_target_pairs={{0,1},{1,2},{2,3},{3,4},{4,5},{5,6},{6,7},{7,8},{8,9},{9,10},{10,1... | collective-permute-start | bytes 73736 | tf_op jit(solution)/shard_map/ppermute | solution.py:39
  80.9 2.1 %collective-permute-start.3 = (f32[192,32]{1,0:T(8,128)S(1)}, f32[192,32]{1,0:T(8,128)S(1)}, u32[]{:S(2)}, u32[]{:S(2)}) collective-permute-start(f32[192,32]{1,0:T(8,128)S(1)} %get-tuple-element.28), channel_id=1, source_target_pairs={{1,0},{2,1},{3,2},{4,3},{5,4},{6,5},{7,6},{8,7},{9,8},{10,9},{11,1... | collective-permute-start | bytes 73736 | tf_op jit(solution)/shard_map/ppermute | solution.py:42
  83.1 0.6 multiply_reduce_fusion.4
  83.7 3.2 %collective-permute-done.3 = f32[192,32]{1,0:T(8,128)S(1)} collective-permute-done((f32[192,32]{1,0:T(8,128)S(1)}, f32[192,32]{1,0:T(8,128)S(1)}, u32[]{:S(2)}, u32[]{:S(2)}) %collective-permute-start.3) | collective-permute-done | bytes 24608 | tf_op jit(solution)/shard_map/ppermute | solution.py:42
  87.4 6.3 %fusion.2 = f32[192,1024]{1,0:T(8,128)S(1)} fusion(f32[192,1088]{1,0:T(8,128)S(1)} %concatenate.17, f32[]{:T(128)} %multiply_reduce_fusion.4), kind=kOutput, calls=%fused_computation.7 | convolution fusion | flops 2582511616 | bytes 1622020 | tf_op jit(solution)/shard_map/dot_general | solution.py:117
  93.7 2.1 %multiply_reduce_fusion.2 = (f32[]{:T(128)}, f32[]{:T(128)}, f32[128,1024]{1,0:T(8,128)S(1)}) fusion(f32[128,1024]{1,0:T(8,128)S(1)} %get-tuple-element.37, f32[128,1024]{1,0:T(8,128)S(1)} %fusion.5, f32[192,1024]{1,0:T(8,128)S(1)} %fusion.2, f32[]{:T(128)} %multiply_reduce_fusion.4), kind=kOutput, calls=%fused_computation.31 | convolution fusion | flops 303251456 | bytes 2359308 | tf_op jit(solution)/shard_map/dot_general | solution.py:118
  95.7 7.7 %all-reduce.5 = (f32[]{:T(128)}, f32[]{:T(128)}) all-reduce(f32[]{:T(128)} %get-tuple-element.5, f32[]{:T(128)} %get-tuple-element.4), channel_id=1, replica_groups=mesh['ty'=4,'tx_0'=4,'tx_1'=4,'tx_2'=2] {'ty'}, use_global_device_ids=true, to_apply=%region_6.7 | all-reduce | flops 2 | bytes 16 | tf_op jit(solution)/shard_map/psum | solution.py:16
  103.4 7.0 %all-reduce.3 = (f32[]{:T(128)}, f32[]{:T(128)}) all-reduce(f32[]{:T(128)} %get-tuple-element.16, f32[]{:T(128)} %get-tuple-element.17), channel_id=1, replica_groups=mesh['ty'=4,'tx_0'=4,'tx_1'=4,'tx_2'=2] {'tx_0'}, use_global_device_ids=true, to_apply=%region_7.8 | all-reduce | flops 2 | bytes 16 | tf_op jit(solution)/shard_map/psum | solution.py:16
  110.4 10.9 %all-reduce.1 = (f32[]{:T(128)}, f32[]{:T(128)}) all-reduce(f32[]{:T(128)} %get-tuple-element.12, f32[]{:T(128)} %get-tuple-element.13), channel_id=1, replica_groups=mesh['ty'=4,'tx_0'=4,'tx_1'=4,'tx_2'=2] {'tx_1'}, use_global_device_ids=true, to_apply=%region_8.9 | all-reduce | flops 2 | bytes 16 | tf_op jit(solution)/shard_map/psum | solution.py:16
  121.3 6.1 %all-reduce.7 = (f32[]{:T(128)}, f32[]{:T(128)}) all-reduce(f32[]{:T(128)} %get-tuple-element.8, f32[]{:T(128)} %get-tuple-element.9), channel_id=1, replica_groups=mesh['ty'=4,'tx_0'=4,'tx_1'=4,'tx_2'=2] {'tx_2'}, use_global_device_ids=true, to_apply=%region_9.10 | all-reduce | flops 2 | bytes 16 | tf_op jit(solution)/shard_map/psum | solution.py:16
  128.9 3.2 %collective-permute-start.4 = (f32[32,1024]{1,0:T(8,128)S(1)}, f32[32,1024]{1,0:T(8,128)S(1)}, u32[]{:S(2)}, u32[]{:S(2)}) collective-permute-start(f32[32,1024]{1,0:T(8,128)S(1)} %get-tuple-element.32), channel_id=1, source_target_pairs={{0,32},{32,64},{64,96},{1,33},{33,65},{65,97},{2,34},{34,66},{66,9... | collective-permute-start | bytes 393224 | tf_op jit(solution)/shard_map/ppermute | solution.py:39
  132.1 1.3 collective-permute-start.5
  133.4 1.2 collective-permute-done.4
  134.7 3.8 %collective-permute-done.5 = f32[32,1024]{1,0:T(8,128)S(1)} collective-permute-done((f32[32,1024]{1,0:T(8,128)S(1)}, f32[32,1024]{1,0:T(8,128)S(1)}, u32[]{:S(2)}, u32[]{:S(2)}) %collective-permute-start.5) | collective-permute-done | bytes 131104 | tf_op jit(solution)/shard_map/ppermute | solution.py:42
  138.6 5.0 %collective-permute-start.6 = (f32[192,32]{1,0:T(8,128)S(1)}, f32[192,32]{1,0:T(8,128)S(1)}, u32[]{:S(2)}, u32[]{:S(2)}) collective-permute-start(f32[192,32]{1,0:T(8,128)S(1)} %get-tuple-element.27), channel_id=1, source_target_pairs={{0,1},{1,2},{2,3},{3,4},{4,5},{5,6},{6,7},{7,8},{8,9},{9,10},{10,1... | collective-permute-start | bytes 73736 | tf_op jit(solution)/shard_map/ppermute | solution.py:39
  143.6 2.1 %collective-permute-start.7 = (f32[192,32]{1,0:T(8,128)S(1)}, f32[192,32]{1,0:T(8,128)S(1)}, u32[]{:S(2)}, u32[]{:S(2)}) collective-permute-start(f32[192,32]{1,0:T(8,128)S(1)} %get-tuple-element.26), channel_id=1, source_target_pairs={{1,0},{2,1},{3,2},{4,3},{5,4},{6,5},{7,6},{8,7},{9,8},{10,9},{11,1... | collective-permute-start | bytes 73736 | tf_op jit(solution)/shard_map/ppermute | solution.py:42
  145.8 3.8 %collective-permute-done.7 = f32[192,32]{1,0:T(8,128)S(1)} collective-permute-done((f32[192,32]{1,0:T(8,128)S(1)}, f32[192,32]{1,0:T(8,128)S(1)}, u32[]{:S(2)}, u32[]{:S(2)}) %collective-permute-start.7) | collective-permute-done | bytes 24608 | tf_op jit(solution)/shard_map/ppermute | solution.py:42
  149.6 1.2 concatenate.19
  150.8 7.5 %fusion.1 = f32[192,1024]{1,0:T(8,128)S(1)} fusion(f32[192,1088]{1,0:T(8,128)} %concatenate.19, f32[]{:T(128)} %multiply_reduce_fusion.4), kind=kOutput, calls=%fused_computation.6 | convolution fusion | flops 2582511616 | bytes 1622020 | tf_op jit(solution)/shard_map/dot_general | solution.py:117
  158.3 2.1 %multiply_reduce_fusion = (f32[]{:T(128)}, f32[]{:T(128)}, f32[128,1024]{1,0:T(8,128)S(1)}) fusion(f32[128,1024]{1,0:T(8,128)S(1)} %get-tuple-element.23, f32[128,1024]{1,0:T(8,128)S(1)} %fusion.5, f32[192,1024]{1,0:T(8,128)S(1)} %fusion.1, f32[]{:T(128)} %multiply_reduce_fusion.4), kind=kOutput, calls=%fused_computation.28 | convolution fusion | flops 303251456 | bytes 2359308 | tf_op jit(solution)/shard_map/dot_general | solution.py:118
  160.4 6.7 %all-reduce.4 = (f32[]{:T(128)}, f32[]{:T(128)}) all-reduce(f32[]{:T(128)} %get-tuple-element.3, f32[]{:T(128)} %get-tuple-element.2), channel_id=1, replica_groups=mesh['ty'=4,'tx_0'=4,'tx_1'=4,'tx_2'=2] {'ty'}, use_global_device_ids=true, to_apply=%region_17.18 | all-reduce | flops 2 | bytes 16 | tf_op jit(solution)/shard_map/psum | solution.py:16
  167.1 6.6 %all-reduce.2 = (f32[]{:T(128)}, f32[]{:T(128)}) all-reduce(f32[]{:T(128)} %get-tuple-element.14, f32[]{:T(128)} %get-tuple-element.15), channel_id=1, replica_groups=mesh['ty'=4,'tx_0'=4,'tx_1'=4,'tx_2'=2] {'tx_0'}, use_global_device_ids=true, to_apply=%region_18.19 | all-reduce | flops 2 | bytes 16 | tf_op jit(solution)/shard_map/psum | solution.py:16
  173.7 9.7 %all-reduce = (f32[]{:T(128)}, f32[]{:T(128)}) all-reduce(f32[]{:T(128)} %get-tuple-element.10, f32[]{:T(128)} %get-tuple-element.11), channel_id=1, replica_groups=mesh['ty'=4,'tx_0'=4,'tx_1'=4,'tx_2'=2] {'tx_1'}, use_global_device_ids=true, to_apply=%region_19.20 | all-reduce | flops 2 | bytes 16 | tf_op jit(solution)/shard_map/psum | solution.py:16
  183.4 5.8 %all-reduce.6 = (f32[]{:T(128)}, f32[]{:T(128)}) all-reduce(f32[]{:T(128)} %get-tuple-element.6, f32[]{:T(128)} %get-tuple-element.7), channel_id=1, replica_groups=mesh['ty'=4,'tx_0'=4,'tx_1'=4,'tx_2'=2] {'tx_2'}, use_global_device_ids=true, to_apply=%region_20.21 | all-reduce | flops 2 | bytes 16 | tf_op jit(solution)/shard_map/psum | solution.py:16
  193.6 1.2 multiply_subtract_fusion
  (18 shorter events, 2.8 us)
Async XLA Ops:
  0.6 18.4 %copy-start.1 = (f32[128,1,1024]{2,1,0:T(1,128)S(1)}, f32[128,1,1024]{2,1,0:T(1,128)}, u32[]{:S(2)}) copy-start(f32[128,1,1024]{2,1,0:T(1,128)} %param.6) | copy-start | bytes 1572868
  5.0 20.9 %all-to-all-start = ((s32[128,1,2]{2,1,0:T(1,128)}), s32[128,1,2]{2,1,0:T(1,128)S(1)}, u32[]{:S(2)}, u32[]{:S(2)}) async-start(s32[128,1,2]{2,1,0:T(1,128)} %bitcast.3), calls=%async_computation | async-start | bytes 131072 | tf_op jit(solution)/shard_map/all_to_all | solution.py:95
  25.9 37.7 %all-to-all-start.1 = ((f32[128,4,1,1024]{3,1,2,0:T(4,128)}), f32[128,4,1,1024]{3,1,2,0:T(4,128)S(1)}, u32[]{:S(2)}, u32[]{:S(2)}) async-start(f32[128,4,1,1024]{3,1,2,0:T(4,128)} %pad_maximum_fusion), calls=%async_computation.1 | async-start | bytes 4194304 | tf_op jit(solution)/shard_map/all_to_all | solution.py:27
  65.4 1.2 copy-start
  69.6 3.2 %collective-permute-start = (f32[32,1024]{1,0:T(8,128)S(1)}, f32[32,1024]{1,0:T(8,128)S(1)}, u32[]{:S(2)}, u32[]{:S(2)}) collective-permute-start(f32[32,1024]{1,0:T(8,128)S(1)} %get-tuple-element.34), channel_id=1, source_target_pairs={{0,32},{32,64},{64,96},{1,33},{33,65},{65,97},{2,34},{34,66},{66,9... | collective-permute-start | bytes 393224 | tf_op jit(solution)/shard_map/ppermute | solution.py:39
  70.9 5.7 %collective-permute-start.1 = (f32[32,1024]{1,0:T(8,128)S(1)}, f32[32,1024]{1,0:T(8,128)S(1)}, u32[]{:S(2)}, u32[]{:S(2)}) collective-permute-start(f32[32,1024]{1,0:T(8,128)S(1)} %get-tuple-element.35), channel_id=1, source_target_pairs={{32,0},{64,32},{96,64},{33,1},{65,33},{97,65},{34,2},{66,34},{98,6... | collective-permute-start | bytes 393224 | tf_op jit(solution)/shard_map/ppermute | solution.py:42
  76.8 6.9 %collective-permute-start.2 = (f32[192,32]{1,0:T(8,128)S(1)}, f32[192,32]{1,0:T(8,128)S(1)}, u32[]{:S(2)}, u32[]{:S(2)}) collective-permute-start(f32[192,32]{1,0:T(8,128)S(1)} %get-tuple-element.29), channel_id=1, source_target_pairs={{0,1},{1,2},{2,3},{3,4},{4,5},{5,6},{6,7},{7,8},{8,9},{9,10},{10,1... | collective-permute-start | bytes 73736 | tf_op jit(solution)/shard_map/ppermute | solution.py:39
  80.9 5.9 %collective-permute-start.3 = (f32[192,32]{1,0:T(8,128)S(1)}, f32[192,32]{1,0:T(8,128)S(1)}, u32[]{:S(2)}, u32[]{:S(2)}) collective-permute-start(f32[192,32]{1,0:T(8,128)S(1)} %get-tuple-element.28), channel_id=1, source_target_pairs={{1,0},{2,1},{3,2},{4,3},{5,4},{6,5},{7,6},{8,7},{9,8},{10,9},{11,1... | collective-permute-start | bytes 73736 | tf_op jit(solution)/shard_map/ppermute | solution.py:42
  128.9 5.8 %collective-permute-start.4 = (f32[32,1024]{1,0:T(8,128)S(1)}, f32[32,1024]{1,0:T(8,128)S(1)}, u32[]{:S(2)}, u32[]{:S(2)}) collective-permute-start(f32[32,1024]{1,0:T(8,128)S(1)} %get-tuple-element.32), channel_id=1, source_target_pairs={{0,32},{32,64},{64,96},{1,33},{33,65},{65,97},{2,34},{34,66},{66,9... | collective-permute-start | bytes 393224 | tf_op jit(solution)/shard_map/ppermute | solution.py:39
  132.1 6.3 %collective-permute-start.5 = (f32[32,1024]{1,0:T(8,128)S(1)}, f32[32,1024]{1,0:T(8,128)S(1)}, u32[]{:S(2)}, u32[]{:S(2)}) collective-permute-start(f32[32,1024]{1,0:T(8,128)S(1)} %get-tuple-element.33), channel_id=1, source_target_pairs={{32,0},{64,32},{96,64},{33,1},{65,33},{97,65},{34,2},{66,34},{98,6... | collective-permute-start | bytes 393224 | tf_op jit(solution)/shard_map/ppermute | solution.py:42
  138.6 7.2 %collective-permute-start.6 = (f32[192,32]{1,0:T(8,128)S(1)}, f32[192,32]{1,0:T(8,128)S(1)}, u32[]{:S(2)}, u32[]{:S(2)}) collective-permute-start(f32[192,32]{1,0:T(8,128)S(1)} %get-tuple-element.27), channel_id=1, source_target_pairs={{0,1},{1,2},{2,3},{3,4},{4,5},{5,6},{6,7},{7,8},{8,9},{9,10},{10,1... | collective-permute-start | bytes 73736 | tf_op jit(solution)/shard_map/ppermute | solution.py:39
  143.6 5.9 %collective-permute-start.7 = (f32[192,32]{1,0:T(8,128)S(1)}, f32[192,32]{1,0:T(8,128)S(1)}, u32[]{:S(2)}, u32[]{:S(2)}) collective-permute-start(f32[192,32]{1,0:T(8,128)S(1)} %get-tuple-element.26), channel_id=1, source_target_pairs={{1,0},{2,1},{3,2},{4,3},{5,4},{6,5},{7,6},{8,7},{9,8},{10,9},{11,1... | collective-permute-start | bytes 73736 | tf_op jit(solution)/shard_map/ppermute | solution.py:42
where the time goes:
time: 196 us; the launch traced here: 195 us
  blocking collectives  60.6 us (31%)
  waiting for transfers between devices  48.1 us (25%)
  starting transfers between devices  39.2 us (20%)
  matrix products  20.1 us (10%)
  local copies, waits for them, and re-layouts  12.7 us (6%)
  other arithmetic  7.61 us (4%)
  between operations  6.5 us (3%)
    psum x8, blocking collectives, over_axes(): return functools.reduce(lax.psum, axes, shard)  60.6 us
    all_to_all x1, waiting for transfers between devices, side_by_side(): lax.all_to_all(both, axis, split_axis=split_dim, concat_axis=concat_dim,...  29.1 us
    ppermute x4, waiting for transfers between devices, padded_2(): lax.ppermute(lax.slice_in_dim(block, 0, width, axis=dim), axis, backward)  14.6 us
    dot_general x2, matrix products, operate(): across = jnp.dot(padded, col_band, precision=lax.Precision.HIGHEST)  13.8 us
    ppermute x4, starting transfers between devices, padded_2(): lax.ppermute(lax.slice_in_dim(block, block.shape[dim] - width, None, axis...  13.7 us
    all_to_all x1, starting transfers between devices, shards(): lax.all_to_all(send_rows.reshape(devices, slots), TY_TX, split_axis=0, co...  11.5 us
    all_to_all x1, starting transfers between devices, side_by_side(): lax.all_to_all(both, axis, split_axis=split_dim, concat_axis=concat_dim,...  7.17 us
    ppermute x4, starting transfers between devices, padded_2(): lax.ppermute(lax.slice_in_dim(block, 0, width, axis=dim), axis, backward)  6.83 us
  transfers between devices with their start and end apart: 10, of which 8 were waited for; matrix products, arithmetic and copies ran while one was open for 5% of the time, Pallas kernels for 0%

commit v1 on v0

v1 whole, which is shorter than its diff:
```python
import functools

import jax
import jax.numpy as jnp
import numpy as np
from jax import lax
from jax.experimental import pallas as pl
from jax.experimental.pallas import tpu as pltpu
from jax.sharding import Mesh
from jax.sharding import PartitionSpec as P

HALF = 32
LANES = 128
SLOTS = 2
TY_TX = ("ty", "tx_0", "tx_1", "tx_2")
TX = ("tx_0", "tx_1", "tx_2")
F32 = jnp.float32
BF16 = jnp.bfloat16


def taps(offset):
    def raw(d):
        scaled = np.abs(d) / (HALF + 1.0)
        return np.where(np.abs(d) <= HALF, (1.0 - scaled) ** 4 * (1.0 + 4.0 * scaled), 0.0)

    values = raw(offset) / raw(np.arange(-HALF, HALF + 1)).sum()
    head = values.astype(BF16)
    tail = (values - head.astype(np.float64)).astype(BF16)
    return jnp.asarray(head), jnp.asarray(tail)


def split2(x):
    head = x.astype(BF16)
    return head, (x - head.astype(F32)).astype(BF16)


def split3(x):
    head = x.astype(BF16)
    rest = x - head.astype(F32)
    mid = rest.astype(BF16)
    return head, mid, (rest - mid.astype(F32)).astype(BF16)


def mm(a, b):
    return jnp.dot(a, b, preferred_element_type=F32)


def pick(select, x):
    head, mid, tail = split3(x)
    return mm(select, tail) + mm(select, mid) + mm(select, head)


def smooth3(left, right):
    (lh, ll), (rh, rl) = left, right
    return mm(ll, rh) + mm(lh, rl) + mm(lh, rh)


def iota(shape, dim):
    return lax.broadcasted_iota(jnp.int32, shape, dim)


def pack_kernel(n_tx, parts, length, tile_ref, row_ref, sums_ref, weights_ref, out_ref):
    count = tile_ref.shape[1]
    devices = out_ref.shape[0] // length
    tile = tile_ref[...]
    t = iota((devices, count), 0)
    same = tile == t
    earlier = iota((count, count), 0) < iota((count, count), 1)
    before = mm(same.astype(F32).astype(BF16), earlier.astype(F32).astype(BF16))
    rank = jnp.sum(jnp.where(same, before, 0.0), axis=0, keepdims=True)
    column = lax.rem(t, n_tx)
    from_left = (tile + 1 == t) & (column != 0)
    from_right = (tile - 1 == t) & (column != n_tx - 1)

    def onehot(mask, k):
        return jnp.where(mask & (rank == float(k)), 1.0, 0.0)

    own = [onehot(same, k) for k in range(SLOTS)]
    own_all = jnp.concatenate(own, axis=0).astype(BF16)
    left_all = jnp.concatenate([onehot(from_left, k) for k in range(SLOTS)], axis=0).astype(BF16)
    right_all = jnp.concatenate(
        [jnp.concatenate([onehot(from_right, k), own[k]], axis=1) for k in range(SLOTS)], axis=0
    ).astype(BF16)

    for which, ref in enumerate((sums_ref, weights_ref)):
        for c in range(0, parts, 2):
            x = jnp.concatenate(
                [ref[pl.ds(c + i, count, stride=parts), :] for i in range(2)], axis=1
            )
            y = pick(own_all, x)
            for k in range(SLOTS):
                for i in range(2):
                    at = (which * SLOTS + k) * parts + c + i
                    out_ref[pl.ds(at, devices, stride=length), :] = y[
                        k * devices : (k + 1) * devices, i * LANES : (i + 1) * LANES
                    ]

    lane = iota((count, LANES), 1)
    number = jnp.transpose(
        jnp.broadcast_to(row_ref[...].astype(F32) + 1.0, (count, count))
    )
    last = parts - 1
    s_last = sums_ref[pl.ds(last, count, stride=parts), :]
    w_last = pltpu.roll(weights_ref[pl.ds(last, count, stride=parts), :], 64, 1)
    s_first = sums_ref[pl.ds(0, count, stride=parts), :]
    w_first = pltpu.roll(weights_ref[pl.ds(0, count, stride=parts), :], 64, 1)
    left_rows = jnp.where(
        lane >= 64, s_last, jnp.where(lane >= 32, w_last, jnp.where(lane == 0, number, 0.0))
    )
    right_rows = jnp.where(
        lane < 64, s_first, jnp.where(lane < 96, w_first, jnp.where(lane == 96, number, 0.0))
    )
    own_rows = jnp.where(lane == 97, number, 0.0)
    to_left = pick(left_all, left_rows)
    to_right = pick(right_all, jnp.concatenate([right_rows, own_rows], axis=0))
    base = 2 * SLOTS * parts
    for k in range(SLOTS):
        part = slice(k * devices, (k + 1) * devices)
        out_ref[pl.ds(base + k, devices, stride=length), :] = to_left[part]
        out_ref[pl.ds(base + SLOTS + k, devices, stride=length), :] = to_right[part]


def select_kernel(
    parts, length, got_ref, prior_ref, prior_right_ref, prior_left_ref, s_ref, w_ref, up_ref, down_ref
):
    rows, cols = prior_ref.shape
    devices = got_ref.shape[0] // length
    base = 2 * SLOTS * parts
    from_left = [got_ref[pl.ds(base + k, devices, stride=length), :] for k in range(SLOTS)]
    from_right = [got_ref[pl.ds(base + SLOTS + k, devices, stride=length), :] for k in range(SLOTS)]
    left_t = [jnp.transpose(x) for x in from_left]
    right_t = [jnp.transpose(x) for x in from_right]
    wanted = (iota((rows, devices), 0) + 1).astype(F32)

    def chooser(lists, at):
        return jnp.concatenate(
            [jnp.where(x[at : at + 1, :] == wanted, 1.0, 0.0) for x in lists], axis=1
        ).astype(BF16)

    own = chooser(right_t, 97)
    for which, dst in enumerate((s_ref, w_ref)):
        for c in range(0, parts, 2):
            x = jnp.concatenate(
                [
                    jnp.concatenate(
                        [
                            got_ref[
                                pl.ds((which * SLOTS + k) * parts + c + i, devices, stride=length), :
                            ]
                            for i in range(2)
                        ],
                        axis=1,
                    )
                    for k in range(SLOTS)
                ],
                axis=0,
            )
            y = pick(own, x)
            at = slice(c * LANES, (c + 2) * LANES)
            if which == 1:
                y = y + prior_ref[:, at]
            dst[:, at] = y
    left = pick(chooser(left_t, 0), jnp.concatenate(from_left, axis=0))
    right = pick(chooser(right_t, 96), jnp.concatenate(from_right, axis=0))
    lane = iota((rows, LANES), 1)
    s_ref[:, cols:] = jnp.where(lane < 64, right, left)
    w_ref[:, cols:] = jnp.where(
        lane < 32,
        pltpu.roll(right, 64, 1) + prior_right_ref[...],
        jnp.where(lane >= 96, pltpu.roll(left, 64, 1) + prior_left_ref[...], 0.0),
    )
    up_ref[: 2 * HALF, :] = s_ref[: 2 * HALF, :]
    up_ref[2 * HALF :, :] = w_ref[:HALF, :]
    down_ref[: 2 * HALF, :] = s_ref[rows - 2 * HALF :, :]
    down_ref[2 * HALF :, :] = w_ref[rows - HALF :, :]


def conv_kernel(
    s_ref,
    w_ref,
    above_ref,
    below_ref,
    row_h_ref,
    row_l_ref,
    col_h_ref,
    col_l_ref,
    edge_h_ref,
    edge_l_ref,
    y0_ref,
    y1_ref,
    moments_ref,
    mid_ref,
    z_ref,
):
    rows, wide = s_ref.shape
    cols = wide - LANES
    tall = rows + 2 * HALF
    col = (col_h_ref[...], col_l_ref[...])
    edge = (edge_h_ref[...], edge_l_ref[...])

    def block(ref, c, height):
        lo, hi = (c - 1) * LANES, (c + 3) * LANES
        if c == 0:
            x = jnp.concatenate([ref[:height, cols:], ref[:height, :hi]], axis=1)
        else:
            x = ref[:height, lo:hi]
        return smooth3(split2(x), col)

    row = (row_h_ref[...], row_l_ref[...])
    for c in range(0, wide, LANES * 3):
        at = slice(c, c + LANES * 3)
        full = jnp.concatenate(
            [above_ref[: 2 * HALF, at], s_ref[:, at], below_ref[: 2 * HALF, at]], axis=0
        )
        mid_ref[:, at] = smooth3(row, split2(full))
    total_sy = jnp.zeros((rows, 2 * LANES), F32)
    total_zy = jnp.zeros((rows, 2 * LANES), F32)
    total_ss = jnp.zeros((rows, 2 * LANES), F32)
    for c in range(0, cols // LANES, 2):
        at = slice(c * LANES, (c + 2) * LANES)
        y = block(mid_ref, c, tall)
        w = jnp.concatenate([above_ref[2 * HALF :, at], w_ref[:, at], below_ref[2 * HALF :, at]], axis=0)
        z = w * y
        z_ref[:, at] = z
        inner = y[HALF : HALF + rows]
        y0_ref[:, at] = inner
        s = s_ref[:, at]
        total_sy += s * inner
        total_zy += z[HALF : HALF + rows] * inner
        total_ss += s * s / w_ref[:, at]
    x = jnp.concatenate([mid_ref[:, cols - LANES :], mid_ref[:, :LANES]], axis=1)
    y = smooth3(split2(x), edge)
    w = jnp.concatenate([above_ref[2 * HALF :, cols:], w_ref[:, cols:], below_ref[2 * HALF :, cols:]], axis=0)
    z_ref[:, cols:] = w * y

    row = (row_h_ref[:rows, :tall], row_l_ref[:rows, :tall])
    for c in range(0, wide, LANES * 3):
        at = slice(c, c + LANES * 3)
        mid_ref[:rows, at] = smooth3(row, split2(z_ref[:, at]))
    total_zz = jnp.zeros((rows, 2 * LANES), F32)
    for c in range(0, cols // LANES, 2):
        at = slice(c * LANES, (c + 2) * LANES)
        y = block(mid_ref, c, rows)
        y1_ref[:, at] = y
        total_zz += z_ref[HALF : HALF + rows, at] * y
    lane = iota((1, LANES), 1)
    packed = jnp.zeros((1, LANES), F32)
    for i, total in enumerate((total_ss, total_sy, total_zy, total_zz)):
        value = jnp.sum(jnp.sum(total, axis=0, keepdims=True), axis=1, keepdims=True)
        packed = jnp.where(lane == i, value, packed)
    moments_ref[...] = jnp.broadcast_to(packed, moments_ref.shape)


def final_kernel(moments_ref, s_ref, w_ref, y0_ref, y1_ref, x_ref, r_ref):
    totals = jnp.sum(moments_ref[...], axis=0, keepdims=True)
    lane = iota(totals.shape, 1)
    m0, n1, n2, n3 = (
        jnp.sum(jnp.where(lane == i, totals, 0.0), axis=1, keepdims=True) for i in range(4)
    )
    mu = n1 / m0
    a = m0 / (0.5 * m0 + n1)
    vv = n2 - mu * n1
    vbv = n3 - 2.0 * mu * n2 + mu * mu * n1
    beta = a * a * vv / m0
    step = vv / (0.5 * vv + vbv - a * vv * vv / m0)
    x_r0 = a + step * beta + step * a * mu
    x_b0 = -step * a
    r_r0 = a * mu - step * (0.5 * a * mu + 0.5 * beta)
    r_b0 = -a - step * (a * mu - 0.5 * a + beta)
    r_b1 = step * a
    w = w_ref[...]
    root = jnp.sqrt(w)
    r0 = s_ref[...] / w
    y0 = y0_ref[...]
    x_ref[...] = root * (x_r0 * r0 + x_b0 * y0)
    r_ref[...] = root * (r_r0 * r0 + r_b0 * y0 + r_b1 * y1_ref[...])


def vmem(count):
    return [pl.BlockSpec(memory_space=pltpu.VMEM)] * count


def call(kernel, shapes, *args, scratch=(), name, flops=0):
    moved = sum(int(np.prod(x.shape)) * x.dtype.itemsize for x in args)
    return pl.pallas_call(
        kernel,
        out_shape=[jax.ShapeDtypeStruct(s, F32) for s in shapes],
        in_specs=vmem(len(args)),
        out_specs=vmem(len(shapes)),
        scratch_shapes=list(scratch),
        compiler_params=pltpu.CompilerParams(vmem_limit_bytes=40 << 20),
        cost_estimate=pl.CostEstimate(flops=flops, bytes_accessed=moved, transcendentals=0),
        name=name,
    )(*args)


def neighbours(axes, step):
    count = int(np.prod([lax.axis_size(a) for a in axes]))
    pairs = [(i, i + 1) for i in range(count - 1)]
    return pairs if step > 0 else [(b, a) for a, b in pairs]


def shards(block_sums, block_weights, block_tile, block_row, prior_weight):
    devices = lax.axis_size(TY_TX)
    n_tx = lax.axis_size(TX)
    blocks, _, cols = block_sums.shape
    rows = prior_weight.shape[0]
    parts = cols // LANES
    length = 2 * SLOTS * parts + 2 * SLOTS
    wide = cols + LANES
    slab = (3 * HALF, wide)

    prior_right = lax.ppermute(prior_weight[:, :LANES], TX, neighbours(TX, -1))
    prior_left = lax.ppermute(prior_weight[:, cols - LANES :], TX, neighbours(TX, 1))

    (message,) = call(
        functools.partial(pack_kernel, n_tx, parts, length),
        [(devices * length, LANES)],
        block_tile.reshape(1, blocks),
        block_row.reshape(1, blocks),
        block_sums.reshape(blocks * parts, LANES),
        block_weights.reshape(blocks * parts, LANES),
        name="pack",
    )
    got = lax.all_to_all(
        message.reshape(devices, 1, length * LANES), TY_TX, split_axis=0, concat_axis=0, tiled=True
    ).reshape(devices * length, LANES)
    s, w, up, down = call(
        functools.partial(select_kernel, parts, length),
        [(rows, wide), (rows, wide), slab, slab],
        got,
        prior_weight,
        prior_right,
        prior_left,
        name="select",
    )
    above = lax.ppermute(down, "ty", neighbours(("ty",), 1))
    below = lax.ppermute(up, "ty", neighbours(("ty",), -1))

    tall = rows + 2 * HALF
    row_taps = taps(np.arange(tall)[:, None] - np.arange(rows + 4 * HALF)[None, :] + HALF)
    col_taps = taps(np.arange(2 * LANES)[None, :] - np.arange(4 * LANES)[:, None] + LANES)
    ring = np.where(np.arange(LANES) < 64, cols, -LANES) + np.arange(LANES)
    near = np.concatenate([np.arange(cols - LANES, cols), ring, np.arange(LANES)])
    edge_taps = taps(ring[None, :] - near[:, None])
    y0, y1, moments = call(
        conv_kernel,
        [(rows, cols), (rows, cols), (devices, LANES)],
        s,
        w,
        above,
        below,
        *row_taps,
        *col_taps,
        *edge_taps,
        scratch=[pltpu.VMEM((tall, wide), F32), pltpu.VMEM((tall, wide), F32)],
        name="smooth",
    )
    moments = lax.all_to_all(
        moments.reshape(devices, 1, LANES), TY_TX, split_axis=0, concat_axis=0, tiled=True
    ).reshape(devices, LANES)
    whole = lambda shape: pl.BlockSpec(shape, lambda i: (0, 0))
    return tuple(
        pl.pallas_call(
            final_kernel,
            grid=(1,),
            out_shape=[jax.ShapeDtypeStruct((rows, cols), F32)] * 2,
            in_specs=[whole((devices, LANES))] + [whole((rows, cols))] * 4,
            out_specs=[whole((rows, cols))] * 2,
            compiler_params=pltpu.CompilerParams(vmem_limit_bytes=40 << 20),
            name="combine",
        )(moments, s, w, y0, y1)
    )


def solution(mesh):
    split = Mesh(mesh.devices.reshape(mesh.shape["ty"], 4, 4, 2), ("ty", "tx_0", "tx_1", "tx_2"))
    in_specs = (P(TY_TX, None, None), P(TY_TX, None, None), P(TY_TX, None), P(TY_TX), P("ty", TX))
    out_specs = (P("ty", TX), P("ty", TX))
    return jax.shard_map(
        shards, mesh=split, in_specs=in_specs, out_specs=out_specs, check_vma=False
    )
```

time: 196 us -> 90.1 us (0.46)
  blocking collectives: 60.6 us -> 19.2 us
  matrix products: 20.1 us -> 0 us
  starting transfers between devices: 39.2 us -> 19.8 us
  waiting for transfers between devices: 48.1 us -> 35.9 us
  other arithmetic: 7.61 us -> 0 us
  Pallas kernels: 0 us -> 6.14 us
  between operations: 6.5 us -> 0.78 us
  local copies, waits for them, and re-layouts: 12.7 us -> 7.84 us
    psum x8 -> x0, blocking collectives: 60.6 us -> none  [over_axes(): return functools.reduce(lax.psum, axes, shard)]
    all_to_all x2 -> x1, waiting for transfers between devices: 31.7 us -> 4.01 us  [shards(): lax.all_to_all(message.reshape(devices, 1, length * LANES), TY_TX, split_...]
    dot_general x6 -> x0, matrix products: 20.1 us -> none  [the longest x2 13.8 us: operate(): across = jnp.dot(padded, col_band, precision=lax.Precision.HIGHEST)]
    all_to_all x0 -> x1, blocking collectives: none -> 19.2 us  [shards(): lax.all_to_all(moments.reshape(devices, 1, LANES), TY_TX, split_axis=0, c...]
    ppermute x8 -> x4, waiting for transfers between devices: 16.4 us -> 31.9 us  [the longest x1 22.2 us: shards(): prior_right = lax.ppermute(prior_weight[:, :LANES], TX, neighbours(TX, -1))]
    ppermute x8 -> x4, starting transfers between devices: 20.6 us -> 8.3 us  [the longest x1 3.11 us: shards(): prior_right = lax.ppermute(prior_weight[:, :LANES], TX, neighbours(TX, -1))]
    unnamed x4 -> x32, local copies, waits for them, and re-layouts: 0.51 us -> 7.83 us
    all_to_all x2 -> x1, starting transfers between devices: 18.7 us -> 11.5 us  [shards(): lax.all_to_all(message.reshape(devices, 1, length * LANES), TY_TX, split_...]
  transfers between devices with their start and end apart: 10 -> 5, of which waited for: 8 -> 4; matrix products, arithmetic and copies ran while one was open for 5% -> 0% of each run, Pallas kernels for 0% -> 0%
where the time goes in v1:
time: 90.1 us; the launch traced here: 89.7 us
  waiting for transfers between devices  35.9 us (40%)
  starting transfers between devices  19.8 us (22%)
  blocking collectives  19.2 us (21%)
  local copies, waits for them, and re-layouts  7.84 us (9%)
  Pallas kernels  6.14 us (7%)
    ppermute x1, waiting for transfers between devices, shards(): prior_right = lax.ppermute(prior_weight[:, :LANES], TX, neighbours(TX, -1))  22.2 us
    all_to_all x1, blocking collectives, shards(): lax.all_to_all(moments.reshape(devices, 1, LANES), TY_TX, split_axis=0, c...  19.2 us
    all_to_all x1, starting transfers between devices, shards(): lax.all_to_all(message.reshape(devices, 1, length * LANES), TY_TX, split_...  11.5 us
    unnamed x32, local copies, waits for them, and re-layouts  7.83 us
    ppermute x1, waiting for transfers between devices, shards(): above = lax.ppermute(down, 'ty', neighbours(('ty',), 1))  5.87 us
    pallas_call x3, Pallas kernels, call(): pl.pallas_call(kernel, out_shape=[jax.ShapeDtypeStruct(s, F32) for s in s...  4.71 us
    all_to_all x1, waiting for transfers between devices, shards(): lax.all_to_all(message.reshape(devices, 1, length * LANES), TY_TX, split_...  4.01 us
    ppermute x1, waiting for transfers between devices, shards(): below = lax.ppermute(up, 'ty', neighbours(('ty',), -1))  3.86 us
  transfers between devices with their start and end apart: 5, of which 4 were waited for; matrix products, arithmetic and copies ran while one was open for 0% of the time, Pallas kernels for 0%

profile of v1, /device:TPU:1, one launch (start us, length us, event | category | flops | bytes accessed | tf_op | source)
XLA Modules:
  0.0 89.7 jit_solution(1151559710391063639)
XLA Ops:
  0.6 0.0 copy-start.2
  0.6 1.0 %copy-done.2 = f32[128,1,1024]{2,1,0:T(1,128)S(1)} copy-done((f32[128,1,1024]{2,1,0:T(1,128)S(1)}, f32[128,1,1024]{2,1,0:T(1,128)}, u32[]{:S(2)}) %copy-start.2) | copy-done | bytes 524312
  1.7 0.0 copy-start.3
  1.7 1.0 %copy-done.3 = f32[128,1,1024]{2,1,0:T(1,128)S(1)} copy-done((f32[128,1,1024]{2,1,0:T(1,128)S(1)}, f32[128,1,1024]{2,1,0:T(1,128)}, u32[]{:S(2)}) %copy-start.3) | copy-done | bytes 524312
  2.7 0.0 copy-start.14
  2.7 0.7 copy-done.14
  3.4 0.0 copy-start.15
  3.4 0.7 copy-done.15
  4.0 1.3 %pack.1 = f32[4608,128]{1,0:T(8,128)S(1)} custom-call(s32[1,128]{1,0:T(1,128)S(1)} %bitcast.16, s32[1,128]{1,0:T(1,128)S(1)} %bitcast.17, f32[1024,128]{1,0:T(8,128)S(1)} %bitcast.12, f32[1024,128]{1,0:T(8,128)S(1)} %bitcast.13), custom_call_target="tpu_custom_call" | custom-call | bytes 1049600 | tf_op jit(solution)/shard_map/pack/pallas_call | solution.py:285
  5.3 0.0 copy-start
  5.3 1.4 %copy-done = f32[4608,128]{1,0:T(8,128)} copy-done((f32[4608,128]{1,0:T(8,128)}, f32[4608,128]{1,0:T(8,128)S(1)}, u32[]{:S(2)}) %copy-start) | copy-done | bytes 2359320
  6.7 0.0 copy-start.1
  6.7 11.5 %all-to-all-start = ((f32[128,1,4608]{2,1,0:T(1,128)}), f32[128,1,4608]{2,1,0:T(1,128)S(1)}, u32[]{:S(2)}, u32[]{:S(2)}) async-start(f32[128,1,4608]{2,1,0:T(1,128)} %bitcast.11), calls=%async_computation | async-start | bytes 4718592 | tf_op jit(solution)/shard_map/all_to_all | solution.py:325
  18.2 0.0 copy-done.1
  18.2 0.0 copy-start.4
  18.3 0.0 copy-start.5
  18.3 0.0 copy-start.6
  18.3 3.1 %collective-permute-start = (f32[128,128]{1,0:T(8,128)S(1)}, f32[128,128]{1,0:T(8,128)S(1)}, u32[]{:S(2)}, u32[]{:S(2)}) collective-permute-start(f32[128,128]{1,0:T(8,128)S(1)} %get-tuple-element.17), channel_id=1, source_target_pairs={{1,0},{2,1},{3,2},{4,3},{5,4},{6,5},{7,6},{8,7},{9,8},{10,9},{11,1... | collective-permute-start | bytes 196616 | tf_op jit(solution)/shard_map/ppermute | solution.py:313
  21.4 2.6 %collective-permute-start.1 = (f32[128,128]{1,0:T(8,128)S(1)}, f32[128,128]{1,0:T(8,128)S(1)}, u32[]{:S(2)}, u32[]{:S(2)}) collective-permute-start(f32[128,128]{1,0:T(8,128)S(1)} %get-tuple-element.16), channel_id=1, source_target_pairs={{0,1},{1,2},{2,3},{3,4},{4,5},{5,6},{6,7},{7,8},{8,9},{9,10},{10,1... | collective-permute-start | bytes 196616 | tf_op jit(solution)/shard_map/ppermute | solution.py:314
  24.0 22.2 %collective-permute-done.prior_right_ref = f32[128,128]{1,0:T(8,128)S(1)} collective-permute-done((f32[128,128]{1,0:T(8,128)S(1)}, f32[128,128]{1,0:T(8,128)S(1)}, u32[]{:S(2)}, u32[]{:S(2)}) %collective-permute-start) | collective-permute-done | bytes 65568 | tf_op jit(solution)/shard_map/ppermute | solution.py:313
  46.2 0.0 copy-start.10
  46.2 0.6 copy-done.10
  46.8 0.0 collective-permute-done.1.prior_left_ref
  46.8 0.0 copy-start.12
  46.8 0.6 copy-done.12
  47.4 4.0 %all-to-all-done = f32[128,1,4608]{2,1,0:T(1,128)S(1)} async-done(((f32[128,1,4608]{2,1,0:T(1,128)}), f32[128,1,4608]{2,1,0:T(1,128)S(1)}, u32[]{:S(2)}, u32[]{:S(2)}) %all-to-all-start) | async-done | bytes 2359328 | tf_op jit(solution)/shard_map/all_to_all | solution.py:325
  51.5 0.0 copy-start.7
  51.5 0.0 copy-start.8
  51.5 0.0 copy-start.9
  51.5 0.0 copy-start.11
  51.5 0.9 copy-done.11
  52.4 0.0 copy-start.13
  52.4 0.8 copy-done.13
  53.2 1.0 %select.1 = (f32[128,1152]{1,0:T(8,128)S(1)}, f32[128,1152]{1,0:T(8,128)S(1)}, f32[96,1152]{1,0:T(8,128)S(1)}, f32[96,1152]{1,0:T(8,128)S(1)}) custom-call(f32[4608,128]{1,0:T(8,128)S(1)} %bitcast.10, f32[128,1024]{1,0:T(8,128)S(1)} %copy-done.1, f32[128,128]{1,0:T(8,128)S(1)} %copy-done.11, f32[128,128]{1,0:T(8,128)S(1)} %copy-done.13), custom_call_target="tpu_custom_call" | custom-call | bytes 3014656 | tf_op jit(solution)/shard_map/select/pallas_call | solution.py:285
  54.2 1.3 %collective-permute-start.2 = (f32[96,1152]{1,0:T(8,128)S(1)}, f32[96,1152]{1,0:T(8,128)S(1)}, u32[]{:S(2)}, u32[]{:S(2)}) collective-permute-start(f32[96,1152]{1,0:T(8,128)S(1)} %get-tuple-element.11), channel_id=1, source_target_pairs={{0,32},{32,64},{64,96},{1,33},{33,65},{65,97},{2,34},{34,66},{66,9... | collective-permute-start | bytes 1327112 | tf_op jit(solution)/shard_map/ppermute | solution.py:337
  55.5 1.3 %collective-permute-start.3 = (f32[96,1152]{1,0:T(8,128)S(1)}, f32[96,1152]{1,0:T(8,128)S(1)}, u32[]{:S(2)}, u32[]{:S(2)}) collective-permute-start(f32[96,1152]{1,0:T(8,128)S(1)} %get-tuple-element.12), channel_id=1, source_target_pairs={{32,0},{64,32},{96,64},{33,1},{65,33},{97,65},{34,2},{66,34},{98,6... | collective-permute-start | bytes 1327112 | tf_op jit(solution)/shard_map/ppermute | solution.py:338
  56.8 5.9 %collective-permute-done.2.above_ref = f32[96,1152]{1,0:T(8,128)S(1)} collective-permute-done((f32[96,1152]{1,0:T(8,128)S(1)}, f32[96,1152]{1,0:T(8,128)S(1)}, u32[]{:S(2)}, u32[]{:S(2)}) %collective-permute-start.2) | collective-permute-done | bytes 442400 | tf_op jit(solution)/shard_map/ppermute | solution.py:337
  62.7 3.9 %collective-permute-done.3.below_ref = f32[96,1152]{1,0:T(8,128)S(1)} collective-permute-done((f32[96,1152]{1,0:T(8,128)S(1)}, f32[96,1152]{1,0:T(8,128)S(1)}, u32[]{:S(2)}, u32[]{:S(2)}) %collective-permute-start.3) | collective-permute-done | bytes 442400 | tf_op jit(solution)/shard_map/ppermute | solution.py:338
  66.5 0.0 copy-done.4
  66.5 0.0 copy-done.5
  66.5 0.0 copy-done.6
  66.5 0.0 copy-done.7
  66.5 0.0 copy-done.8
  66.6 0.0 copy-done.9
  66.6 2.5 %smooth.1 = (f32[128,1024]{1,0:T(8,128)S(1)}, f32[128,1024]{1,0:T(8,128)S(1)}, f32[128,128]{1,0:T(8,128)S(1)}) custom-call(f32[128,1152]{1,0:T(8,128)S(1)} %get-tuple-element.9.s_ref, f32[128,1152]{1,0:T(8,128)S(1)} %get-tuple-element.10.w_ref, f32[96,1152]{1,0:T(8,128)S(1)} %collective-permute-done.2.above_ref, ...), custom_call_target="tpu_custom_call" | custom-call | bytes 2981888 | tf_op jit(solution)/shard_map/smooth/pallas_call | solution.py:285
  69.0 19.2 %all_to_all.10 = f32[128,1,128]{2,1,0:T(1,128)S(1)} all-to-all(f32[128,1,128]{2,1,0:T(1,128)S(1)} %bitcast.15), channel_id=1, replica_groups=mesh['ty'=4,'tx_0'=4,'tx_1'=4,'tx_2'=2] {'ty','tx_0','tx_1','tx_2'}, dimensions={0} | all-to-all | bytes 131072 | tf_op jit(solution)/shard_map/all_to_all | solution.py:359
  88.2 1.4 %combine.1 = (f32[128,1024]{1,0:T(8,128)}, f32[128,1024]{1,0:T(8,128)}) custom-call(f32[128,128]{1,0:T(8,128)S(1)} %bitcast.14, f32[128,1152]{1,0:T(8,128)S(1)} %get-tuple-element.9.s_ref, f32[128,1152]{1,0:T(8,128)S(1)} %get-tuple-element.10.w_ref, f32[128,1024]{1,0:T(8,128)S(1)} %get-tuple-element.14.y0_ref, f32[128,1024]{1,0:T(8,128)S(1)} %get-tuple-element.15.y1_ref), custom_call_target="tpu_custom_call" | custom-call | tf_op jit(solution)/shard_map/combine/pallas_call | solution.py:364
  (1 shorter events, 0.0 us)
Async XLA Ops:
  0.6 1.0 %copy-start.2 = (f32[128,1,1024]{2,1,0:T(1,128)S(1)}, f32[128,1,1024]{2,1,0:T(1,128)}, u32[]{:S(2)}) copy-start(f32[128,1,1024]{2,1,0:T(1,128)} %param.11) | copy-start | bytes 1572868
  1.7 1.0 %copy-start.3 = (f32[128,1,1024]{2,1,0:T(1,128)S(1)}, f32[128,1,1024]{2,1,0:T(1,128)}, u32[]{:S(2)}) copy-start(f32[128,1,1024]{2,1,0:T(1,128)} %param.12) | copy-start | bytes 1572868
  2.7 0.7 copy-start.14
  3.4 0.7 copy-start.15
  5.3 1.4 %copy-start = (f32[4608,128]{1,0:T(8,128)}, f32[4608,128]{1,0:T(8,128)S(1)}, u32[]{:S(2)}) copy-start(f32[4608,128]{1,0:T(8,128)S(1)} %pack.1) | copy-start | bytes 7077892
  6.7 11.5 %copy-start.1 = (f32[128,1024]{1,0:T(8,128)S(1)}, f32[128,1024]{1,0:T(8,128)}, u32[]{:S(2)}) copy-start(f32[128,1024]{1,0:T(8,128)} %prior_ref.1) | copy-start | bytes 1572868
  6.7 44.7 %all-to-all-start = ((f32[128,1,4608]{2,1,0:T(1,128)}), f32[128,1,4608]{2,1,0:T(1,128)S(1)}, u32[]{:S(2)}, u32[]{:S(2)}) async-start(f32[128,1,4608]{2,1,0:T(1,128)} %bitcast.11), calls=%async_computation | async-start | bytes 4718592 | tf_op jit(solution)/shard_map/all_to_all | solution.py:325
  18.2 48.3 %copy-start.4 = (bf16[512,256]{1,0:T(8,128)(2,1)S(1)}, bf16[512,256]{1,0:T(8,128)(2,1)}, u32[]{:S(2)}) copy-start(bf16[512,256]{1,0:T(8,128)(2,1)} %constant.14.clone.col_h_ref) | copy-start | bytes 786436
  18.3 48.3 %copy-start.5 = (bf16[512,256]{1,0:T(8,128)(2,1)S(1)}, bf16[512,256]{1,0:T(8,128)(2,1)}, u32[]{:S(2)}) copy-start(bf16[512,256]{1,0:T(8,128)(2,1)} %constant.15.clone.col_l_ref) | copy-start | bytes 786436
  18.3 48.3 %copy-start.6 = (bf16[192,256]{1,0:T(8,128)(2,1)S(1)}, bf16[192,256]{1,0:T(8,128)(2,1)}, u32[]{:S(2)}) copy-start(bf16[192,256]{1,0:T(8,128)(2,1)} %constant.12.clone.row_h_ref) | copy-start | bytes 294916
  18.3 27.9 %collective-permute-start = (f32[128,128]{1,0:T(8,128)S(1)}, f32[128,128]{1,0:T(8,128)S(1)}, u32[]{:S(2)}, u32[]{:S(2)}) collective-permute-start(f32[128,128]{1,0:T(8,128)S(1)} %get-tuple-element.17), channel_id=1, source_target_pairs={{1,0},{2,1},{3,2},{4,3},{5,4},{6,5},{7,6},{8,7},{9,8},{10,9},{11,1... | collective-permute-start | bytes 196616 | tf_op jit(solution)/shard_map/ppermute | solution.py:313
  21.4 25.4 %collective-permute-start.1 = (f32[128,128]{1,0:T(8,128)S(1)}, f32[128,128]{1,0:T(8,128)S(1)}, u32[]{:S(2)}, u32[]{:S(2)}) collective-permute-start(f32[128,128]{1,0:T(8,128)S(1)} %get-tuple-element.16), channel_id=1, source_target_pairs={{0,1},{1,2},{2,3},{3,4},{4,5},{5,6},{6,7},{7,8},{8,9},{9,10},{10,1... | collective-permute-start | bytes 196616 | tf_op jit(solution)/shard_map/ppermute | solution.py:314
  46.2 0.6 copy-start.10
  46.8 0.6 copy-start.12
  51.5 15.1 %copy-start.7 = (bf16[192,256]{1,0:T(8,128)(2,1)S(1)}, bf16[192,256]{1,0:T(8,128)(2,1)}, u32[]{:S(2)}) copy-start(bf16[192,256]{1,0:T(8,128)(2,1)} %constant.13.clone.row_l_ref) | copy-start | bytes 294916
  51.5 15.1 %copy-start.8 = (bf16[384,128]{1,0:T(8,128)(2,1)S(1)}, bf16[384,128]{1,0:T(8,128)(2,1)}, u32[]{:S(2)}) copy-start(bf16[384,128]{1,0:T(8,128)(2,1)} %constant.16.clone.edge_h_ref) | copy-start | bytes 294916
  51.5 15.1 %copy-start.9 = (bf16[384,128]{1,0:T(8,128)(2,1)S(1)}, bf16[384,128]{1,0:T(8,128)(2,1)}, u32[]{:S(2)}) copy-start(bf16[384,128]{1,0:T(8,128)(2,1)} %constant.17.clone.edge_l_ref) | copy-start | bytes 294916
  51.5 0.9 copy-start.11
  52.4 0.8 copy-start.13
  54.2 8.5 %collective-permute-start.2 = (f32[96,1152]{1,0:T(8,128)S(1)}, f32[96,1152]{1,0:T(8,128)S(1)}, u32[]{:S(2)}, u32[]{:S(2)}) collective-permute-start(f32[96,1152]{1,0:T(8,128)S(1)} %get-tuple-element.11), channel_id=1, source_target_pairs={{0,32},{32,64},{64,96},{1,33},{33,65},{65,97},{2,34},{34,66},{66,9... | collective-permute-start | bytes 1327112 | tf_op jit(solution)/shard_map/ppermute | solution.py:337
  55.5 11.0 %collective-permute-start.3 = (f32[96,1152]{1,0:T(8,128)S(1)}, f32[96,1152]{1,0:T(8,128)S(1)}, u32[]{:S(2)}, u32[]{:S(2)}) collective-permute-start(f32[96,1152]{1,0:T(8,128)S(1)} %get-tuple-element.12), channel_id=1, source_target_pairs={{32,0},{64,32},{96,64},{33,1},{65,33},{97,65},{34,2},{66,34},{98,6... | collective-permute-start | bytes 1327112 | tf_op jit(solution)/shard_map/ppermute | solution.py:338

commit v2 on v1

--- a/solution.py
+++ b/solution.py
@@ -12,6 +12,8 @@
 HALF = 32
 LANES = 128
 SLOTS = 2
+GROUPS = 2
+CHUNKS = 4
 TY_TX = ("ty", "tx_0", "tx_1", "tx_2")
 TX = ("tx_0", "tx_1", "tx_2")
 F32 = jnp.float32
@@ -59,9 +61,28 @@
     return lax.broadcasted_iota(jnp.int32, shape, dim)
 
 
-def pack_kernel(n_tx, parts, length, tile_ref, row_ref, sums_ref, weights_ref, out_ref):
+def pack_kernel(
+    n_tx, parts, length, tile_hbm, row_hbm, sums_hbm, weights_hbm, out_hbm,
+    tile_ref, row_ref, sums_ref, weights_ref, split_ref, out_ref, in_sem, out_sem
+):
+    fetches = [
+        pltpu.make_async_copy(src, dst, in_sem.at[i])
+        for i, (src, dst) in enumerate(
+            (
+                (tile_hbm, tile_ref),
+                (row_hbm, row_ref),
+                (sums_hbm, sums_ref),
+                (weights_hbm, weights_ref),
+            )
+        )
+    ]
+    for fetch in fetches:
+        fetch.start()
+    fetches[0].wait()
+    fetches[1].wait()
     count = tile_ref.shape[1]
     devices = out_ref.shape[0] // length
+    group = devices // GROUPS
     tile = tile_ref[...]
     t = iota((devices, count), 0)
     same = tile == t
@@ -76,29 +97,24 @@
         return jnp.where(mask & (rank == float(k)), 1.0, 0.0)
 
     own = [onehot(same, k) for k in range(SLOTS)]
-    own_all = jnp.concatenate(own, axis=0).astype(BF16)
-    left_all = jnp.concatenate([onehot(from_left, k) for k in range(SLOTS)], axis=0).astype(BF16)
-    right_all = jnp.concatenate(
-        [jnp.concatenate([onehot(from_right, k), own[k]], axis=1) for k in range(SLOTS)], axis=0
-    ).astype(BF16)
-
+    left = [onehot(from_left, k) for k in range(SLOTS)]
+    right = [
+        jnp.concatenate([onehot(from_right, k), own[k]], axis=1) for k in range(SLOTS)
+    ]
+
+    def of_group(masks, g):
+        part = slice(g * group, (g + 1) * group)
+        return jnp.concatenate([m[part] for m in masks], axis=0).astype(BF16)
+
+    lane = iota((count, LANES), 1)
+    number = jnp.transpose(jnp.broadcast_to(row_ref[...].astype(F32) + 1.0, (count, count)))
     for which, ref in enumerate((sums_ref, weights_ref)):
-        for c in range(0, parts, 2):
-            x = jnp.concatenate(
-                [ref[pl.ds(c + i, count, stride=parts), :] for i in range(2)], axis=1
-            )
-            y = pick(own_all, x)
-            for k in range(SLOTS):
-                for i in range(2):
-                    at = (which * SLOTS + k) * parts + c + i
-                    out_ref[pl.ds(at, devices, stride=length), :] = y[
-                        k * devices : (k + 1) * devices, i * LANES : (i + 1) * LANES
-                    ]
-
-    lane = iota((count, LANES), 1)
-    number = jnp.transpose(
-        jnp.broadcast_to(row_ref[...].astype(F32) + 1.0, (count, count))
-    )
+        fetches[2 + which].wait()
+        for c in range(parts):
+            at = slice((which * parts + c) * LANES, (which * parts + c + 1) * LANES)
+            for i, piece in enumerate(split3(ref[pl.ds(c, count, stride=parts), :])):
+                split_ref[i, :, at] = piece
+
     last = parts - 1
     s_last = sums_ref[pl.ds(last, count, stride=parts), :]
     w_last = pltpu.roll(weights_ref[pl.ds(last, count, stride=parts), :], 64, 1)
@@ -111,17 +127,43 @@
         lane < 64, s_first, jnp.where(lane < 96, w_first, jnp.where(lane == 96, number, 0.0))
     )
     own_rows = jnp.where(lane == 97, number, 0.0)
-    to_left = pick(left_all, left_rows)
-    to_right = pick(right_all, jnp.concatenate([right_rows, own_rows], axis=0))
+    both_rows = jnp.concatenate([right_rows, own_rows], axis=0)
+
     base = 2 * SLOTS * parts
-    for k in range(SLOTS):
-        part = slice(k * devices, (k + 1) * devices)
-        out_ref[pl.ds(base + k, devices, stride=length), :] = to_left[part]
-        out_ref[pl.ds(base + SLOTS + k, devices, stride=length), :] = to_right[part]
+    sends = []
+    for g in range(GROUPS):
+        first = g * group * length
+        own_all = of_group(own, g)
+        for c in range(0, 2 * parts, 2):
+            at = slice(c * LANES, (c + 2) * LANES)
+            y = (
+                mm(own_all, split_ref[2, :, at])
+                + mm(own_all, split_ref[1, :, at])
+                + mm(own_all, split_ref[0, :, at])
+            )
+            which, chunk = divmod(c, parts)
+            for k in range(SLOTS):
+                for i in range(2):
+                    to = first + (which * SLOTS + k) * parts + chunk + i
+                    out_ref[pl.ds(to, group, stride=length), :] = y[
+                        k * group : (k + 1) * group, i * LANES : (i + 1) * LANES
+                    ]
+        to_left = pick(of_group(left, g), left_rows)
+        to_right = pick(of_group(right, g), both_rows)
+        for k in range(SLOTS):
+            part = slice(k * group, (k + 1) * group)
+            out_ref[pl.ds(first + base + k, group, stride=length), :] = to_left[part]
+            out_ref[pl.ds(first + base + SLOTS + k, group, stride=length), :] = to_right[part]
+        span = pl.ds(first, group * length)
+        send = pltpu.make_async_copy(out_ref.at[span], out_hbm.at[span], out_sem.at[g])
+        send.start()
+        sends.append(send)
+    for send in sends:
+        send.wait()
 
 
 def select_kernel(
-    parts, length, got_ref, prior_ref, prior_right_ref, prior_left_ref, s_ref, w_ref, up_ref, down_ref
+    parts, length, got_ref, prior_ref, prior_halo_ref, s_ref, w_ref, up_ref, down_ref
 ):
     rows, cols = prior_ref.shape
     devices = got_ref.shape[0] // length
@@ -164,10 +206,10 @@
     right = pick(chooser(right_t, 96), jnp.concatenate(from_right, axis=0))
     lane = iota((rows, LANES), 1)
     s_ref[:, cols:] = jnp.where(lane < 64, right, left)
-    w_ref[:, cols:] = jnp.where(
+    w_ref[:, cols:] = prior_halo_ref[...] + jnp.where(
         lane < 32,
-        pltpu.roll(right, 64, 1) + prior_right_ref[...],
-        jnp.where(lane >= 96, pltpu.roll(left, 64, 1) + prior_left_ref[...], 0.0),
+        pltpu.roll(right, 64, 1),
+        jnp.where(lane >= 96, pltpu.roll(left, 64, 1), 0.0),
     )
     up_ref[: 2 * HALF, :] = s_ref[: 2 * HALF, :]
     up_ref[2 * HALF :, :] = w_ref[:HALF, :]
@@ -251,7 +293,9 @@
     moments_ref[...] = jnp.broadcast_to(packed, moments_ref.shape)
 
 
-def final_kernel(moments_ref, s_ref, w_ref, y0_ref, y1_ref, x_ref, r_ref):
+def final_kernel(
+    moments_ref, s_ref, w_ref, y0_ref, y1_ref, x_hbm, r_hbm, x_ref, r_ref, sem
+):
     totals = jnp.sum(moments_ref[...], axis=0, keepdims=True)
     lane = iota(totals.shape, 1)
     m0, n1, n2, n3 = (
@@ -268,27 +312,39 @@
     r_r0 = a * mu - step * (0.5 * a * mu + 0.5 * beta)
     r_b0 = -a - step * (a * mu - 0.5 * a + beta)
     r_b1 = step * a
-    w = w_ref[...]
-    root = jnp.sqrt(w)
-    r0 = s_ref[...] / w
-    y0 = y0_ref[...]
-    x_ref[...] = root * (x_r0 * r0 + x_b0 * y0)
-    r_ref[...] = root * (r_r0 * r0 + r_b0 * y0 + r_b1 * y1_ref[...])
-
-
-def vmem(count):
-    return [pl.BlockSpec(memory_space=pltpu.VMEM)] * count
-
-
-def call(kernel, shapes, *args, scratch=(), name, flops=0):
+    sends = []
+    rows, cols = y0_ref.shape
+    step_rows = rows // CHUNKS
+    for c in range(CHUNKS):
+        at = slice(c * step_rows, (c + 1) * step_rows)
+        w = w_ref[at, :cols]
+        root = jnp.sqrt(w)
+        r0 = s_ref[at, :cols] / w
+        y0 = y0_ref[at, :]
+        x_ref[at, :] = root * (x_r0 * r0 + x_b0 * y0)
+        r_ref[at, :] = root * (r_r0 * r0 + r_b0 * y0 + r_b1 * y1_ref[at, :])
+        for i, (src, dst) in enumerate(((x_ref, x_hbm), (r_ref, r_hbm))):
+            send = pltpu.make_async_copy(src.at[at], dst.at[at], sem.at[c, i])
+            send.start()
+            sends.append(send)
+    for send in sends:
+        send.wait()
+
+
+VMEM = pl.BlockSpec(memory_space=pltpu.VMEM)
+ANY = pl.BlockSpec(memory_space=pl.ANY)
+HBM = pl.BlockSpec(memory_space=pltpu.HBM)
+
+
+def call(kernel, shapes, *args, ins=None, outs=None, scratch=(), name, limit=24, flops=0):
     moved = sum(int(np.prod(x.shape)) * x.dtype.itemsize for x in args)
     return pl.pallas_call(
         kernel,
         out_shape=[jax.ShapeDtypeStruct(s, F32) for s in shapes],
-        in_specs=vmem(len(args)),
-        out_specs=vmem(len(shapes)),
+        in_specs=ins or [VMEM] * len(args),
+        out_specs=outs or [VMEM] * len(shapes),
         scratch_shapes=list(scratch),
-        compiler_params=pltpu.CompilerParams(vmem_limit_bytes=40 << 20),
+        compiler_params=pltpu.CompilerParams(vmem_limit_bytes=limit << 20),
         cost_estimate=pl.CostEstimate(flops=flops, bytes_accessed=moved, transcendentals=0),
         name=name,
     )(*args)
@@ -312,6 +368,8 @@
 
     prior_right = lax.ppermute(prior_weight[:, :LANES], TX, neighbours(TX, -1))
     prior_left = lax.ppermute(prior_weight[:, cols - LANES :], TX, neighbours(TX, 1))
+    lane = jnp.arange(LANES)[None, :]
+    prior_halo = jnp.where(lane < HALF, prior_right, jnp.where(lane >= LANES - HALF, prior_left, 0.0))
 
     (message,) = call(
         functools.partial(pack_kernel, n_tx, parts, length),
@@ -320,7 +378,20 @@
         block_row.reshape(1, blocks),
         block_sums.reshape(blocks * parts, LANES),
         block_weights.reshape(blocks * parts, LANES),
+        ins=[HBM] * 4,
+        outs=[HBM],
+        scratch=[
+            pltpu.VMEM((1, blocks), jnp.int32),
+            pltpu.VMEM((1, blocks), jnp.int32),
+            pltpu.VMEM((blocks * parts, LANES), F32),
+            pltpu.VMEM((blocks * parts, LANES), F32),
+            pltpu.VMEM((3, blocks, 2 * cols), BF16),
+            pltpu.VMEM((devices * length, LANES), F32),
+            pltpu.SemaphoreType.DMA((4,)),
+            pltpu.SemaphoreType.DMA((GROUPS,)),
+        ],
         name="pack",
+        limit=63,
     )
     got = lax.all_to_all(
         message.reshape(devices, 1, length * LANES), TY_TX, split_axis=0, concat_axis=0, tiled=True
@@ -330,8 +401,7 @@
         [(rows, wide), (rows, wide), slab, slab],
         got,
         prior_weight,
-        prior_right,
-        prior_left,
+        prior_halo,
         name="select",
     )
     above = lax.ppermute(down, "ty", neighbours(("ty",), 1))
@@ -359,17 +429,23 @@
     moments = lax.all_to_all(
         moments.reshape(devices, 1, LANES), TY_TX, split_axis=0, concat_axis=0, tiled=True
     ).reshape(devices, LANES)
-    whole = lambda shape: pl.BlockSpec(shape, lambda i: (0, 0))
     return tuple(
-        pl.pallas_call(
+        call(
             final_kernel,
-            grid=(1,),
-            out_shape=[jax.ShapeDtypeStruct((rows, cols), F32)] * 2,
-            in_specs=[whole((devices, LANES))] + [whole((rows, cols))] * 4,
-            out_specs=[whole((rows, cols))] * 2,
-            compiler_params=pltpu.CompilerParams(vmem_limit_bytes=40 << 20),
+            [(rows, cols), (rows, cols)],
+            moments,
+            s,
+            w,
+            y0,
+            y1,
+            outs=[HBM, HBM],
+            scratch=[
+                pltpu.VMEM((rows, cols), F32),
+                pltpu.VMEM((rows, cols), F32),
+                pltpu.SemaphoreType.DMA((CHUNKS, 2)),
+            ],
             name="combine",
-        )(moments, s, w, y0, y1)
+        )
     )
 
 

time: 90.1 us -> 84.3 us (0.936)
  local copies, waits for them, and re-layouts: 7.84 us -> 0.05 us
  Pallas kernels: 6.14 us -> 8.23 us
  waiting for transfers between devices: 35.9 us -> 37.2 us
  blocking collectives: 19.2 us -> 18 us
    unnamed x32 -> x14, local copies, waits for them, and re-layouts: 7.83 us -> 0.03 us
    pallas_call x3 -> x4, Pallas kernels: 4.71 us -> 8.23 us  [call(): pl.pallas_call(kernel, out_shape=[jax.ShapeDtypeStruct(s, F32) for s in s...]
    pallas_call x1 -> x0, Pallas kernels: 1.43 us -> none  [shards(): pl.pallas_call(final_kernel, grid=(1,), out_shape=[jax.ShapeDtypeStruct((...]
    all_to_all x1, waiting for transfers between devices: 4.01 us -> 5.26 us  [shards(): lax.all_to_all(message.reshape(devices, 1, length * LANES), TY_TX, split_...]
    all_to_all x1, blocking collectives: 19.2 us -> 18 us  [shards(): lax.all_to_all(moments.reshape(devices, 1, LANES), TY_TX, split_axis=0, c...]
where the time goes in v2:
time: 84.3 us; the launch traced here: 84 us
  waiting for transfers between devices  37.2 us (44%)
  starting transfers between devices  19.8 us (23%)
  blocking collectives  18 us (21%)
  Pallas kernels  8.23 us (10%)
    ppermute x1, waiting for transfers between devices, shards(): prior_right = lax.ppermute(prior_weight[:, :LANES], TX, neighbours(TX, -1))  22.2 us
    all_to_all x1, blocking collectives, shards(): lax.all_to_all(moments.reshape(devices, 1, LANES), TY_TX, split_axis=0, c...  18 us
    all_to_all x1, starting transfers between devices, shards(): lax.all_to_all(message.reshape(devices, 1, length * LANES), TY_TX, split_...  11.5 us
    pallas_call x4, Pallas kernels, call(): pl.pallas_call(kernel, out_shape=[jax.ShapeDtypeStruct(s, F32) for s in s...  8.23 us
    ppermute x1, waiting for transfers between devices, shards(): above = lax.ppermute(down, 'ty', neighbours(('ty',), 1))  5.87 us
    all_to_all x1, waiting for transfers between devices, shards(): lax.all_to_all(message.reshape(devices, 1, length * LANES), TY_TX, split_...  5.26 us
    ppermute x1, waiting for transfers between devices, shards(): below = lax.ppermute(up, 'ty', neighbours(('ty',), -1))  3.86 us
    ppermute x1, starting transfers between devices, shards(): prior_right = lax.ppermute(prior_weight[:, :LANES], TX, neighbours(TX, -1))  3.11 us
  transfers between devices with their start and end apart: 5, of which 4 were waited for; matrix products, arithmetic and copies ran while one was open for 0% of the time, Pallas kernels for 0%

profile of v2, /device:TPU:1, one launch (start us, length us, event | category | flops | bytes accessed | tf_op | source)
XLA Modules:
  0.0 84.0 jit_solution(7865888483942171295)
XLA Ops:
  0.6 3.6 %pack.1 = f32[4608,128]{1,0:T(8,128)} custom-call(s32[1,128]{1,0:T(1,128)} %bitcast.16, s32[1,128]{1,0:T(1,128)} %bitcast.17, f32[1024,128]{1,0:T(8,128)} %bitcast.14, f32[1024,128]{1,0:T(8,128)} %bitcast.15), custom_call_target="tpu_custom_call" | custom-call | bytes 1049600 | tf_op jit(solution)/shard_map/pack/pallas_call | solution.py:341
  4.3 0.0 copy-start
  4.3 11.5 %all-to-all-start = ((f32[128,1,4608]{2,1,0:T(1,128)}), f32[128,1,4608]{2,1,0:T(1,128)S(1)}, u32[]{:S(2)}, u32[]{:S(2)}) async-start(f32[128,1,4608]{2,1,0:T(1,128)} %bitcast.13), calls=%async_computation | async-start | bytes 4718592 | tf_op jit(solution)/shard_map/all_to_all | solution.py:396
  15.8 0.0 copy-done
  15.8 0.0 copy-start.1
  15.8 0.0 copy-start.2
  15.8 3.1 %collective-permute-start = (f32[128,128]{1,0:T(8,128)S(1)}, f32[128,128]{1,0:T(8,128)S(1)}, u32[]{:S(2)}, u32[]{:S(2)}) collective-permute-start(f32[128,128]{1,0:T(8,128)S(1)} %get-tuple-element.17), channel_id=1, source_target_pairs={{1,0},{2,1},{3,2},{4,3},{5,4},{6,5},{7,6},{8,7},{9,8},{10,9},{11,1... | collective-permute-start | bytes 196616 | tf_op jit(solution)/shard_map/ppermute | solution.py:369
  18.9 2.6 %collective-permute-start.1 = (f32[128,128]{1,0:T(8,128)S(1)}, f32[128,128]{1,0:T(8,128)S(1)}, u32[]{:S(2)}, u32[]{:S(2)}) collective-permute-start(f32[128,128]{1,0:T(8,128)S(1)} %get-tuple-element.16), channel_id=1, source_target_pairs={{0,1},{1,2},{2,3},{3,4},{4,5},{5,6},{6,7},{7,8},{8,9},{9,10},{10,1... | collective-permute-start | bytes 196616 | tf_op jit(solution)/shard_map/ppermute | solution.py:370
  21.6 22.2 %collective-permute-done = f32[128,128]{1,0:T(8,128)S(1)} collective-permute-done((f32[128,128]{1,0:T(8,128)S(1)}, f32[128,128]{1,0:T(8,128)S(1)}, u32[]{:S(2)}, u32[]{:S(2)}) %collective-permute-start) | collective-permute-done | bytes 65568 | tf_op jit(solution)/shard_map/ppermute | solution.py:369
  43.7 0.0 collective-permute-done.1
  43.7 5.3 %all-to-all-done = f32[128,1,4608]{2,1,0:T(1,128)S(1)} async-done(((f32[128,1,4608]{2,1,0:T(1,128)}), f32[128,1,4608]{2,1,0:T(1,128)S(1)}, u32[]{:S(2)}, u32[]{:S(2)}) %all-to-all-start) | async-done | bytes 2359328 | tf_op jit(solution)/shard_map/all_to_all | solution.py:396
  49.0 0.0 copy-start.3
  49.0 0.0 copy-start.4
  49.0 0.0 copy-start.5
  49.0 0.0 copy-start.6
  49.0 1.0 %select.1 = (f32[128,1152]{1,0:T(8,128)S(1)}, f32[128,1152]{1,0:T(8,128)S(1)}, f32[96,1152]{1,0:T(8,128)S(1)}, f32[96,1152]{1,0:T(8,128)S(1)}) custom-call(f32[4608,128]{1,0:T(8,128)S(1)} %bitcast.10, f32[128,1024]{1,0:T(8,128)S(1)} %copy-done, f32[128,128]{1,0:T(8,128)S(1)} %select_select_fusion.prior_halo_ref), custom_call_target="tpu_custom_call" | custom-call | bytes 2949120 | tf_op jit(solution)/shard_map/select/pallas_call | solution.py:341
  50.0 1.3 %collective-permute-start.2 = (f32[96,1152]{1,0:T(8,128)S(1)}, f32[96,1152]{1,0:T(8,128)S(1)}, u32[]{:S(2)}, u32[]{:S(2)}) collective-permute-start(f32[96,1152]{1,0:T(8,128)S(1)} %get-tuple-element.11), channel_id=1, source_target_pairs={{0,32},{32,64},{64,96},{1,33},{33,65},{65,97},{2,34},{34,66},{66,9... | collective-permute-start | bytes 1327112 | tf_op jit(solution)/shard_map/ppermute | solution.py:407
  51.3 1.3 %collective-permute-start.3 = (f32[96,1152]{1,0:T(8,128)S(1)}, f32[96,1152]{1,0:T(8,128)S(1)}, u32[]{:S(2)}, u32[]{:S(2)}) collective-permute-start(f32[96,1152]{1,0:T(8,128)S(1)} %get-tuple-element.12), channel_id=1, source_target_pairs={{32,0},{64,32},{96,64},{33,1},{65,33},{97,65},{34,2},{66,34},{98,6... | collective-permute-start | bytes 1327112 | tf_op jit(solution)/shard_map/ppermute | solution.py:408
  52.6 5.9 %collective-permute-done.2.above_ref = f32[96,1152]{1,0:T(8,128)S(1)} collective-permute-done((f32[96,1152]{1,0:T(8,128)S(1)}, f32[96,1152]{1,0:T(8,128)S(1)}, u32[]{:S(2)}, u32[]{:S(2)}) %collective-permute-start.2) | collective-permute-done | bytes 442400 | tf_op jit(solution)/shard_map/ppermute | solution.py:407
  58.5 3.9 %collective-permute-done.3.below_ref = f32[96,1152]{1,0:T(8,128)S(1)} collective-permute-done((f32[96,1152]{1,0:T(8,128)S(1)}, f32[96,1152]{1,0:T(8,128)S(1)}, u32[]{:S(2)}, u32[]{:S(2)}) %collective-permute-start.3) | collective-permute-done | bytes 442400 | tf_op jit(solution)/shard_map/ppermute | solution.py:408
  62.3 0.0 copy-done.1
  62.3 0.0 copy-done.2
  62.3 0.0 copy-done.3
  62.4 0.0 copy-done.4
  62.4 0.0 copy-done.5
  62.4 0.0 copy-done.6
  62.4 2.5 %smooth.1 = (f32[128,1024]{1,0:T(8,128)S(1)}, f32[128,1024]{1,0:T(8,128)S(1)}, f32[128,128]{1,0:T(8,128)S(1)}) custom-call(f32[128,1152]{1,0:T(8,128)S(1)} %get-tuple-element.9.s_ref, f32[128,1152]{1,0:T(8,128)S(1)} %get-tuple-element.10.w_ref, f32[96,1152]{1,0:T(8,128)S(1)} %collective-permute-done.2.above_ref, ...), custom_call_target="tpu_custom_call" | custom-call | bytes 2981888 | tf_op jit(solution)/shard_map/smooth/pallas_call | solution.py:341
  64.9 18.0 %all_to_all.10 = f32[128,1,128]{2,1,0:T(1,128)S(1)} all-to-all(f32[128,1,128]{2,1,0:T(1,128)S(1)} %bitcast.12), channel_id=1, replica_groups=mesh['ty'=4,'tx_0'=4,'tx_1'=4,'tx_2'=2] {'ty','tx_0','tx_1','tx_2'}, dimensions={0} | all-to-all | bytes 131072 | tf_op jit(solution)/shard_map/all_to_all | solution.py:429
  82.9 1.2 %combine.1 = (f32[128,1024]{1,0:T(8,128)}, f32[128,1024]{1,0:T(8,128)}) custom-call(f32[128,128]{1,0:T(8,128)S(1)} %bitcast.11, f32[128,1152]{1,0:T(8,128)S(1)} %get-tuple-element.9.s_ref, f32[128,1152]{1,0:T(8,128)S(1)} %get-tuple-element.10.w_ref, f32[128,1024]{1,0:T(8,128)S(1)} %get-tuple-element.14.y0_ref, f32[128,1024]{1,0:T(8,128)S(1)} %get-tuple-element.15.y1_ref), custom_call_target="tpu_custom_call" | custom-call | bytes 2293760 | tf_op jit(solution)/shard_map/combine/pallas_call | solution.py:341
  (3 shorter events, 0.0 us)
Async XLA Ops:
  4.3 11.5 %copy-start = (f32[128,1024]{1,0:T(8,128)S(1)}, f32[128,1024]{1,0:T(8,128)}, u32[]{:S(2)}) copy-start(f32[128,1024]{1,0:T(8,128)} %prior_ref.1) | copy-start | bytes 1572868
  4.3 44.7 %all-to-all-start = ((f32[128,1,4608]{2,1,0:T(1,128)}), f32[128,1,4608]{2,1,0:T(1,128)S(1)}, u32[]{:S(2)}, u32[]{:S(2)}) async-start(f32[128,1,4608]{2,1,0:T(1,128)} %bitcast.13), calls=%async_computation | async-start | bytes 4718592 | tf_op jit(solution)/shard_map/all_to_all | solution.py:396
  15.8 46.6 %copy-start.1 = (bf16[512,256]{1,0:T(8,128)(2,1)S(1)}, bf16[512,256]{1,0:T(8,128)(2,1)}, u32[]{:S(2)}) copy-start(bf16[512,256]{1,0:T(8,128)(2,1)} %constant.20.clone.col_h_ref) | copy-start | bytes 786436
  15.8 46.5 %copy-start.2 = (bf16[512,256]{1,0:T(8,128)(2,1)S(1)}, bf16[512,256]{1,0:T(8,128)(2,1)}, u32[]{:S(2)}) copy-start(bf16[512,256]{1,0:T(8,128)(2,1)} %constant.21.clone.col_l_ref) | copy-start | bytes 786436
  15.8 27.9 %collective-permute-start = (f32[128,128]{1,0:T(8,128)S(1)}, f32[128,128]{1,0:T(8,128)S(1)}, u32[]{:S(2)}, u32[]{:S(2)}) collective-permute-start(f32[128,128]{1,0:T(8,128)S(1)} %get-tuple-element.17), channel_id=1, source_target_pairs={{1,0},{2,1},{3,2},{4,3},{5,4},{6,5},{7,6},{8,7},{9,8},{10,9},{11,1... | collective-permute-start | bytes 196616 | tf_op jit(solution)/shard_map/ppermute | solution.py:369
  18.9 24.8 %collective-permute-start.1 = (f32[128,128]{1,0:T(8,128)S(1)}, f32[128,128]{1,0:T(8,128)S(1)}, u32[]{:S(2)}, u32[]{:S(2)}) collective-permute-start(f32[128,128]{1,0:T(8,128)S(1)} %get-tuple-element.16), channel_id=1, source_target_pairs={{0,1},{1,2},{2,3},{3,4},{4,5},{5,6},{6,7},{7,8},{8,9},{9,10},{10,1... | collective-permute-start | bytes 196616 | tf_op jit(solution)/shard_map/ppermute | solution.py:370
  49.0 13.3 %copy-start.3 = (bf16[192,256]{1,0:T(8,128)(2,1)S(1)}, bf16[192,256]{1,0:T(8,128)(2,1)}, u32[]{:S(2)}) copy-start(bf16[192,256]{1,0:T(8,128)(2,1)} %constant.18.clone.row_h_ref) | copy-start | bytes 294916
  49.0 13.4 %copy-start.4 = (bf16[192,256]{1,0:T(8,128)(2,1)S(1)}, bf16[192,256]{1,0:T(8,128)(2,1)}, u32[]{:S(2)}) copy-start(bf16[192,256]{1,0:T(8,128)(2,1)} %constant.19.clone.row_l_ref) | copy-start | bytes 294916
  49.0 13.4 %copy-start.5 = (bf16[384,128]{1,0:T(8,128)(2,1)S(1)}, bf16[384,128]{1,0:T(8,128)(2,1)}, u32[]{:S(2)}) copy-start(bf16[384,128]{1,0:T(8,128)(2,1)} %constant.22.clone.edge_h_ref) | copy-start | bytes 294916
  49.0 13.4 %copy-start.6 = (bf16[384,128]{1,0:T(8,128)(2,1)S(1)}, bf16[384,128]{1,0:T(8,128)(2,1)}, u32[]{:S(2)}) copy-start(bf16[384,128]{1,0:T(8,128)(2,1)} %constant.23.clone.edge_l_ref) | copy-start | bytes 294916
  50.0 8.5 %collective-permute-start.2 = (f32[96,1152]{1,0:T(8,128)S(1)}, f32[96,1152]{1,0:T(8,128)S(1)}, u32[]{:S(2)}, u32[]{:S(2)}) collective-permute-start(f32[96,1152]{1,0:T(8,128)S(1)} %get-tuple-element.11), channel_id=1, source_target_pairs={{0,32},{32,64},{64,96},{1,33},{33,65},{65,97},{2,34},{34,66},{66,9... | collective-permute-start | bytes 1327112 | tf_op jit(solution)/shard_map/ppermute | solution.py:407
  51.3 11.0 %collective-permute-start.3 = (f32[96,1152]{1,0:T(8,128)S(1)}, f32[96,1152]{1,0:T(8,128)S(1)}, u32[]{:S(2)}, u32[]{:S(2)}) collective-permute-start(f32[96,1152]{1,0:T(8,128)S(1)} %get-tuple-element.12), channel_id=1, source_target_pairs={{32,0},{64,32},{96,64},{33,1},{65,33},{97,65},{34,2},{66,34},{98,6... | collective-permute-start | bytes 1327112 | tf_op jit(solution)/shard_map/ppermute | solution.py:408

commit v3 on v2

--- a/solution.py
+++ b/solution.py
@@ -206,10 +206,14 @@
     right = pick(chooser(right_t, 96), jnp.concatenate(from_right, axis=0))
     lane = iota((rows, LANES), 1)
     s_ref[:, cols:] = jnp.where(lane < 64, right, left)
-    w_ref[:, cols:] = prior_halo_ref[...] + jnp.where(
+    column = lax.axis_index(TX)
+    has_left = jnp.where(column > 0, 1.0, 0.0)
+    has_right = jnp.where(column < lax.axis_size(TX) - 1, 1.0, 0.0)
+    prior_halo = prior_halo_ref[...]
+    w_ref[:, cols:] = jnp.where(
         lane < 32,
-        pltpu.roll(right, 64, 1),
-        jnp.where(lane >= 96, pltpu.roll(left, 64, 1), 0.0),
+        prior_halo * has_right + pltpu.roll(right, 64, 1),
+        jnp.where(lane >= 96, prior_halo * has_left + pltpu.roll(left, 64, 1), 0.0),
     )
     up_ref[: 2 * HALF, :] = s_ref[: 2 * HALF, :]
     up_ref[2 * HALF :, :] = w_ref[:HALF, :]
@@ -218,6 +222,7 @@
 
 
 def conv_kernel(
+    n_ty,
     s_ref,
     w_ref,
     above_ref,
@@ -239,6 +244,16 @@
     tall = rows + 2 * HALF
     col = (col_h_ref[...], col_l_ref[...])
     edge = (edge_h_ref[...], edge_l_ref[...])
+    row_at = lax.axis_index("ty")
+    has_above = jnp.where(row_at > 0, 1.0, 0.0)
+    has_below = jnp.where(row_at < n_ty - 1, 1.0, 0.0)
+
+    def with_halo(part, at, ref):
+        above = above_ref[part, at] * has_above
+        below = below_ref[part, at] * has_below
+        return jnp.concatenate([above, ref[:, at], below], axis=0)
+
+    sums, weights = slice(0, 2 * HALF), slice(2 * HALF, 3 * HALF)
 
     def block(ref, c, height):
         lo, hi = (c - 1) * LANES, (c + 3) * LANES
@@ -251,18 +266,14 @@
     row = (row_h_ref[...], row_l_ref[...])
     for c in range(0, wide, LANES * 3):
         at = slice(c, c + LANES * 3)
-        full = jnp.concatenate(
-            [above_ref[: 2 * HALF, at], s_ref[:, at], below_ref[: 2 * HALF, at]], axis=0
-        )
-        mid_ref[:, at] = smooth3(row, split2(full))
+        mid_ref[:, at] = smooth3(row, split2(with_halo(sums, at, s_ref)))
     total_sy = jnp.zeros((rows, 2 * LANES), F32)
     total_zy = jnp.zeros((rows, 2 * LANES), F32)
     total_ss = jnp.zeros((rows, 2 * LANES), F32)
     for c in range(0, cols // LANES, 2):
         at = slice(c * LANES, (c + 2) * LANES)
         y = block(mid_ref, c, tall)
-        w = jnp.concatenate([above_ref[2 * HALF :, at], w_ref[:, at], below_ref[2 * HALF :, at]], axis=0)
-        z = w * y
+        z = with_halo(weights, at, w_ref) * y
         z_ref[:, at] = z
         inner = y[HALF : HALF + rows]
         y0_ref[:, at] = inner
@@ -272,8 +283,7 @@
         total_ss += s * s / w_ref[:, at]
     x = jnp.concatenate([mid_ref[:, cols - LANES :], mid_ref[:, :LANES]], axis=1)
     y = smooth3(split2(x), edge)
-    w = jnp.concatenate([above_ref[2 * HALF :, cols:], w_ref[:, cols:], below_ref[2 * HALF :, cols:]], axis=0)
-    z_ref[:, cols:] = w * y
+    z_ref[:, cols:] = with_halo(weights, slice(cols, wide), w_ref) * y
 
     row = (row_h_ref[:rows, :tall], row_l_ref[:rows, :tall])
     for c in range(0, wide, LANES * 3):
@@ -352,8 +362,7 @@
 
 def neighbours(axes, step):
     count = int(np.prod([lax.axis_size(a) for a in axes]))
-    pairs = [(i, i + 1) for i in range(count - 1)]
-    return pairs if step > 0 else [(b, a) for a, b in pairs]
+    return [(i, (i + step) % count) for i in range(count)]
 
 
 def shards(block_sums, block_weights, block_tile, block_row, prior_weight):
@@ -414,7 +423,7 @@
     near = np.concatenate([np.arange(cols - LANES, cols), ring, np.arange(LANES)])
     edge_taps = taps(ring[None, :] - near[:, None])
     y0, y1, moments = call(
-        conv_kernel,
+        functools.partial(conv_kernel, lax.axis_size("ty")),
         [(rows, cols), (rows, cols), (devices, LANES)],
         s,
         w,

time: 84.3 us -> 82.4 us (0.977)
  starting transfers between devices: 19.8 us -> 16.1 us
  waiting for transfers between devices: 37.2 us -> 39.8 us
    ppermute x1, waiting for transfers between devices: 22.2 us -> 26.1 us  [shards(): prior_right = lax.ppermute(prior_weight[:, :LANES], TX, neighbours(TX, -1))]
    ppermute x1, waiting for transfers between devices: 3.86 us -> 0.01 us  [shards(): below = lax.ppermute(up, 'ty', neighbours(('ty',), -1))]
    ppermute x1, waiting for transfers between devices: 5.87 us -> 8.55 us  [shards(): above = lax.ppermute(down, 'ty', neighbours(('ty',), 1))]
    ppermute x1, starting transfers between devices: 3.11 us -> 1.14 us  [shards(): prior_right = lax.ppermute(prior_weight[:, :LANES], TX, neighbours(TX, -1))]
    ppermute x1, starting transfers between devices: 2.59 us -> 0.68 us  [shards(): lax.ppermute(prior_weight[:, cols - LANES:], TX, neighbours(TX, 1))]
    ppermute x1, starting transfers between devices: 1.29 us -> 2.66 us  [shards(): below = lax.ppermute(up, 'ty', neighbours(('ty',), -1))]
    ppermute x1, starting transfers between devices: 1.32 us -> 0.07 us  [shards(): above = lax.ppermute(down, 'ty', neighbours(('ty',), 1))]
  transfers between devices with their start and end apart: 5 -> 5, of which waited for: 4 -> 3; matrix products, arithmetic and copies ran while one was open for 0% -> 0% of each run, Pallas kernels for 0% -> 0%
where the time goes in v3:
time: 82.4 us; the launch traced here: 82.2 us
  waiting for transfers between devices  39.8 us (48%)
  blocking collectives  17.3 us (21%)
  starting transfers between devices  16.1 us (20%)
  Pallas kernels  8.25 us (10%)
    ppermute x1, waiting for transfers between devices, shards(): prior_right = lax.ppermute(prior_weight[:, :LANES], TX, neighbours(TX, -1))  26.1 us
    all_to_all x1, blocking collectives, shards(): lax.all_to_all(moments.reshape(devices, 1, LANES), TY_TX, split_axis=0, c...  17.3 us
    all_to_all x1, starting transfers between devices, shards(): lax.all_to_all(message.reshape(devices, 1, length * LANES), TY_TX, split_...  11.5 us
    ppermute x1, waiting for transfers between devices, shards(): above = lax.ppermute(down, 'ty', neighbours(('ty',), 1))  8.55 us
    pallas_call x4, Pallas kernels, call(): pl.pallas_call(kernel, out_shape=[jax.ShapeDtypeStruct(s, F32) for s in s...  8.25 us
    all_to_all x1, waiting for transfers between devices, shards(): lax.all_to_all(message.reshape(devices, 1, length * LANES), TY_TX, split_...  5.13 us
    ppermute x1, starting transfers between devices, shards(): below = lax.ppermute(up, 'ty', neighbours(('ty',), -1))  2.66 us
  transfers between devices with their start and end apart: 5, of which 3 were waited for; matrix products, arithmetic and copies ran while one was open for 0% of the time, Pallas kernels for 0%

profile of v3, /device:TPU:1, one launch (start us, length us, event | category | flops | bytes accessed | tf_op | source)
XLA Modules:
  0.0 82.2 jit_solution(10195608874973127668)
XLA Ops:
  0.6 3.6 %pack.1 = f32[4608,128]{1,0:T(8,128)} custom-call(s32[1,128]{1,0:T(1,128)} %bitcast.16, s32[1,128]{1,0:T(1,128)} %bitcast.17, f32[1024,128]{1,0:T(8,128)} %bitcast.14, f32[1024,128]{1,0:T(8,128)} %bitcast.15), custom_call_target="tpu_custom_call" | custom-call | bytes 1049600 | tf_op jit(solution)/shard_map/pack/pallas_call | solution.py:351
  4.3 0.0 copy-start
  4.3 11.5 %all-to-all-start = ((f32[128,1,4608]{2,1,0:T(1,128)}), f32[128,1,4608]{2,1,0:T(1,128)S(1)}, u32[]{:S(2)}, u32[]{:S(2)}) async-start(f32[128,1,4608]{2,1,0:T(1,128)} %bitcast.13), calls=%async_computation | async-start | bytes 4718592 | tf_op jit(solution)/shard_map/all_to_all | solution.py:405
  15.8 0.0 copy-done
  15.8 0.0 copy-start.1
  15.8 0.0 copy-start.2
  15.8 1.1 %collective-permute-start = (f32[128,128]{1,0:T(8,128)S(1)}, f32[128,128]{1,0:T(8,128)S(1)}, u32[]{:S(2)}, u32[]{:S(2)}) collective-permute-start(f32[128,128]{1,0:T(8,128)S(1)} %get-tuple-element.17), channel_id=1, source_target_pairs={{0,31},{1,0},{2,1},{3,2},{4,3},{5,4},{6,5},{7,6},{8,7},{9,8},{10,9... | collective-permute-start | bytes 196616 | tf_op jit(solution)/shard_map/ppermute | solution.py:378
  17.0 0.7 collective-permute-start.1
  17.6 26.1 %collective-permute-done = f32[128,128]{1,0:T(8,128)S(1)} collective-permute-done((f32[128,128]{1,0:T(8,128)S(1)}, f32[128,128]{1,0:T(8,128)S(1)}, u32[]{:S(2)}, u32[]{:S(2)}) %collective-permute-start) | collective-permute-done | bytes 65568 | tf_op jit(solution)/shard_map/ppermute | solution.py:378
  43.7 0.0 collective-permute-done.1
  43.7 5.1 %all-to-all-done = f32[128,1,4608]{2,1,0:T(1,128)S(1)} async-done(((f32[128,1,4608]{2,1,0:T(1,128)}), f32[128,1,4608]{2,1,0:T(1,128)S(1)}, u32[]{:S(2)}, u32[]{:S(2)}) %all-to-all-start) | async-done | bytes 2359328 | tf_op jit(solution)/shard_map/all_to_all | solution.py:405
  48.9 0.0 copy-start.3
  48.9 0.0 copy-start.4
  48.9 0.0 copy-start.5
  48.9 0.0 copy-start.6
  48.9 1.0 %select.1 = (f32[128,1152]{1,0:T(8,128)S(1)}, f32[128,1152]{1,0:T(8,128)S(1)}, f32[96,1152]{1,0:T(8,128)S(1)}, f32[96,1152]{1,0:T(8,128)S(1)}) custom-call(f32[4608,128]{1,0:T(8,128)S(1)} %bitcast.10, f32[128,1024]{1,0:T(8,128)S(1)} %copy-done, f32[128,128]{1,0:T(8,128)S(1)} %select_select_fusion.prior_halo_ref), custom_call_target="tpu_custom_call" | custom-call | bytes 2949120 | tf_op jit(solution)/shard_map/select/pallas_call | solution.py:351
  49.9 0.1 collective-permute-start.2
  49.9 2.7 %collective-permute-start.3 = (f32[96,1152]{1,0:T(8,128)S(1)}, f32[96,1152]{1,0:T(8,128)S(1)}, u32[]{:S(2)}, u32[]{:S(2)}) collective-permute-start(f32[96,1152]{1,0:T(8,128)S(1)} %get-tuple-element.12), channel_id=1, source_target_pairs={{0,96},{32,0},{64,32},{96,64},{1,97},{33,1},{65,33},{97,65},{2,98}... | collective-permute-start | bytes 1327112 | tf_op jit(solution)/shard_map/ppermute | solution.py:417
  52.6 8.6 %collective-permute-done.2.above_ref = f32[96,1152]{1,0:T(8,128)S(1)} collective-permute-done((f32[96,1152]{1,0:T(8,128)S(1)}, f32[96,1152]{1,0:T(8,128)S(1)}, u32[]{:S(2)}, u32[]{:S(2)}) %collective-permute-start.2) | collective-permute-done | bytes 442400 | tf_op jit(solution)/shard_map/ppermute | solution.py:416
  61.2 0.0 collective-permute-done.3.below_ref
  61.2 0.0 copy-done.1
  61.2 0.0 copy-done.2
  61.2 0.0 copy-done.3
  61.2 0.0 copy-done.4
  61.2 0.0 copy-done.5
  61.2 0.0 copy-done.6
  61.2 2.5 %smooth.1 = (f32[128,1024]{1,0:T(8,128)S(1)}, f32[128,1024]{1,0:T(8,128)S(1)}, f32[128,128]{1,0:T(8,128)S(1)}) custom-call(f32[128,1152]{1,0:T(8,128)S(1)} %get-tuple-element.9.s_ref, f32[128,1152]{1,0:T(8,128)S(1)} %get-tuple-element.10.w_ref, f32[96,1152]{1,0:T(8,128)S(1)} %collective-permute-done.2.above_ref, ...), custom_call_target="tpu_custom_call" | custom-call | bytes 2981888 | tf_op jit(solution)/shard_map/smooth/pallas_call | solution.py:351
  63.7 17.3 %all_to_all.10 = f32[128,1,128]{2,1,0:T(1,128)S(1)} all-to-all(f32[128,1,128]{2,1,0:T(1,128)S(1)} %bitcast.12), channel_id=1, replica_groups=mesh['ty'=4,'tx_0'=4,'tx_1'=4,'tx_2'=2] {'ty','tx_0','tx_1','tx_2'}, dimensions={0} | all-to-all | bytes 131072 | tf_op jit(solution)/shard_map/all_to_all | solution.py:438
  81.0 1.2 %combine.1 = (f32[128,1024]{1,0:T(8,128)}, f32[128,1024]{1,0:T(8,128)}) custom-call(f32[128,128]{1,0:T(8,128)S(1)} %bitcast.11, f32[128,1152]{1,0:T(8,128)S(1)} %get-tuple-element.9.s_ref, f32[128,1152]{1,0:T(8,128)S(1)} %get-tuple-element.10.w_ref, f32[128,1024]{1,0:T(8,128)S(1)} %get-tuple-element.14.y0_ref, f32[128,1024]{1,0:T(8,128)S(1)} %get-tuple-element.15.y1_ref), custom_call_target="tpu_custom_call" | custom-call | bytes 2293760 | tf_op jit(solution)/shard_map/combine/pallas_call | solution.py:351
  (3 shorter events, 0.0 us)
Async XLA Ops:
  4.3 11.5 %copy-start = (f32[128,1024]{1,0:T(8,128)S(1)}, f32[128,1024]{1,0:T(8,128)}, u32[]{:S(2)}) copy-start(f32[128,1024]{1,0:T(8,128)} %prior_ref.1) | copy-start | bytes 1572868
  4.3 44.6 %all-to-all-start = ((f32[128,1,4608]{2,1,0:T(1,128)}), f32[128,1,4608]{2,1,0:T(1,128)S(1)}, u32[]{:S(2)}, u32[]{:S(2)}) async-start(f32[128,1,4608]{2,1,0:T(1,128)} %bitcast.13), calls=%async_computation | async-start | bytes 4718592 | tf_op jit(solution)/shard_map/all_to_all | solution.py:405
  15.8 45.4 %copy-start.1 = (bf16[512,256]{1,0:T(8,128)(2,1)S(1)}, bf16[512,256]{1,0:T(8,128)(2,1)}, u32[]{:S(2)}) copy-start(bf16[512,256]{1,0:T(8,128)(2,1)} %constant.20.clone.col_h_ref) | copy-start | bytes 786436
  15.8 45.4 %copy-start.2 = (bf16[512,256]{1,0:T(8,128)(2,1)S(1)}, bf16[512,256]{1,0:T(8,128)(2,1)}, u32[]{:S(2)}) copy-start(bf16[512,256]{1,0:T(8,128)(2,1)} %constant.21.clone.col_l_ref) | copy-start | bytes 786436
  15.8 27.9 %collective-permute-start = (f32[128,128]{1,0:T(8,128)S(1)}, f32[128,128]{1,0:T(8,128)S(1)}, u32[]{:S(2)}, u32[]{:S(2)}) collective-permute-start(f32[128,128]{1,0:T(8,128)S(1)} %get-tuple-element.17), channel_id=1, source_target_pairs={{0,31},{1,0},{2,1},{3,2},{4,3},{5,4},{6,5},{7,6},{8,7},{9,8},{10,9... | collective-permute-start | bytes 196616 | tf_op jit(solution)/shard_map/ppermute | solution.py:378
  17.0 26.8 %collective-permute-start.1 = (f32[128,128]{1,0:T(8,128)S(1)}, f32[128,128]{1,0:T(8,128)S(1)}, u32[]{:S(2)}, u32[]{:S(2)}) collective-permute-start(f32[128,128]{1,0:T(8,128)S(1)} %get-tuple-element.16), channel_id=1, source_target_pairs={{0,1},{1,2},{2,3},{3,4},{4,5},{5,6},{6,7},{7,8},{8,9},{9,10},{10,1... | collective-permute-start | bytes 196616 | tf_op jit(solution)/shard_map/ppermute | solution.py:379
  48.9 12.3 %copy-start.3 = (bf16[192,256]{1,0:T(8,128)(2,1)S(1)}, bf16[192,256]{1,0:T(8,128)(2,1)}, u32[]{:S(2)}) copy-start(bf16[192,256]{1,0:T(8,128)(2,1)} %constant.18.clone.row_h_ref) | copy-start | bytes 294916
  48.9 12.3 %copy-start.4 = (bf16[192,256]{1,0:T(8,128)(2,1)S(1)}, bf16[192,256]{1,0:T(8,128)(2,1)}, u32[]{:S(2)}) copy-start(bf16[192,256]{1,0:T(8,128)(2,1)} %constant.19.clone.row_l_ref) | copy-start | bytes 294916
  48.9 12.3 %copy-start.5 = (bf16[384,128]{1,0:T(8,128)(2,1)S(1)}, bf16[384,128]{1,0:T(8,128)(2,1)}, u32[]{:S(2)}) copy-start(bf16[384,128]{1,0:T(8,128)(2,1)} %constant.22.clone.edge_h_ref) | copy-start | bytes 294916
  48.9 12.3 %copy-start.6 = (bf16[384,128]{1,0:T(8,128)(2,1)S(1)}, bf16[384,128]{1,0:T(8,128)(2,1)}, u32[]{:S(2)}) copy-start(bf16[384,128]{1,0:T(8,128)(2,1)} %constant.23.clone.edge_l_ref) | copy-start | bytes 294916
  49.9 11.3 %collective-permute-start.2 = (f32[96,1152]{1,0:T(8,128)S(1)}, f32[96,1152]{1,0:T(8,128)S(1)}, u32[]{:S(2)}, u32[]{:S(2)}) collective-permute-start(f32[96,1152]{1,0:T(8,128)S(1)} %get-tuple-element.11), channel_id=1, source_target_pairs={{0,32},{32,64},{64,96},{96,0},{1,33},{33,65},{65,97},{97,1},{2,34}... | collective-permute-start | bytes 1327112 | tf_op jit(solution)/shard_map/ppermute | solution.py:416
  49.9 11.2 %collective-permute-start.3 = (f32[96,1152]{1,0:T(8,128)S(1)}, f32[96,1152]{1,0:T(8,128)S(1)}, u32[]{:S(2)}, u32[]{:S(2)}) collective-permute-start(f32[96,1152]{1,0:T(8,128)S(1)} %get-tuple-element.12), channel_id=1, source_target_pairs={{0,96},{32,0},{64,32},{96,64},{1,97},{33,1},{65,33},{97,65},{2,98}... | collective-permute-start | bytes 1327112 | tf_op jit(solution)/shard_map/ppermute | solution.py:417

commit v4 on v3

--- a/solution.py
+++ b/solution.py
@@ -163,7 +163,8 @@
 
 
 def select_kernel(
-    parts, length, got_ref, prior_ref, prior_halo_ref, s_ref, w_ref, up_ref, down_ref
+    parts, length, got_ref, prior_ref, prior_halo_ref, s_ref, w_ref, s_up_ref, s_down_ref,
+    w_up_ref, w_down_ref
 ):
     rows, cols = prior_ref.shape
     devices = got_ref.shape[0] // length
@@ -215,13 +216,30 @@
         prior_halo * has_right + pltpu.roll(right, 64, 1),
         jnp.where(lane >= 96, prior_halo * has_left + pltpu.roll(left, 64, 1), 0.0),
     )
-    up_ref[: 2 * HALF, :] = s_ref[: 2 * HALF, :]
-    up_ref[2 * HALF :, :] = w_ref[:HALF, :]
-    down_ref[: 2 * HALF, :] = s_ref[rows - 2 * HALF :, :]
-    down_ref[2 * HALF :, :] = w_ref[rows - HALF :, :]
-
-
-def conv_kernel(
+    s_up_ref[...] = s_ref[: 2 * HALF, :]
+    s_down_ref[...] = s_ref[rows - 2 * HALF :, :]
+    w_up_ref[...] = w_ref[:HALF, :]
+    w_down_ref[...] = w_ref[rows - HALF :, :]
+
+
+def with_halo(n_ty, above_ref, ref, below_ref, at):
+    row_at = lax.axis_index("ty")
+    above = above_ref[:, at] * jnp.where(row_at > 0, 1.0, 0.0)
+    below = below_ref[:, at] * jnp.where(row_at < n_ty - 1, 1.0, 0.0)
+    return jnp.concatenate([above, ref[:, at], below], axis=0)
+
+
+def along_columns(mid_ref, c, height, col):
+    cols = mid_ref.shape[1] - LANES
+    lo, hi = (c - 1) * LANES, (c + 3) * LANES
+    if c == 0:
+        x = jnp.concatenate([mid_ref[:height, cols:], mid_ref[:height, :hi]], axis=1)
+    else:
+        x = mid_ref[:height, lo:hi]
+    return smooth3(split2(x), col)
+
+
+def first_kernel(
     n_ty,
     s_ref,
     w_ref,
@@ -234,7 +252,50 @@
     edge_h_ref,
     edge_l_ref,
     y0_ref,
-    y1_ref,
+    root_ref,
+    r0_ref,
+    m0_ref,
+    mid_ref,
+):
+    rows, wide = s_ref.shape
+    cols = wide - LANES
+    tall = rows + 2 * HALF
+    row = (row_h_ref[...], row_l_ref[...])
+    col = (col_h_ref[...], col_l_ref[...])
+    for c in range(0, wide, LANES * 3):
+        at = slice(c, c + LANES * 3)
+        mid_ref[:, at] = smooth3(row, split2(with_halo(n_ty, above_ref, s_ref, below_ref, at)))
+    for c in range(0, cols // LANES, 2):
+        at = slice(c * LANES, (c + 2) * LANES)
+        y0_ref[:, at] = along_columns(mid_ref, c, tall, col)
+    x = jnp.concatenate([mid_ref[:, cols - LANES :], mid_ref[:, :LANES]], axis=1)
+    y0_ref[:, cols:] = smooth3(split2(x), (edge_h_ref[...], edge_l_ref[...]))
+    total = jnp.zeros((8, cols), F32)
+    for r in range(0, rows, 8):
+        at = slice(r, r + 8)
+        root = jnp.sqrt(w_ref[at, :cols])
+        r0 = s_ref[at, :cols] / root
+        root_ref[at, :] = root
+        r0_ref[at, :] = r0
+        total += r0 * r0
+    m0_ref[...] = sum(total[:, c : c + LANES] for c in range(0, cols, LANES))
+
+
+def second_kernel(
+    n_ty,
+    s_ref,
+    w_ref,
+    above_ref,
+    below_ref,
+    y0_ref,
+    root_ref,
+    m0_ref,
+    row_h_ref,
+    row_l_ref,
+    col_h_ref,
+    col_l_ref,
+    b0_ref,
+    b1_ref,
     moments_ref,
     mid_ref,
     z_ref,
@@ -242,70 +303,36 @@
     rows, wide = s_ref.shape
     cols = wide - LANES
     tall = rows + 2 * HALF
+    row = (row_h_ref[:rows, :tall], row_l_ref[:rows, :tall])
     col = (col_h_ref[...], col_l_ref[...])
-    edge = (edge_h_ref[...], edge_l_ref[...])
-    row_at = lax.axis_index("ty")
-    has_above = jnp.where(row_at > 0, 1.0, 0.0)
-    has_below = jnp.where(row_at < n_ty - 1, 1.0, 0.0)
-
-    def with_halo(part, at, ref):
-        above = above_ref[part, at] * has_above
-        below = below_ref[part, at] * has_below
-        return jnp.concatenate([above, ref[:, at], below], axis=0)
-
-    sums, weights = slice(0, 2 * HALF), slice(2 * HALF, 3 * HALF)
-
-    def block(ref, c, height):
-        lo, hi = (c - 1) * LANES, (c + 3) * LANES
-        if c == 0:
-            x = jnp.concatenate([ref[:height, cols:], ref[:height, :hi]], axis=1)
-        else:
-            x = ref[:height, lo:hi]
-        return smooth3(split2(x), col)
-
-    row = (row_h_ref[...], row_l_ref[...])
     for c in range(0, wide, LANES * 3):
         at = slice(c, c + LANES * 3)
-        mid_ref[:, at] = smooth3(row, split2(with_halo(sums, at, s_ref)))
+        z = with_halo(n_ty, above_ref, w_ref, below_ref, at) * y0_ref[:, at]
+        z_ref[:, at] = z[HALF : HALF + rows]
+        mid_ref[:, at] = smooth3(row, split2(z))
     total_sy = jnp.zeros((rows, 2 * LANES), F32)
     total_zy = jnp.zeros((rows, 2 * LANES), F32)
-    total_ss = jnp.zeros((rows, 2 * LANES), F32)
-    for c in range(0, cols // LANES, 2):
-        at = slice(c * LANES, (c + 2) * LANES)
-        y = block(mid_ref, c, tall)
-        z = with_halo(weights, at, w_ref) * y
-        z_ref[:, at] = z
-        inner = y[HALF : HALF + rows]
-        y0_ref[:, at] = inner
-        s = s_ref[:, at]
-        total_sy += s * inner
-        total_zy += z[HALF : HALF + rows] * inner
-        total_ss += s * s / w_ref[:, at]
-    x = jnp.concatenate([mid_ref[:, cols - LANES :], mid_ref[:, :LANES]], axis=1)
-    y = smooth3(split2(x), edge)
-    z_ref[:, cols:] = with_halo(weights, slice(cols, wide), w_ref) * y
-
-    row = (row_h_ref[:rows, :tall], row_l_ref[:rows, :tall])
-    for c in range(0, wide, LANES * 3):
-        at = slice(c, c + LANES * 3)
-        mid_ref[:rows, at] = smooth3(row, split2(z_ref[:, at]))
     total_zz = jnp.zeros((rows, 2 * LANES), F32)
     for c in range(0, cols // LANES, 2):
         at = slice(c * LANES, (c + 2) * LANES)
-        y = block(mid_ref, c, rows)
-        y1_ref[:, at] = y
-        total_zz += z_ref[HALF : HALF + rows, at] * y
+        y1 = along_columns(mid_ref, c, rows, col)
+        y0 = y0_ref[HALF : HALF + rows, at]
+        z = z_ref[:, at]
+        root = root_ref[:, at]
+        b0_ref[:, at] = root * y0
+        b1_ref[:, at] = root * y1
+        total_sy += s_ref[:, at] * y0
+        total_zy += z * y0
+        total_zz += z * y1
     lane = iota((1, LANES), 1)
     packed = jnp.zeros((1, LANES), F32)
-    for i, total in enumerate((total_ss, total_sy, total_zy, total_zz)):
+    for i, total in enumerate((m0_ref[...], total_sy, total_zy, total_zz)):
         value = jnp.sum(jnp.sum(total, axis=0, keepdims=True), axis=1, keepdims=True)
         packed = jnp.where(lane == i, value, packed)
     moments_ref[...] = jnp.broadcast_to(packed, moments_ref.shape)
 
 
-def final_kernel(
-    moments_ref, s_ref, w_ref, y0_ref, y1_ref, x_hbm, r_hbm, x_ref, r_ref, sem
-):
+def final_kernel(moments_ref, r0_ref, b0_ref, b1_ref, x_hbm, r_hbm, x_ref, r_ref, sem):
     totals = jnp.sum(moments_ref[...], axis=0, keepdims=True)
     lane = iota(totals.shape, 1)
     m0, n1, n2, n3 = (
@@ -323,16 +350,13 @@
     r_b0 = -a - step * (a * mu - 0.5 * a + beta)
     r_b1 = step * a
     sends = []
-    rows, cols = y0_ref.shape
-    step_rows = rows // CHUNKS
+    step_rows = r0_ref.shape[0] // CHUNKS
     for c in range(CHUNKS):
         at = slice(c * step_rows, (c + 1) * step_rows)
-        w = w_ref[at, :cols]
-        root = jnp.sqrt(w)
-        r0 = s_ref[at, :cols] / w
-        y0 = y0_ref[at, :]
-        x_ref[at, :] = root * (x_r0 * r0 + x_b0 * y0)
-        r_ref[at, :] = root * (r_r0 * r0 + r_b0 * y0 + r_b1 * y1_ref[at, :])
+        r0 = r0_ref[at, :]
+        b0 = b0_ref[at, :]
+        x_ref[at, :] = x_r0 * r0 + x_b0 * b0
+        r_ref[at, :] = r_r0 * r0 + r_b0 * b0 + r_b1 * b1_ref[at, :]
         for i, (src, dst) in enumerate(((x_ref, x_hbm), (r_ref, r_hbm))):
             send = pltpu.make_async_copy(src.at[at], dst.at[at], sem.at[c, i])
             send.start()
@@ -373,7 +397,6 @@
     parts = cols // LANES
     length = 2 * SLOTS * parts + 2 * SLOTS
     wide = cols + LANES
-    slab = (3 * HALF, wide)
 
     prior_right = lax.ppermute(prior_weight[:, :LANES], TX, neighbours(TX, -1))
     prior_left = lax.ppermute(prior_weight[:, cols - LANES :], TX, neighbours(TX, 1))
@@ -405,16 +428,19 @@
     got = lax.all_to_all(
         message.reshape(devices, 1, length * LANES), TY_TX, split_axis=0, concat_axis=0, tiled=True
     ).reshape(devices * length, LANES)
-    s, w, up, down = call(
+    s_slab, w_slab = (2 * HALF, wide), (HALF, wide)
+    s, w, s_up, s_down, w_up, w_down = call(
         functools.partial(select_kernel, parts, length),
-        [(rows, wide), (rows, wide), slab, slab],
+        [(rows, wide), (rows, wide), s_slab, s_slab, w_slab, w_slab],
         got,
         prior_weight,
         prior_halo,
         name="select",
     )
-    above = lax.ppermute(down, "ty", neighbours(("ty",), 1))
-    below = lax.ppermute(up, "ty", neighbours(("ty",), -1))
+    n_ty = lax.axis_size("ty")
+    downward, upward = neighbours(("ty",), 1), neighbours(("ty",), -1)
+    s_above, s_below = lax.ppermute(s_down, "ty", downward), lax.ppermute(s_up, "ty", upward)
+    w_above, w_below = lax.ppermute(w_down, "ty", downward), lax.ppermute(w_up, "ty", upward)
 
     tall = rows + 2 * HALF
     row_taps = taps(np.arange(tall)[:, None] - np.arange(rows + 4 * HALF)[None, :] + HALF)
@@ -422,18 +448,36 @@
     ring = np.where(np.arange(LANES) < 64, cols, -LANES) + np.arange(LANES)
     near = np.concatenate([np.arange(cols - LANES, cols), ring, np.arange(LANES)])
     edge_taps = taps(ring[None, :] - near[:, None])
-    y0, y1, moments = call(
-        functools.partial(conv_kernel, lax.axis_size("ty")),
-        [(rows, cols), (rows, cols), (devices, LANES)],
+    tile = (rows, cols)
+    y0, root, r0, m0 = call(
+        functools.partial(first_kernel, n_ty),
+        [(tall, wide), tile, tile, (8, LANES)],
         s,
         w,
-        above,
-        below,
+        s_above,
+        s_below,
         *row_taps,
         *col_taps,
         *edge_taps,
-        scratch=[pltpu.VMEM((tall, wide), F32), pltpu.VMEM((tall, wide), F32)],
-        name="smooth",
+        scratch=[pltpu.VMEM((tall, wide), F32)],
+        flops=3 * 2 * tall * wide * (2 * LANES + 4 * LANES),
+        name="first",
+    )
+    b0, b1, moments = call(
+        functools.partial(second_kernel, n_ty),
+        [tile, tile, (devices, LANES)],
+        s,
+        w,
+        w_above,
+        w_below,
+        y0,
+        root,
+        m0,
+        *row_taps,
+        *col_taps,
+        scratch=[pltpu.VMEM((rows, wide), F32), pltpu.VMEM((rows, wide), F32)],
+        flops=3 * 2 * rows * wide * (2 * LANES + 4 * LANES),
+        name="second",
     )
     moments = lax.all_to_all(
         moments.reshape(devices, 1, LANES), TY_TX, split_axis=0, concat_axis=0, tiled=True
@@ -441,16 +485,15 @@
     return tuple(
         call(
             final_kernel,
-            [(rows, cols), (rows, cols)],
+            [tile, tile],
             moments,
-            s,
-            w,
-            y0,
-            y1,
+            r0,
+            b0,
+            b1,
             outs=[HBM, HBM],
             scratch=[
-                pltpu.VMEM((rows, cols), F32),
-                pltpu.VMEM((rows, cols), F32),
+                pltpu.VMEM(tile, F32),
+                pltpu.VMEM(tile, F32),
                 pltpu.SemaphoreType.DMA((CHUNKS, 2)),
             ],
             name="combine",

time: 82.4 us -> 80.9 us (0.982)
  waiting for transfers between devices: 39.8 us -> 35.5 us
  starting transfers between devices: 16.1 us -> 18.7 us
    ppermute x2 -> x4, waiting for transfers between devices: 8.56 us -> 4.26 us  [the longest x1 2.72 us: shards(): lax.ppermute(s_down, 'ty', downward)]
    ppermute x2 -> x4, starting transfers between devices: 2.74 us -> 5.41 us  [the longest x1 2.67 us: shards(): lax.ppermute(w_up, 'ty', upward)]
    pallas_call x4 -> x5, Pallas kernels: 8.25 us -> 8.4 us  [call(): pl.pallas_call(kernel, out_shape=[jax.ShapeDtypeStruct(s, F32) for s in s...]
  transfers between devices with their start and end apart: 5 -> 7, of which waited for: 3 -> 4; matrix products, arithmetic and copies ran while one was open for 0% -> 0% of each run, Pallas kernels for 0% -> 2%
where the time goes in v4:
time: 80.9 us; the launch traced here: 80.7 us
  waiting for transfers between devices  35.5 us (44%)
  starting transfers between devices  18.7 us (23%)
  blocking collectives  17.3 us (21%)
  Pallas kernels  8.4 us (10%)
    ppermute x1, waiting for transfers between devices, shards(): prior_right = lax.ppermute(prior_weight[:, :LANES], TX, neighbours(TX, -1))  26.1 us
    all_to_all x1, blocking collectives, shards(): lax.all_to_all(moments.reshape(devices, 1, LANES), TY_TX, split_axis=0, c...  17.3 us
    all_to_all x1, starting transfers between devices, shards(): lax.all_to_all(message.reshape(devices, 1, length * LANES), TY_TX, split_...  11.5 us
    pallas_call x5, Pallas kernels, call(): pl.pallas_call(kernel, out_shape=[jax.ShapeDtypeStruct(s, F32) for s in s...  8.4 us
    all_to_all x1, waiting for transfers between devices, shards(): lax.all_to_all(message.reshape(devices, 1, length * LANES), TY_TX, split_...  5.13 us
    ppermute x1, waiting for transfers between devices, shards(): lax.ppermute(s_down, 'ty', downward)  2.72 us
    ppermute x1, starting transfers between devices, shards(): lax.ppermute(w_up, 'ty', upward)  2.67 us
    ppermute x1, starting transfers between devices, shards(): lax.ppermute(s_up, 'ty', upward)  2.66 us
  transfers between devices with their start and end apart: 7, of which 4 were waited for; matrix products, arithmetic and copies ran while one was open for 0% of the time, Pallas kernels for 2%

profile of v4, /device:TPU:1, one launch (start us, length us, event | category | flops | bytes accessed | tf_op | source)
XLA Modules:
  0.0 80.7 jit_solution(10952143490775652516)
XLA Ops:
  0.6 3.6 %pack.1 = f32[4608,128]{1,0:T(8,128)} custom-call(s32[1,128]{1,0:T(1,128)} %bitcast.16, s32[1,128]{1,0:T(1,128)} %bitcast.17, f32[1024,128]{1,0:T(8,128)} %bitcast.14, f32[1024,128]{1,0:T(8,128)} %bitcast.15), custom_call_target="tpu_custom_call" | custom-call | bytes 1049600 | tf_op jit(solution)/shard_map/pack/pallas_call | solution.py:375
  4.2 0.0 copy-start
  4.2 11.5 %all-to-all-start = ((f32[128,1,4608]{2,1,0:T(1,128)}), f32[128,1,4608]{2,1,0:T(1,128)S(1)}, u32[]{:S(2)}, u32[]{:S(2)}) async-start(f32[128,1,4608]{2,1,0:T(1,128)} %bitcast.13), calls=%async_computation | async-start | bytes 4718592 | tf_op jit(solution)/shard_map/all_to_all | solution.py:428
  15.8 0.0 copy-done
  15.8 0.0 copy-start.1
  15.8 0.0 copy-start.2
  15.8 1.1 %collective-permute-start = (f32[128,128]{1,0:T(8,128)S(1)}, f32[128,128]{1,0:T(8,128)S(1)}, u32[]{:S(2)}, u32[]{:S(2)}) collective-permute-start(f32[128,128]{1,0:T(8,128)S(1)} %get-tuple-element.29), channel_id=1, source_target_pairs={{0,31},{1,0},{2,1},{3,2},{4,3},{5,4},{6,5},{7,6},{8,7},{9,8},{10,9... | collective-permute-start | bytes 196616 | tf_op jit(solution)/shard_map/ppermute | solution.py:401
  16.9 0.7 collective-permute-start.1
  17.6 26.1 %collective-permute-done = f32[128,128]{1,0:T(8,128)S(1)} collective-permute-done((f32[128,128]{1,0:T(8,128)S(1)}, f32[128,128]{1,0:T(8,128)S(1)}, u32[]{:S(2)}, u32[]{:S(2)}) %collective-permute-start) | collective-permute-done | bytes 65568 | tf_op jit(solution)/shard_map/ppermute | solution.py:401
  43.7 0.0 collective-permute-done.1
  43.7 5.1 %all-to-all-done = f32[128,1,4608]{2,1,0:T(1,128)S(1)} async-done(((f32[128,1,4608]{2,1,0:T(1,128)}), f32[128,1,4608]{2,1,0:T(1,128)S(1)}, u32[]{:S(2)}, u32[]{:S(2)}) %all-to-all-start) | async-done | bytes 2359328 | tf_op jit(solution)/shard_map/all_to_all | solution.py:428
  48.8 0.0 copy-start.3
  48.9 0.0 copy-start.4
  48.9 0.0 copy-start.5
  48.9 0.0 copy-start.6
  48.9 1.0 %select.1 = (f32[128,1152]{1,0:T(8,128)S(1)}, f32[128,1152]{1,0:T(8,128)S(1)}, f32[64,1152]{1,0:T(8,128)S(1)}, f32[64,1152]{1,0:T(8,128)S(1)}, f32[32,1152]{1,0:T(8,128)S(1)}, /*index=5*/f32[32,1152]{1,0:T(8,128)S(1)}) custom-call(f32[4608,128]{1,0:T(8,128)S(1)} %bitcast.10, f32[128,1024]{1,0:T(8,128)S(1)} %copy-done, ...), custom_call_target="tpu_custom_call" | custom-call | bytes 2949120 | tf_op jit(solution)/shard_map/select/pallas_call | solution.py:375
  49.8 0.1 collective-permute-start.4
  49.9 2.7 %collective-permute-start.5 = (f32[64,1152]{1,0:T(8,128)S(1)}, f32[64,1152]{1,0:T(8,128)S(1)}, u32[]{:S(2)}, u32[]{:S(2)}) collective-permute-start(f32[64,1152]{1,0:T(8,128)S(1)} %get-tuple-element.20), channel_id=1, source_target_pairs={{0,96},{32,0},{64,32},{96,64},{1,97},{33,1},{65,33},{97,65},{2,98}... | collective-permute-start | bytes 884744 | tf_op jit(solution)/shard_map/ppermute | solution.py:442
  52.6 0.0 collective-permute-start.2
  52.6 2.7 %collective-permute-start.3 = (f32[32,1152]{1,0:T(8,128)S(1)}, f32[32,1152]{1,0:T(8,128)S(1)}, u32[]{:S(2)}, u32[]{:S(2)}) collective-permute-start(f32[32,1152]{1,0:T(8,128)S(1)} %get-tuple-element.18), channel_id=1, source_target_pairs={{0,96},{32,0},{64,32},{96,64},{1,97},{33,1},{65,33},{97,65},{2,98}... | collective-permute-start | bytes 442376 | tf_op jit(solution)/shard_map/ppermute | solution.py:443
  55.3 2.7 %collective-permute-done.4.above_ref = f32[64,1152]{1,0:T(8,128)S(1)} collective-permute-done((f32[64,1152]{1,0:T(8,128)S(1)}, f32[64,1152]{1,0:T(8,128)S(1)}, u32[]{:S(2)}, u32[]{:S(2)}) %collective-permute-start.4) | collective-permute-done | bytes 294944 | tf_op jit(solution)/shard_map/ppermute | solution.py:442
  58.0 0.0 collective-permute-done.5.below_ref
  58.0 0.0 copy-done.1
  58.0 0.0 copy-done.2
  58.0 0.0 copy-done.3
  58.0 0.0 copy-done.4
  58.0 0.0 copy-done.5
  58.0 0.0 copy-done.6
  58.0 1.6 %first.1 = (f32[192,1152]{1,0:T(8,128)S(1)}, f32[128,1024]{1,0:T(8,128)S(1)}, f32[128,1024]{1,0:T(8,128)S(1)}, f32[8,128]{1,0:T(8,128)S(1)}) custom-call(f32[128,1152]{1,0:T(8,128)S(1)} %get-tuple-element.15.s_ref, f32[128,1152]{1,0:T(8,128)S(1)} %get-tuple-element.16.w_ref, f32[64,1152]{1,0:T(8,128)S(1)} %collective-permute-done.4.above_ref, ...), custom_call_target="tpu_custom_call" | custom-call | flops 1019215872 | bytes 2686976 | tf_op jit(solution)/shard_map/first/pallas_call | solution.py:375
  59.6 1.5 %collective-permute-done.2.above_ref = f32[32,1152]{1,0:T(8,128)S(1)} collective-permute-done((f32[32,1152]{1,0:T(8,128)S(1)}, f32[32,1152]{1,0:T(8,128)S(1)}, u32[]{:S(2)}, u32[]{:S(2)}) %collective-permute-start.2) | collective-permute-done | bytes 147488 | tf_op jit(solution)/shard_map/ppermute | solution.py:443
  61.1 0.0 collective-permute-done.3.below_ref
  61.1 1.1 %second.1 = (f32[128,1024]{1,0:T(8,128)S(1)}, f32[128,1024]{1,0:T(8,128)S(1)}, f32[128,128]{1,0:T(8,128)S(1)}) custom-call(f32[128,1152]{1,0:T(8,128)S(1)} %get-tuple-element.15.s_ref, f32[128,1152]{1,0:T(8,128)S(1)} %get-tuple-element.16.w_ref, f32[32,1152]{1,0:T(8,128)S(1)} %collective-permute-done.2.above_ref, ...), custom_call_target="tpu_custom_call" | custom-call | flops 679477248 | bytes 3608576 | tf_op jit(solution)/shard_map/second/pallas_call | solution.py:375
  62.3 17.3 %all_to_all.10 = f32[128,1,128]{2,1,0:T(1,128)S(1)} all-to-all(f32[128,1,128]{2,1,0:T(1,128)S(1)} %bitcast.12), channel_id=1, replica_groups=mesh['ty'=4,'tx_0'=4,'tx_1'=4,'tx_2'=2] {'ty','tx_0','tx_1','tx_2'}, dimensions={0} | all-to-all | bytes 131072 | tf_op jit(solution)/shard_map/all_to_all | solution.py:482
  79.5 1.2 %combine.1 = (f32[128,1024]{1,0:T(8,128)}, f32[128,1024]{1,0:T(8,128)}) custom-call(f32[128,128]{1,0:T(8,128)S(1)} %bitcast.11, f32[128,1024]{1,0:T(8,128)S(1)} %get-tuple-element.25.r0_ref, f32[128,1024]{1,0:T(8,128)S(1)} %get-tuple-element.26.b0_ref, f32[128,1024]{1,0:T(8,128)S(1)} %get-tuple-element.27.b1_ref), custom_call_target="tpu_custom_call" | custom-call | bytes 1638400 | tf_op jit(solution)/shard_map/combine/pallas_call | solution.py:375
  (3 shorter events, 0.0 us)
Async XLA Ops:
  4.2 11.5 %copy-start = (f32[128,1024]{1,0:T(8,128)S(1)}, f32[128,1024]{1,0:T(8,128)}, u32[]{:S(2)}) copy-start(f32[128,1024]{1,0:T(8,128)} %prior_ref.1) | copy-start | bytes 1572868
  4.2 44.6 %all-to-all-start = ((f32[128,1,4608]{2,1,0:T(1,128)}), f32[128,1,4608]{2,1,0:T(1,128)S(1)}, u32[]{:S(2)}, u32[]{:S(2)}) async-start(f32[128,1,4608]{2,1,0:T(1,128)} %bitcast.13), calls=%async_computation | async-start | bytes 4718592 | tf_op jit(solution)/shard_map/all_to_all | solution.py:428
  15.8 42.2 %copy-start.1 = (bf16[512,256]{1,0:T(8,128)(2,1)S(1)}, bf16[512,256]{1,0:T(8,128)(2,1)}, u32[]{:S(2)}) copy-start(bf16[512,256]{1,0:T(8,128)(2,1)} %constant.20.clone.col_h_ref) | copy-start | bytes 786436
  15.8 42.2 %copy-start.2 = (bf16[512,256]{1,0:T(8,128)(2,1)S(1)}, bf16[512,256]{1,0:T(8,128)(2,1)}, u32[]{:S(2)}) copy-start(bf16[512,256]{1,0:T(8,128)(2,1)} %constant.21.clone.col_l_ref) | copy-start | bytes 786436
  15.8 27.9 %collective-permute-start = (f32[128,128]{1,0:T(8,128)S(1)}, f32[128,128]{1,0:T(8,128)S(1)}, u32[]{:S(2)}, u32[]{:S(2)}) collective-permute-start(f32[128,128]{1,0:T(8,128)S(1)} %get-tuple-element.29), channel_id=1, source_target_pairs={{0,31},{1,0},{2,1},{3,2},{4,3},{5,4},{6,5},{7,6},{8,7},{9,8},{10,9... | collective-permute-start | bytes 196616 | tf_op jit(solution)/shard_map/ppermute | solution.py:401
  16.9 26.8 %collective-permute-start.1 = (f32[128,128]{1,0:T(8,128)S(1)}, f32[128,128]{1,0:T(8,128)S(1)}, u32[]{:S(2)}, u32[]{:S(2)}) collective-permute-start(f32[128,128]{1,0:T(8,128)S(1)} %get-tuple-element.28), channel_id=1, source_target_pairs={{0,1},{1,2},{2,3},{3,4},{4,5},{5,6},{6,7},{7,8},{8,9},{9,10},{10,1... | collective-permute-start | bytes 196616 | tf_op jit(solution)/shard_map/ppermute | solution.py:402
  48.8 9.1 %copy-start.3 = (bf16[192,256]{1,0:T(8,128)(2,1)S(1)}, bf16[192,256]{1,0:T(8,128)(2,1)}, u32[]{:S(2)}) copy-start(bf16[192,256]{1,0:T(8,128)(2,1)} %constant.18.clone.row_h_ref) | copy-start | bytes 294916
  48.9 9.2 %copy-start.4 = (bf16[192,256]{1,0:T(8,128)(2,1)S(1)}, bf16[192,256]{1,0:T(8,128)(2,1)}, u32[]{:S(2)}) copy-start(bf16[192,256]{1,0:T(8,128)(2,1)} %constant.19.clone.row_l_ref) | copy-start | bytes 294916
  48.9 9.2 %copy-start.5 = (bf16[384,128]{1,0:T(8,128)(2,1)S(1)}, bf16[384,128]{1,0:T(8,128)(2,1)}, u32[]{:S(2)}) copy-start(bf16[384,128]{1,0:T(8,128)(2,1)} %constant.22.clone.edge_h_ref) | copy-start | bytes 294916
  48.9 9.2 %copy-start.6 = (bf16[384,128]{1,0:T(8,128)(2,1)S(1)}, bf16[384,128]{1,0:T(8,128)(2,1)}, u32[]{:S(2)}) copy-start(bf16[384,128]{1,0:T(8,128)(2,1)} %constant.23.clone.edge_l_ref) | copy-start | bytes 294916
  49.8 8.1 %collective-permute-start.4 = (f32[64,1152]{1,0:T(8,128)S(1)}, f32[64,1152]{1,0:T(8,128)S(1)}, u32[]{:S(2)}, u32[]{:S(2)}) collective-permute-start(f32[64,1152]{1,0:T(8,128)S(1)} %get-tuple-element.19), channel_id=1, source_target_pairs={{0,32},{32,64},{64,96},{96,0},{1,33},{33,65},{65,97},{97,1},{2,34}... | collective-permute-start | bytes 884744 | tf_op jit(solution)/shard_map/ppermute | solution.py:442
  49.9 8.1 %collective-permute-start.5 = (f32[64,1152]{1,0:T(8,128)S(1)}, f32[64,1152]{1,0:T(8,128)S(1)}, u32[]{:S(2)}, u32[]{:S(2)}) collective-permute-start(f32[64,1152]{1,0:T(8,128)S(1)} %get-tuple-element.20), channel_id=1, source_target_pairs={{0,96},{32,0},{64,32},{96,64},{1,97},{33,1},{65,33},{97,65},{2,98}... | collective-permute-start | bytes 884744 | tf_op jit(solution)/shard_map/ppermute | solution.py:442
  52.6 8.6 %collective-permute-start.2 = (f32[32,1152]{1,0:T(8,128)S(1)}, f32[32,1152]{1,0:T(8,128)S(1)}, u32[]{:S(2)}, u32[]{:S(2)}) collective-permute-start(f32[32,1152]{1,0:T(8,128)S(1)} %get-tuple-element.17), channel_id=1, source_target_pairs={{0,32},{32,64},{64,96},{96,0},{1,33},{33,65},{65,97},{97,1},{2,34}... | collective-permute-start | bytes 442376 | tf_op jit(solution)/shard_map/ppermute | solution.py:443
  52.6 8.6 %collective-permute-start.3 = (f32[32,1152]{1,0:T(8,128)S(1)}, f32[32,1152]{1,0:T(8,128)S(1)}, u32[]{:S(2)}, u32[]{:S(2)}) collective-permute-start(f32[32,1152]{1,0:T(8,128)S(1)} %get-tuple-element.18), channel_id=1, source_target_pairs={{0,96},{32,0},{64,32},{96,64},{1,97},{33,1},{65,33},{97,65},{2,98}... | collective-permute-start | bytes 442376 | tf_op jit(solution)/shard_map/ppermute | solution.py:443

commit v5 on v4

--- a/solution.py
+++ b/solution.py
@@ -162,15 +162,38 @@
         send.wait()
 
 
-def select_kernel(
-    parts, length, got_ref, prior_ref, prior_halo_ref, s_ref, w_ref, s_up_ref, s_down_ref,
-    w_up_ref, w_down_ref
-):
-    rows, cols = prior_ref.shape
+def slot_rows(got_ref, length, at, devices):
+    return got_ref[pl.ds(at, devices, stride=length), :]
+
+
+def gather_tile(got_ref, parts, length, which, select, dst, extra):
+    devices = got_ref.shape[0] // length
+    for c in range(0, parts, 2):
+        x = jnp.concatenate(
+            [
+                jnp.concatenate(
+                    [
+                        slot_rows(got_ref, length, (which * SLOTS + k) * parts + c + i, devices)
+                        for i in range(2)
+                    ],
+                    axis=1,
+                )
+                for k in range(SLOTS)
+            ],
+            axis=0,
+        )
+        at = slice(c * LANES, (c + 2) * LANES)
+        y = pick(select, x)
+        dst[:, at] = y if extra is None else y + extra[:, at]
+
+
+def sums_kernel(parts, length, got_ref, s_ref, up_ref, down_ref, select_ref, strip_ref):
+    rows, wide = s_ref.shape
+    cols = wide - LANES
     devices = got_ref.shape[0] // length
     base = 2 * SLOTS * parts
-    from_left = [got_ref[pl.ds(base + k, devices, stride=length), :] for k in range(SLOTS)]
-    from_right = [got_ref[pl.ds(base + SLOTS + k, devices, stride=length), :] for k in range(SLOTS)]
+    from_left = [slot_rows(got_ref, length, base + k, devices) for k in range(SLOTS)]
+    from_right = [slot_rows(got_ref, length, base + SLOTS + k, devices) for k in range(SLOTS)]
     left_t = [jnp.transpose(x) for x in from_left]
     right_t = [jnp.transpose(x) for x in from_right]
     wanted = (iota((rows, devices), 0) + 1).astype(F32)
@@ -181,45 +204,37 @@
         ).astype(BF16)
 
     own = chooser(right_t, 97)
-    for which, dst in enumerate((s_ref, w_ref)):
-        for c in range(0, parts, 2):
-            x = jnp.concatenate(
-                [
-                    jnp.concatenate(
-                        [
-                            got_ref[
-                                pl.ds((which * SLOTS + k) * parts + c + i, devices, stride=length), :
-                            ]
-                            for i in range(2)
-                        ],
-                        axis=1,
-                    )
-                    for k in range(SLOTS)
-                ],
-                axis=0,
-            )
-            y = pick(own, x)
-            at = slice(c * LANES, (c + 2) * LANES)
-            if which == 1:
-                y = y + prior_ref[:, at]
-            dst[:, at] = y
+    select_ref[...] = own
+    gather_tile(got_ref, parts, length, 0, own, s_ref, None)
     left = pick(chooser(left_t, 0), jnp.concatenate(from_left, axis=0))
     right = pick(chooser(right_t, 96), jnp.concatenate(from_right, axis=0))
     lane = iota((rows, LANES), 1)
     s_ref[:, cols:] = jnp.where(lane < 64, right, left)
+    strip_ref[...] = jnp.where(lane < 64, pltpu.roll(right, 64, 1), pltpu.roll(left, 64, 1))
+    up_ref[...] = s_ref[: 2 * HALF, :]
+    down_ref[...] = s_ref[rows - 2 * HALF :, :]
+
+
+def weights_kernel(
+    parts, length, n_tx, got_ref, prior_ref, prior_halo_ref, select_ref, strip_ref,
+    w_ref, up_ref, down_ref
+):
+    rows, wide = w_ref.shape
+    cols = wide - LANES
+    gather_tile(got_ref, parts, length, 1, select_ref[...], w_ref, prior_ref)
+    lane = iota((rows, LANES), 1)
     column = lax.axis_index(TX)
     has_left = jnp.where(column > 0, 1.0, 0.0)
-    has_right = jnp.where(column < lax.axis_size(TX) - 1, 1.0, 0.0)
+    has_right = jnp.where(column < n_tx - 1, 1.0, 0.0)
     prior_halo = prior_halo_ref[...]
+    strip = strip_ref[...]
     w_ref[:, cols:] = jnp.where(
-        lane < 32,
-        prior_halo * has_right + pltpu.roll(right, 64, 1),
-        jnp.where(lane >= 96, prior_halo * has_left + pltpu.roll(left, 64, 1), 0.0),
-    )
-    s_up_ref[...] = s_ref[: 2 * HALF, :]
-    s_down_ref[...] = s_ref[rows - 2 * HALF :, :]
-    w_up_ref[...] = w_ref[:HALF, :]
-    w_down_ref[...] = w_ref[rows - HALF :, :]
+        lane < HALF,
+        prior_halo * has_right + strip,
+        jnp.where(lane >= LANES - HALF, prior_halo * has_left + strip, 0.0),
+    )
+    up_ref[...] = w_ref[:HALF, :]
+    down_ref[...] = w_ref[rows - HALF :, :]
 
 
 def with_halo(n_ty, above_ref, ref, below_ref, at):
@@ -281,52 +296,108 @@
     m0_ref[...] = sum(total[:, c : c + LANES] for c in range(0, cols, LANES))
 
 
+def folded(total):
+    rows, cols = total.shape
+    total = sum(total[r : r + 8] for r in range(0, rows, 8))
+    return sum(total[:, c : c + LANES] for c in range(0, cols, LANES))
+
+
 def second_kernel(
-    n_ty,
     s_ref,
     w_ref,
+    y0_ref,
+    root_ref,
+    m0_ref,
+    own_h_ref,
+    own_l_ref,
+    col_h_ref,
+    col_l_ref,
+    b0_ref,
+    inner_ref,
+    z_ref,
+    mid_ref,
+    sums_ref,
+    deep_ref,
+):
+    rows, wide = s_ref.shape
+    cols = wide - LANES
+    tile = slice(HALF, HALF + rows)
+    deep = slice(HALF, rows - HALF)
+    row = (own_h_ref[...], own_l_ref[...])
+    col = (col_h_ref[...], col_l_ref[...])
+    for c in range(0, wide, LANES * 3):
+        at = slice(c, c + LANES * 3)
+        z = w_ref[:, at] * y0_ref[tile, at]
+        z_ref[:, at] = z
+        mid = smooth3(row, split2(z))
+        mid_ref[:, at] = mid
+        deep_ref[:, at] = mid[deep]
+    total_sy = total_zy = total_zz = jnp.zeros((8, LANES), F32)
+    for c in range(0, cols // LANES, 2):
+        at = slice(c * LANES, (c + 2) * LANES)
+        y0 = y0_ref[tile, at]
+        b0_ref[:, at] = root_ref[:, at] * y0
+        total_sy += folded(s_ref[:, at] * y0)
+        total_zy += folded(z_ref[:, at] * y0)
+        y1 = along_columns(deep_ref, c, rows - 2 * HALF, col)
+        inner_ref[:, at] = root_ref[deep, at] * y1
+        total_zz += folded(z_ref[deep, at] * y1)
+    for i, total in enumerate((m0_ref[...], total_sy, total_zy, total_zz)):
+        sums_ref[8 * i : 8 * i + 8, :] = total
+
+
+def third_kernel(
+    n_ty,
     above_ref,
     below_ref,
     y0_ref,
     root_ref,
-    m0_ref,
-    row_h_ref,
-    row_l_ref,
+    z_ref,
+    part_ref,
+    inner_ref,
+    sums_ref,
+    halo_h_ref,
+    halo_l_ref,
     col_h_ref,
     col_l_ref,
-    b0_ref,
     b1_ref,
     moments_ref,
     mid_ref,
-    z_ref,
 ):
-    rows, wide = s_ref.shape
+    rows, wide = z_ref.shape
     cols = wide - LANES
-    tall = rows + 2 * HALF
-    row = (row_h_ref[:rows, :tall], row_l_ref[:rows, :tall])
+    row_at = lax.axis_index("ty")
+    has_above = jnp.where(row_at > 0, 1.0, 0.0)
+    has_below = jnp.where(row_at < n_ty - 1, 1.0, 0.0)
+    row = (halo_h_ref[...], halo_l_ref[...])
     col = (col_h_ref[...], col_l_ref[...])
+    top, bottom = slice(0, HALF), slice(rows - HALF, rows)
+    b1_ref[HALF : rows - HALF, :] = inner_ref[...]
+
+    def border(ref, at):
+        return jnp.concatenate([ref[top, at], ref[bottom, at]], axis=0)
+
     for c in range(0, wide, LANES * 3):
         at = slice(c, c + LANES * 3)
-        z = with_halo(n_ty, above_ref, w_ref, below_ref, at) * y0_ref[:, at]
-        z_ref[:, at] = z[HALF : HALF + rows]
-        mid_ref[:, at] = smooth3(row, split2(z))
-    total_sy = jnp.zeros((rows, 2 * LANES), F32)
-    total_zy = jnp.zeros((rows, 2 * LANES), F32)
-    total_zz = jnp.zeros((rows, 2 * LANES), F32)
+        z = jnp.concatenate(
+            [
+                above_ref[:, at] * has_above * y0_ref[:HALF, at],
+                below_ref[:, at] * has_below * y0_ref[rows + HALF :, at],
+            ],
+            axis=0,
+        )
+        mid_ref[:, at] = border(part_ref, at) + smooth3(row, split2(z))
+    total_zz = sums_ref[24:32, :]
     for c in range(0, cols // LANES, 2):
         at = slice(c * LANES, (c + 2) * LANES)
-        y1 = along_columns(mid_ref, c, rows, col)
-        y0 = y0_ref[HALF : HALF + rows, at]
-        z = z_ref[:, at]
-        root = root_ref[:, at]
-        b0_ref[:, at] = root * y0
-        b1_ref[:, at] = root * y1
-        total_sy += s_ref[:, at] * y0
-        total_zy += z * y0
-        total_zz += z * y1
+        y1 = along_columns(mid_ref, c, 2 * HALF, col)
+        b1 = border(root_ref, at) * y1
+        b1_ref[top, at] = b1[:HALF]
+        b1_ref[bottom, at] = b1[HALF:]
+        total_zz += folded(border(z_ref, at) * y1)
     lane = iota((1, LANES), 1)
     packed = jnp.zeros((1, LANES), F32)
-    for i, total in enumerate((m0_ref[...], total_sy, total_zy, total_zz)):
+    for i, total in enumerate((sums_ref[0:8, :], sums_ref[8:16, :], sums_ref[16:24, :], total_zz)):
         value = jnp.sum(jnp.sum(total, axis=0, keepdims=True), axis=1, keepdims=True)
         packed = jnp.where(lane == i, value, packed)
     moments_ref[...] = jnp.broadcast_to(packed, moments_ref.shape)
@@ -374,7 +445,9 @@
     moved = sum(int(np.prod(x.shape)) * x.dtype.itemsize for x in args)
     return pl.pallas_call(
         kernel,
-        out_shape=[jax.ShapeDtypeStruct(s, F32) for s in shapes],
+        out_shape=[
+            jax.ShapeDtypeStruct(s, F32) if isinstance(s, tuple) else s for s in shapes
+        ],
         in_specs=ins or [VMEM] * len(args),
         out_specs=outs or [VMEM] * len(shapes),
         scratch_shapes=list(scratch),
@@ -429,13 +502,29 @@
         message.reshape(devices, 1, length * LANES), TY_TX, split_axis=0, concat_axis=0, tiled=True
     ).reshape(devices * length, LANES)
     s_slab, w_slab = (2 * HALF, wide), (HALF, wide)
-    s, w, s_up, s_down, w_up, w_down = call(
-        functools.partial(select_kernel, parts, length),
-        [(rows, wide), (rows, wide), s_slab, s_slab, w_slab, w_slab],
+    s, s_up, s_down, chosen, strip = call(
+        functools.partial(sums_kernel, parts, length),
+        [
+            (rows, wide),
+            s_slab,
+            s_slab,
+            jax.ShapeDtypeStruct((rows, SLOTS * devices), BF16),
+            (rows, LANES),
+        ],
+        got,
+        flops=3 * 2 * rows * wide * SLOTS * devices,
+        name="sums",
+    )
+    w, w_up, w_down = call(
+        functools.partial(weights_kernel, parts, length, n_tx),
+        [(rows, wide), w_slab, w_slab],
         got,
         prior_weight,
         prior_halo,
-        name="select",
+        chosen,
+        strip,
+        flops=3 * 2 * rows * wide * SLOTS * devices,
+        name="weights",
     )
     n_ty = lax.axis_size("ty")
     downward, upward = neighbours(("ty",), 1), neighbours(("ty",), -1)
@@ -463,21 +552,41 @@
         flops=3 * 2 * tall * wide * (2 * LANES + 4 * LANES),
         name="first",
     )
-    b0, b1, moments = call(
-        functools.partial(second_kernel, n_ty),
-        [tile, tile, (devices, LANES)],
+    inside = np.arange(rows)
+    own_taps = taps(inside[:, None] - inside[None, :])
+    border = np.concatenate([inside[:HALF], inside[rows - HALF :]])
+    outside = np.concatenate([np.arange(-HALF, 0), np.arange(rows, rows + HALF)])
+    halo_taps = taps(border[:, None] - outside[None, :])
+    b0, inner, z, part, sums = call(
+        second_kernel,
+        [tile, (rows - 2 * HALF, cols), (rows, wide), (rows, wide), (32, LANES)],
         s,
         w,
+        y0,
+        root,
+        m0,
+        *own_taps,
+        *col_taps,
+        scratch=[pltpu.VMEM((rows - 2 * HALF, wide), F32)],
+        flops=3 * 2 * rows * wide * 3 * LANES,
+        name="second",
+    )
+    b1, moments = call(
+        functools.partial(third_kernel, n_ty),
+        [tile, (devices, LANES)],
         w_above,
         w_below,
         y0,
         root,
-        m0,
-        *row_taps,
+        z,
+        part,
+        inner,
+        sums,
+        *halo_taps,
         *col_taps,
-        scratch=[pltpu.VMEM((rows, wide), F32), pltpu.VMEM((rows, wide), F32)],
-        flops=3 * 2 * rows * wide * (2 * LANES + 4 * LANES),
-        name="second",
+        scratch=[pltpu.VMEM((2 * HALF, wide), F32)],
+        flops=3 * 2 * rows * wide * 3 * LANES,
+        name="third",
     )
     moments = lax.all_to_all(
         moments.reshape(devices, 1, LANES), TY_TX, split_axis=0, concat_axis=0, tiled=True

time: 80.9 us -> 80.9 us (level)
  waiting for transfers between devices: 35.5 us -> 34.1 us
  Pallas kernels: 8.4 us -> 9.24 us
    all_to_all x1, waiting for transfers between devices: 5.13 us -> 31.4 us  [shards(): lax.all_to_all(message.reshape(devices, 1, length * LANES), TY_TX, split_...]
    ppermute x1, waiting for transfers between devices: 26.1 us -> 0.01 us  [shards(): prior_right = lax.ppermute(prior_weight[:, :LANES], TX, neighbours(TX, -1))]
    ppermute x1, starting transfers between devices: 1.14 us -> 0.01 us  [shards(): prior_right = lax.ppermute(prior_weight[:, :LANES], TX, neighbours(TX, -1))]
    ppermute x1, starting transfers between devices: 0.68 us -> 1.7 us  [shards(): lax.ppermute(prior_weight[:, cols - LANES:], TX, neighbours(TX, 1))]
    ppermute x1, waiting for transfers between devices: 1.54 us -> 0.57 us  [shards(): lax.ppermute(w_down, 'ty', downward)]
    pallas_call x5 -> x7, Pallas kernels: 8.4 us -> 9.24 us  [call(): pl.pallas_call(kernel, out_shape=[jax.ShapeDtypeStruct(s, F32) if isinsta...]
  transfers between devices with their start and end apart: 7 -> 7, of which waited for: 4 -> 3; matrix products, arithmetic and copies ran while one was open for 0% -> 0% of each run, Pallas kernels for 2% -> 4%
where the time goes in v5:
time: 80.9 us; the launch traced here: 80.7 us
  waiting for transfers between devices  34.1 us (42%)
  starting transfers between devices  18.7 us (23%)
  blocking collectives  17.7 us (22%)
  Pallas kernels  9.24 us (11%)
  between operations  0.84 us (1%)
    all_to_all x1, waiting for transfers between devices, shards(): lax.all_to_all(message.reshape(devices, 1, length * LANES), TY_TX, split_...  31.4 us
    all_to_all x1, blocking collectives, shards(): lax.all_to_all(moments.reshape(devices, 1, LANES), TY_TX, split_axis=0, c...  17.7 us
    all_to_all x1, starting transfers between devices, shards(): lax.all_to_all(message.reshape(devices, 1, length * LANES), TY_TX, split_...  11.5 us
    pallas_call x7, Pallas kernels, call(): pl.pallas_call(kernel, out_shape=[jax.ShapeDtypeStruct(s, F32) if isinsta...  9.24 us
    ppermute x1, starting transfers between devices, shards(): lax.ppermute(s_up, 'ty', upward)  2.66 us
    ppermute x1, starting transfers between devices, shards(): lax.ppermute(w_up, 'ty', upward)  2.66 us
    ppermute x1, waiting for transfers between devices, shards(): lax.ppermute(s_down, 'ty', downward)  2.16 us
    ppermute x1, starting transfers between devices, shards(): lax.ppermute(prior_weight[:, cols - LANES:], TX, neighbours(TX, 1))  1.7 us
  transfers between devices with their start and end apart: 7, of which 3 were waited for; matrix products, arithmetic and copies ran while one was open for 0% of the time, Pallas kernels for 4%

profile of v5, /device:TPU:1, one launch (start us, length us, event | category | flops | bytes accessed | tf_op | source)
XLA Modules:
  0.0 80.7 jit_solution(13671289740651982591)
XLA Ops:
  0.6 3.6 %pack.1 = f32[4608,128]{1,0:T(8,128)} custom-call(s32[1,128]{1,0:T(1,128)} %bitcast.17, s32[1,128]{1,0:T(1,128)} %bitcast.18, f32[1024,128]{1,0:T(8,128)} %bitcast.15, f32[1024,128]{1,0:T(8,128)} %bitcast.16), custom_call_target="tpu_custom_call" | custom-call | bytes 1049600 | tf_op jit(solution)/shard_map/pack/pallas_call | solution.py:446
  4.2 0.0 copy-start.2
  4.2 11.5 %all-to-all-start = ((f32[128,1,4608]{2,1,0:T(1,128)}), f32[128,1,4608]{2,1,0:T(1,128)S(1)}, u32[]{:S(2)}, u32[]{:S(2)}) async-start(f32[128,1,4608]{2,1,0:T(1,128)} %bitcast.14), calls=%async_computation | async-start | bytes 4718592 | tf_op jit(solution)/shard_map/all_to_all | solution.py:501
  15.8 0.0 copy-done.2
  15.8 1.7 %collective-permute-start.1 = (f32[128,128]{1,0:T(8,128)S(1)}, f32[128,128]{1,0:T(8,128)S(1)}, u32[]{:S(2)}, u32[]{:S(2)}) collective-permute-start(f32[128,128]{1,0:T(8,128)S(1)} %get-tuple-element.40), channel_id=1, source_target_pairs={{0,1},{1,2},{2,3},{3,4},{4,5},{5,6},{6,7},{7,8},{8,9},{9,10},{10,1... | collective-permute-start | bytes 196616 | tf_op jit(solution)/shard_map/ppermute | solution.py:475
  17.5 0.0 collective-permute-start
  17.5 31.4 %all-to-all-done = f32[128,1,4608]{2,1,0:T(1,128)S(1)} async-done(((f32[128,1,4608]{2,1,0:T(1,128)}), f32[128,1,4608]{2,1,0:T(1,128)S(1)}, u32[]{:S(2)}, u32[]{:S(2)}) %all-to-all-start) | async-done | bytes 2359328 | tf_op jit(solution)/shard_map/all_to_all | solution.py:501
  48.9 0.0 copy-start
  48.9 0.0 copy-start.1
  48.9 0.0 copy-start.7
  48.9 0.0 copy-start.8
  48.9 0.0 copy-start.9
  48.9 0.0 copy-start.10
  48.9 0.6 sums.1
  49.5 0.1 collective-permute-start.4
  49.6 2.7 %collective-permute-start.5 = (f32[64,1152]{1,0:T(8,128)S(1)}, f32[64,1152]{1,0:T(8,128)S(1)}, u32[]{:S(2)}, u32[]{:S(2)}) collective-permute-start(f32[64,1152]{1,0:T(8,128)S(1)} %get-tuple-element.28), channel_id=1, source_target_pairs={{0,96},{32,0},{64,32},{96,64},{1,97},{33,1},{65,33},{97,65},{2,98}... | collective-permute-start | bytes 884744 | tf_op jit(solution)/shard_map/ppermute | solution.py:531
  52.3 0.0 collective-permute-done.1
  52.3 0.0 collective-permute-done
  52.3 0.4 weights.1
  52.7 0.0 copy-start.3
  52.8 0.0 copy-start.4
  52.8 0.1 collective-permute-start.2
  52.8 2.7 %collective-permute-start.3 = (f32[32,1152]{1,0:T(8,128)S(1)}, f32[32,1152]{1,0:T(8,128)S(1)}, u32[]{:S(2)}, u32[]{:S(2)}) collective-permute-start(f32[32,1152]{1,0:T(8,128)S(1)} %get-tuple-element.24), channel_id=1, source_target_pairs={{0,96},{32,0},{64,32},{96,64},{1,97},{33,1},{65,33},{97,65},{2,98}... | collective-permute-start | bytes 442376 | tf_op jit(solution)/shard_map/ppermute | solution.py:532
  55.5 2.2 %collective-permute-done.4.above_ref = f32[64,1152]{1,0:T(8,128)S(1)} collective-permute-done((f32[64,1152]{1,0:T(8,128)S(1)}, f32[64,1152]{1,0:T(8,128)S(1)}, u32[]{:S(2)}, u32[]{:S(2)}) %collective-permute-start.4) | collective-permute-done | bytes 294944 | tf_op jit(solution)/shard_map/ppermute | solution.py:531
  57.7 0.0 collective-permute-done.5.below_ref
  57.7 0.0 copy-done
  57.7 0.0 copy-done.1
  57.7 0.0 copy-done.7
  57.7 0.0 copy-done.8
  57.7 0.0 copy-done.9
  57.7 0.0 copy-done.10
  57.7 1.6 %first.1 = (f32[192,1152]{1,0:T(8,128)S(1)}, f32[128,1024]{1,0:T(8,128)S(1)}, f32[128,1024]{1,0:T(8,128)S(1)}, f32[8,128]{1,0:T(8,128)S(1)}) custom-call(f32[128,1152]{1,0:T(8,128)S(1)} %get-tuple-element.25.s_ref, f32[128,1152]{1,0:T(8,128)S(1)} %get-tuple-element.26.w_ref, f32[64,1152]{1,0:T(8,128)S(1)} %collective-permute-done.4.above_ref, ...), custom_call_target="tpu_custom_call" | custom-call | flops 1019215872 | bytes 2686976 | tf_op jit(solution)/shard_map/first/pallas_call | solution.py:446
  59.3 0.0 copy-start.5
  59.3 0.0 copy-start.6
  59.3 0.0 copy-done.3
  59.3 0.0 copy-done.4
  59.3 0.9 %second.1 = (f32[128,1024]{1,0:T(8,128)S(1)}, f32[64,1024]{1,0:T(8,128)S(1)}, f32[128,1152]{1,0:T(8,128)S(1)}, f32[128,1152]{1,0:T(8,128)S(1)}, f32[32,128]{1,0:T(8,128)S(1)}) custom-call(f32[128,1152]{1,0:T(8,128)S(1)} %get-tuple-element.25.s_ref, f32[128,1152]{1,0:T(8,128)S(1)} %get-tuple-element.26.w_ref, f32[192,1152]{1,0:T(8,128)S(1)} %get-tuple-element.29.y0_ref, ...), custom_call_target="tpu_custom_call" | custom-call | flops 339738624 | bytes 3182592 | tf_op jit(solution)/shard_map/second/pallas_call | solution.py:446
  60.3 0.6 collective-permute-done.2.above_ref
  60.8 0.0 collective-permute-done.3.below_ref
  60.8 0.0 copy-done.5
  60.8 0.0 copy-done.6
  60.8 0.9 %third.1 = (f32[128,1024]{1,0:T(8,128)S(1)}, f32[128,128]{1,0:T(8,128)S(1)}) custom-call(f32[32,1152]{1,0:T(8,128)S(1)} %collective-permute-done.2.above_ref, f32[32,1152]{1,0:T(8,128)S(1)} %collective-permute-done.3.below_ref, f32[192,1152]{1,0:T(8,128)S(1)} %get-tuple-element.29.y0_ref, f32[128,1024]{1,0:T(8,128)S(1)} %get-tuple-element.30.root_ref, ...), custom_call_target="tpu_custom_call" | custom-call | flops 339738624 | bytes 3702784 | tf_op jit(solution)/shard_map/third/pallas_call | solution.py:446
  61.8 17.7 %all_to_all.10 = f32[128,1,128]{2,1,0:T(1,128)S(1)} all-to-all(f32[128,1,128]{2,1,0:T(1,128)S(1)} %bitcast.13), channel_id=1, replica_groups=mesh['ty'=4,'tx_0'=4,'tx_1'=4,'tx_2'=2] {'ty','tx_0','tx_1','tx_2'}, dimensions={0} | all-to-all | bytes 131072 | tf_op jit(solution)/shard_map/all_to_all | solution.py:591
  79.5 1.2 %combine.1 = (f32[128,1024]{1,0:T(8,128)}, f32[128,1024]{1,0:T(8,128)}) custom-call(f32[128,128]{1,0:T(8,128)S(1)} %bitcast.12, f32[128,1024]{1,0:T(8,128)S(1)} %get-tuple-element.37.r0_ref, f32[128,1024]{1,0:T(8,128)S(1)} %get-tuple-element.38.b0_ref, f32[128,1024]{1,0:T(8,128)S(1)} %get-tuple-element.39.b1_ref), custom_call_target="tpu_custom_call" | custom-call | bytes 1638400 | tf_op jit(solution)/shard_map/combine/pallas_call | solution.py:446
  (3 shorter events, 0.0 us)
Async XLA Ops:
  4.2 11.5 %copy-start.2 = (f32[128,1024]{1,0:T(8,128)S(1)}, f32[128,1024]{1,0:T(8,128)}, u32[]{:S(2)}) copy-start(f32[128,1024]{1,0:T(8,128)} %prior_ref.1) | copy-start | bytes 1572868
  4.2 44.6 %all-to-all-start = ((f32[128,1,4608]{2,1,0:T(1,128)}), f32[128,1,4608]{2,1,0:T(1,128)S(1)}, u32[]{:S(2)}, u32[]{:S(2)}) async-start(f32[128,1,4608]{2,1,0:T(1,128)} %bitcast.14), calls=%async_computation | async-start | bytes 4718592 | tf_op jit(solution)/shard_map/all_to_all | solution.py:501
  15.8 36.5 %collective-permute-start.1 = (f32[128,128]{1,0:T(8,128)S(1)}, f32[128,128]{1,0:T(8,128)S(1)}, u32[]{:S(2)}, u32[]{:S(2)}) collective-permute-start(f32[128,128]{1,0:T(8,128)S(1)} %get-tuple-element.40), channel_id=1, source_target_pairs={{0,1},{1,2},{2,3},{3,4},{4,5},{5,6},{6,7},{7,8},{8,9},{9,10},{10,1... | collective-permute-start | bytes 196616 | tf_op jit(solution)/shard_map/ppermute | solution.py:475
  17.5 34.8 %collective-permute-start = (f32[128,128]{1,0:T(8,128)S(1)}, f32[128,128]{1,0:T(8,128)S(1)}, u32[]{:S(2)}, u32[]{:S(2)}) collective-permute-start(f32[128,128]{1,0:T(8,128)S(1)} %get-tuple-element.41), channel_id=1, source_target_pairs={{0,31},{1,0},{2,1},{3,2},{4,3},{5,4},{6,5},{7,6},{8,7},{9,8},{10,9... | collective-permute-start | bytes 196616 | tf_op jit(solution)/shard_map/ppermute | solution.py:474
  48.9 8.8 %copy-start = (bf16[512,256]{1,0:T(8,128)(2,1)S(1)}, bf16[512,256]{1,0:T(8,128)(2,1)}, u32[]{:S(2)}) copy-start(bf16[512,256]{1,0:T(8,128)(2,1)} %constant.29.clone.col_l_ref) | copy-start | bytes 786436
  48.9 8.8 %copy-start.1 = (bf16[512,256]{1,0:T(8,128)(2,1)S(1)}, bf16[512,256]{1,0:T(8,128)(2,1)}, u32[]{:S(2)}) copy-start(bf16[512,256]{1,0:T(8,128)(2,1)} %constant.28.clone.col_h_ref) | copy-start | bytes 786436
  48.9 8.8 %copy-start.7 = (bf16[384,128]{1,0:T(8,128)(2,1)S(1)}, bf16[384,128]{1,0:T(8,128)(2,1)}, u32[]{:S(2)}) copy-start(bf16[384,128]{1,0:T(8,128)(2,1)} %constant.31.clone.edge_l_ref) | copy-start | bytes 294916
  48.9 8.8 %copy-start.8 = (bf16[384,128]{1,0:T(8,128)(2,1)S(1)}, bf16[384,128]{1,0:T(8,128)(2,1)}, u32[]{:S(2)}) copy-start(bf16[384,128]{1,0:T(8,128)(2,1)} %constant.30.clone.edge_h_ref) | copy-start | bytes 294916
  48.9 8.8 %copy-start.9 = (bf16[192,256]{1,0:T(8,128)(2,1)S(1)}, bf16[192,256]{1,0:T(8,128)(2,1)}, u32[]{:S(2)}) copy-start(bf16[192,256]{1,0:T(8,128)(2,1)} %constant.27.clone.row_l_ref) | copy-start | bytes 294916
  48.9 8.8 %copy-start.10 = (bf16[192,256]{1,0:T(8,128)(2,1)S(1)}, bf16[192,256]{1,0:T(8,128)(2,1)}, u32[]{:S(2)}) copy-start(bf16[192,256]{1,0:T(8,128)(2,1)} %constant.26.clone.row_h_ref) | copy-start | bytes 294916
  49.5 8.1 %collective-permute-start.4 = (f32[64,1152]{1,0:T(8,128)S(1)}, f32[64,1152]{1,0:T(8,128)S(1)}, u32[]{:S(2)}, u32[]{:S(2)}) collective-permute-start(f32[64,1152]{1,0:T(8,128)S(1)} %get-tuple-element.27), channel_id=1, source_target_pairs={{0,32},{32,64},{64,96},{96,0},{1,33},{33,65},{65,97},{97,1},{2,34}... | collective-permute-start | bytes 884744 | tf_op jit(solution)/shard_map/ppermute | solution.py:531
  49.6 8.1 %collective-permute-start.5 = (f32[64,1152]{1,0:T(8,128)S(1)}, f32[64,1152]{1,0:T(8,128)S(1)}, u32[]{:S(2)}, u32[]{:S(2)}) collective-permute-start(f32[64,1152]{1,0:T(8,128)S(1)} %get-tuple-element.28), channel_id=1, source_target_pairs={{0,96},{32,0},{64,32},{96,64},{1,97},{33,1},{65,33},{97,65},{2,98}... | collective-permute-start | bytes 884744 | tf_op jit(solution)/shard_map/ppermute | solution.py:531
  52.7 6.6 %copy-start.3 = (bf16[128,128]{1,0:T(8,128)(2,1)S(1)}, bf16[128,128]{1,0:T(8,128)(2,1)}, u32[]{:S(2)}) copy-start(bf16[128,128]{1,0:T(8,128)(2,1)} %constant.33.clone.own_l_ref) | copy-start | bytes 98308
  52.8 6.6 %copy-start.4 = (bf16[128,128]{1,0:T(8,128)(2,1)S(1)}, bf16[128,128]{1,0:T(8,128)(2,1)}, u32[]{:S(2)}) copy-start(bf16[128,128]{1,0:T(8,128)(2,1)} %constant.32.clone.own_h_ref) | copy-start | bytes 98308
  52.8 8.1 %collective-permute-start.2 = (f32[32,1152]{1,0:T(8,128)S(1)}, f32[32,1152]{1,0:T(8,128)S(1)}, u32[]{:S(2)}, u32[]{:S(2)}) collective-permute-start(f32[32,1152]{1,0:T(8,128)S(1)} %get-tuple-element.23), channel_id=1, source_target_pairs={{0,32},{32,64},{64,96},{96,0},{1,33},{33,65},{65,97},{97,1},{2,34}... | collective-permute-start | bytes 442376 | tf_op jit(solution)/shard_map/ppermute | solution.py:532
  52.8 8.0 %collective-permute-start.3 = (f32[32,1152]{1,0:T(8,128)S(1)}, f32[32,1152]{1,0:T(8,128)S(1)}, u32[]{:S(2)}, u32[]{:S(2)}) collective-permute-start(f32[32,1152]{1,0:T(8,128)S(1)} %get-tuple-element.24), channel_id=1, source_target_pairs={{0,96},{32,0},{64,32},{96,64},{1,97},{33,1},{65,33},{97,65},{2,98}... | collective-permute-start | bytes 442376 | tf_op jit(solution)/shard_map/ppermute | solution.py:532
  59.3 1.5 %copy-start.5 = (bf16[64,64]{1,0:T(8,128)(2,1)S(1)}, bf16[64,64]{1,0:T(8,128)(2,1)}, u32[]{:S(2)}) copy-start(bf16[64,64]{1,0:T(8,128)(2,1)} %constant.35.clone.halo_l_ref) | copy-start | bytes 24580
  59.3 1.5 %copy-start.6 = (bf16[64,64]{1,0:T(8,128)(2,1)S(1)}, bf16[64,64]{1,0:T(8,128)(2,1)}, u32[]{:S(2)}) copy-start(bf16[64,64]{1,0:T(8,128)(2,1)} %constant.34.clone.halo_h_ref) | copy-start | bytes 24580

commit v6 on v5

--- a/solution.py
+++ b/solution.py
@@ -20,7 +20,7 @@
 BF16 = jnp.bfloat16
 
 
-def taps(offset):
+def taps(offset, axis):
     def raw(d):
         scaled = np.abs(d) / (HALF + 1.0)
         return np.where(np.abs(d) <= HALF, (1.0 - scaled) ** 4 * (1.0 + 4.0 * scaled), 0.0)
@@ -28,12 +28,7 @@
     values = raw(offset) / raw(np.arange(-HALF, HALF + 1)).sum()
     head = values.astype(BF16)
     tail = (values - head.astype(np.float64)).astype(BF16)
-    return jnp.asarray(head), jnp.asarray(tail)
-
-
-def split2(x):
-    head = x.astype(BF16)
-    return head, (x - head.astype(F32)).astype(BF16)
+    return jnp.asarray(np.concatenate([head, tail], axis=axis))
 
 
 def split3(x):
@@ -52,9 +47,25 @@
     return mm(select, tail) + mm(select, mid) + mm(select, head)
 
 
-def smooth3(left, right):
-    (lh, ll), (rh, rl) = left, right
-    return mm(ll, rh) + mm(lh, rl) + mm(lh, rh)
+def taps_times(taps_ref, x):
+    rows = taps_ref.shape[0] // 2
+    xh, xm, xl = split3(x)
+    low = mm(taps_ref[:rows, :], xl)
+    mid = mm(taps_ref[...], xm)
+    high = mm(taps_ref[...], xh)
+    return low + mid[rows:] + high[rows:] + mid[:rows] + high[:rows]
+
+
+def times_taps(pieces, taps_ref):
+    xh, xm, xl = pieces
+    depth = taps_ref.shape[0] // 2
+    head, tail = taps_ref[:depth, :], taps_ref[depth:, :]
+    return mm(xl, head) + mm(xm, tail) + mm(xh, tail) + mm(xm, head) + mm(xh, head)
+
+
+def spans(wide):
+    cols = wide - LANES
+    return [slice(c, c + 2 * LANES) for c in range(0, cols, 2 * LANES)] + [slice(cols, wide)]
 
 
 def iota(shape, dim):
@@ -244,14 +255,23 @@
     return jnp.concatenate([above, ref[:, at], below], axis=0)
 
 
-def along_columns(mid_ref, c, height, col):
-    cols = mid_ref.shape[1] - LANES
-    lo, hi = (c - 1) * LANES, (c + 3) * LANES
-    if c == 0:
-        x = jnp.concatenate([mid_ref[:height, cols:], mid_ref[:height, :hi]], axis=1)
-    else:
-        x = mid_ref[:height, lo:hi]
-    return smooth3(split2(x), col)
+def along_columns(pieces, taps_ref):
+    height, wide = pieces[0].shape
+    cols = wide - LANES
+
+    def stacked(x):
+        first = jnp.concatenate([x[:, cols:], x[:, : 3 * LANES]], axis=1)
+        rest = [
+            x[:, (c - 1) * LANES : (c + 3) * LANES] for c in range(2, cols // LANES, 2)
+        ]
+        return jnp.concatenate([first] + rest, axis=0)
+
+    half = [stacked(x) for x in pieces]
+    out = []
+    for r in range(0, half[0].shape[0], 2 * height):
+        y = times_taps([x[r : r + 2 * height] for x in half], taps_ref)
+        out += [y[:height], y[height:]]
+    return out
 
 
 def first_kernel(
@@ -260,40 +280,38 @@
     w_ref,
     above_ref,
     below_ref,
-    row_h_ref,
-    row_l_ref,
-    col_h_ref,
-    col_l_ref,
-    edge_h_ref,
-    edge_l_ref,
+    row_ref,
+    col_ref,
+    edge_ref,
     y0_ref,
     root_ref,
     r0_ref,
-    m0_ref,
+    sums_ref,
     mid_ref,
 ):
     rows, wide = s_ref.shape
     cols = wide - LANES
-    tall = rows + 2 * HALF
-    row = (row_h_ref[...], row_l_ref[...])
-    col = (col_h_ref[...], col_l_ref[...])
-    for c in range(0, wide, LANES * 3):
-        at = slice(c, c + LANES * 3)
-        mid_ref[:, at] = smooth3(row, split2(with_halo(n_ty, above_ref, s_ref, below_ref, at)))
-    for c in range(0, cols // LANES, 2):
-        at = slice(c * LANES, (c + 2) * LANES)
-        y0_ref[:, at] = along_columns(mid_ref, c, tall, col)
-    x = jnp.concatenate([mid_ref[:, cols - LANES :], mid_ref[:, :LANES]], axis=1)
-    y0_ref[:, cols:] = smooth3(split2(x), (edge_h_ref[...], edge_l_ref[...]))
-    total = jnp.zeros((8, cols), F32)
+    for at in spans(wide):
+        mid_ref[:, at] = taps_times(row_ref, with_halo(n_ty, above_ref, s_ref, below_ref, at))
+    pieces = split3(mid_ref[...])
+    for c, y in enumerate(along_columns(pieces, col_ref)):
+        y0_ref[:, 2 * c * LANES : 2 * (c + 1) * LANES] = y
+    near = [jnp.concatenate([x[:, cols - LANES :], x[:, :LANES]], axis=1) for x in pieces]
+    y0_ref[:, cols:] = times_taps(near, edge_ref)
+    total_rr = total_rb = jnp.zeros((8, cols), F32)
     for r in range(0, rows, 8):
         at = slice(r, r + 8)
         root = jnp.sqrt(w_ref[at, :cols])
-        r0 = s_ref[at, :cols] / root
+        s = s_ref[at, :cols]
+        r0 = s / root
         root_ref[at, :] = root
         r0_ref[at, :] = r0
-        total += r0 * r0
-    m0_ref[...] = sum(total[:, c : c + LANES] for c in range(0, cols, LANES))
+        total_rr += r0 * r0
+        total_rb += s * y0_ref[HALF + r : HALF + r + 8, :cols]
+    for i, total in enumerate((total_rr, total_rb)):
+        sums_ref[8 * i : 8 * i + 8, :] = sum(
+            total[:, c : c + LANES] for c in range(0, cols, LANES)
+        )
 
 
 def folded(total):
@@ -302,48 +320,57 @@
     return sum(total[:, c : c + LANES] for c in range(0, cols, LANES))
 
 
+def whole(total):
+    return jnp.sum(jnp.sum(total, axis=0, keepdims=True), axis=1, keepdims=True)
+
+
+def centred(r0, b0, b1, c):
+    v, q = b0 - c * r0, b1 - c * b0
+    return v * q, v * b0 + r0 * q
+
+
 def second_kernel(
-    s_ref,
     w_ref,
     y0_ref,
     root_ref,
-    m0_ref,
-    own_h_ref,
-    own_l_ref,
-    col_h_ref,
-    col_l_ref,
+    r0_ref,
+    first_ref,
+    own_ref,
+    col_ref,
     b0_ref,
     inner_ref,
-    z_ref,
     mid_ref,
     sums_ref,
-    deep_ref,
 ):
-    rows, wide = s_ref.shape
+    rows, wide = w_ref.shape
     cols = wide - LANES
     tile = slice(HALF, HALF + rows)
     deep = slice(HALF, rows - HALF)
-    row = (own_h_ref[...], own_l_ref[...])
-    col = (col_h_ref[...], col_l_ref[...])
-    for c in range(0, wide, LANES * 3):
-        at = slice(c, c + LANES * 3)
-        z = w_ref[:, at] * y0_ref[tile, at]
-        z_ref[:, at] = z
-        mid = smooth3(row, split2(z))
-        mid_ref[:, at] = mid
-        deep_ref[:, at] = mid[deep]
-    total_sy = total_zy = total_zz = jnp.zeros((8, LANES), F32)
-    for c in range(0, cols // LANES, 2):
-        at = slice(c * LANES, (c + 2) * LANES)
-        y0 = y0_ref[tile, at]
-        b0_ref[:, at] = root_ref[:, at] * y0
-        total_sy += folded(s_ref[:, at] * y0)
-        total_zy += folded(z_ref[:, at] * y0)
-        y1 = along_columns(deep_ref, c, rows - 2 * HALF, col)
-        inner_ref[:, at] = root_ref[deep, at] * y1
-        total_zz += folded(z_ref[deep, at] * y1)
-    for i, total in enumerate((m0_ref[...], total_sy, total_zy, total_zz)):
-        sums_ref[8 * i : 8 * i + 8, :] = total
+    m0, n1 = whole(first_ref[0:8, :]), whole(first_ref[8:16, :])
+    c0 = n1 / jnp.where(m0 > 0.0, m0, 1.0)
+    for at in spans(wide):
+        mid_ref[:, at] = taps_times(own_ref, w_ref[:, at] * y0_ref[tile, at])
+    total_vv = total_rv = total_vq = total_mix = jnp.zeros((8, LANES), F32)
+    for c, y1 in enumerate(along_columns(split3(mid_ref[deep, :]), col_ref)):
+        at = slice(2 * c * LANES, 2 * (c + 1) * LANES)
+        r0 = r0_ref[:, at]
+        b0 = root_ref[:, at] * y0_ref[tile, at]
+        b0_ref[:, at] = b0
+        v = b0 - c0 * r0
+        total_vv += folded(v * v)
+        total_rv += folded(r0 * v)
+        b1 = root_ref[deep, at] * y1
+        inner_ref[:, at] = b1
+        vq, mix = centred(r0[deep], b0[deep], b1, c0)
+        total_vq += folded(vq)
+        total_mix += folded(mix)
+    lane = iota((8, LANES), 1)
+    known = jnp.zeros((8, LANES), F32)
+    for i, value in enumerate((m0, n1, c0, whole(total_vv), whole(total_rv))):
+        known = jnp.where(lane == i, value, known)
+    sums_ref[0:8, :] = known
+    sums_ref[8:16, :] = total_vq
+    sums_ref[16:24, :] = total_mix
 
 
 def third_kernel(
@@ -352,33 +379,32 @@
     below_ref,
     y0_ref,
     root_ref,
-    z_ref,
+    r0_ref,
+    b0_ref,
     part_ref,
     inner_ref,
     sums_ref,
-    halo_h_ref,
-    halo_l_ref,
-    col_h_ref,
-    col_l_ref,
+    halo_ref,
+    col_ref,
     b1_ref,
     moments_ref,
     mid_ref,
 ):
-    rows, wide = z_ref.shape
+    rows, wide = part_ref.shape
     cols = wide - LANES
     row_at = lax.axis_index("ty")
     has_above = jnp.where(row_at > 0, 1.0, 0.0)
     has_below = jnp.where(row_at < n_ty - 1, 1.0, 0.0)
-    row = (halo_h_ref[...], halo_l_ref[...])
-    col = (col_h_ref[...], col_l_ref[...])
     top, bottom = slice(0, HALF), slice(rows - HALF, rows)
     b1_ref[HALF : rows - HALF, :] = inner_ref[...]
+    known = sums_ref[0:1, :]
+    lane = iota(known.shape, 1)
+    c0 = jnp.sum(jnp.where(lane == 2, known, 0.0), axis=1, keepdims=True)
 
     def border(ref, at):
         return jnp.concatenate([ref[top, at], ref[bottom, at]], axis=0)
 
-    for c in range(0, wide, LANES * 3):
-        at = slice(c, c + LANES * 3)
+    for at in spans(wide):
         z = jnp.concatenate(
             [
                 above_ref[:, at] * has_above * y0_ref[:HALF, at],
@@ -386,35 +412,37 @@
             ],
             axis=0,
         )
-        mid_ref[:, at] = border(part_ref, at) + smooth3(row, split2(z))
-    total_zz = sums_ref[24:32, :]
-    for c in range(0, cols // LANES, 2):
-        at = slice(c * LANES, (c + 2) * LANES)
-        y1 = along_columns(mid_ref, c, 2 * HALF, col)
+        mid_ref[:, at] = border(part_ref, at) + taps_times(halo_ref, z)
+    total_vq, total_mix = sums_ref[8:16, :], sums_ref[16:24, :]
+    for c, y1 in enumerate(along_columns(split3(mid_ref[...]), col_ref)):
+        at = slice(2 * c * LANES, 2 * (c + 1) * LANES)
         b1 = border(root_ref, at) * y1
         b1_ref[top, at] = b1[:HALF]
         b1_ref[bottom, at] = b1[HALF:]
-        total_zz += folded(border(z_ref, at) * y1)
-    lane = iota((1, LANES), 1)
-    packed = jnp.zeros((1, LANES), F32)
-    for i, total in enumerate((sums_ref[0:8, :], sums_ref[8:16, :], sums_ref[16:24, :], total_zz)):
-        value = jnp.sum(jnp.sum(total, axis=0, keepdims=True), axis=1, keepdims=True)
-        packed = jnp.where(lane == i, value, packed)
-    moments_ref[...] = jnp.broadcast_to(packed, moments_ref.shape)
+        vq, mix = centred(border(r0_ref, at), border(b0_ref, at), b1, c0)
+        total_vq += folded(vq)
+        total_mix += folded(mix)
+    known = jnp.where(lane == 5, whole(total_vq), known)
+    known = jnp.where(lane == 6, whole(total_mix), known)
+    moments_ref[...] = jnp.broadcast_to(known, moments_ref.shape)
 
 
 def final_kernel(moments_ref, r0_ref, b0_ref, b1_ref, x_hbm, r_hbm, x_ref, r_ref, sem):
-    totals = jnp.sum(moments_ref[...], axis=0, keepdims=True)
-    lane = iota(totals.shape, 1)
-    m0, n1, n2, n3 = (
-        jnp.sum(jnp.where(lane == i, totals, 0.0), axis=1, keepdims=True) for i in range(4)
-    )
+    parts = jnp.transpose(moments_ref[...])
+    m0_at, n1_at, c_at, vv_at, rv_at, vq_at, mix_at = (parts[i : i + 1, :] for i in range(7))
+
+    def total(x):
+        return jnp.sum(x, axis=1, keepdims=True)
+
+    m0, n1 = total(m0_at), total(n1_at)
     mu = n1 / m0
+    shift = c_at - mu
+    vv = total(vv_at + shift * (2.0 * rv_at + shift * m0_at))
+    vbv = total(vq_at + shift * (mix_at + shift * n1_at))
     a = m0 / (0.5 * m0 + n1)
-    vv = n2 - mu * n1
-    vbv = n3 - 2.0 * mu * n2 + mu * mu * n1
-    beta = a * a * vv / m0
-    step = vv / (0.5 * vv + vbv - a * vv * vv / m0)
+    ratio = vv / m0
+    beta = a * a * ratio
+    step = vv / (0.5 * vv + vbv - a * vv * ratio)
     x_r0 = a + step * beta + step * a * mu
     x_b0 = -step * a
     r_r0 = a * mu - step * (0.5 * a * mu + 0.5 * beta)
@@ -532,43 +560,42 @@
     w_above, w_below = lax.ppermute(w_down, "ty", downward), lax.ppermute(w_up, "ty", upward)
 
     tall = rows + 2 * HALF
-    row_taps = taps(np.arange(tall)[:, None] - np.arange(rows + 4 * HALF)[None, :] + HALF)
-    col_taps = taps(np.arange(2 * LANES)[None, :] - np.arange(4 * LANES)[:, None] + LANES)
+    row_taps = taps(np.arange(tall)[:, None] - np.arange(rows + 4 * HALF)[None, :] + HALF, 0)
+    col_taps = taps(np.arange(2 * LANES)[None, :] - np.arange(4 * LANES)[:, None] + LANES, 0)
     ring = np.where(np.arange(LANES) < 64, cols, -LANES) + np.arange(LANES)
     near = np.concatenate([np.arange(cols - LANES, cols), ring, np.arange(LANES)])
-    edge_taps = taps(ring[None, :] - near[:, None])
+    edge_taps = taps(ring[None, :] - near[:, None], 0)
     tile = (rows, cols)
-    y0, root, r0, m0 = call(
+    y0, root, r0, early = call(
         functools.partial(first_kernel, n_ty),
-        [(tall, wide), tile, tile, (8, LANES)],
+        [(tall, wide), tile, tile, (16, LANES)],
         s,
         w,
         s_above,
         s_below,
-        *row_taps,
-        *col_taps,
-        *edge_taps,
+        row_taps,
+        col_taps,
+        edge_taps,
         scratch=[pltpu.VMEM((tall, wide), F32)],
-        flops=3 * 2 * tall * wide * (2 * LANES + 4 * LANES),
+        flops=5 * 2 * tall * wide * (2 * LANES + 4 * LANES),
         name="first",
     )
     inside = np.arange(rows)
-    own_taps = taps(inside[:, None] - inside[None, :])
+    own_taps = taps(inside[:, None] - inside[None, :], 0)
     border = np.concatenate([inside[:HALF], inside[rows - HALF :]])
     outside = np.concatenate([np.arange(-HALF, 0), np.arange(rows, rows + HALF)])
-    halo_taps = taps(border[:, None] - outside[None, :])
-    b0, inner, z, part, sums = call(
+    halo_taps = taps(border[:, None] - outside[None, :], 0)
+    b0, inner, part, sums = call(
         second_kernel,
-        [tile, (rows - 2 * HALF, cols), (rows, wide), (rows, wide), (32, LANES)],
-        s,
+        [tile, (rows - 2 * HALF, cols), (rows, wide), (24, LANES)],
         w,
         y0,
         root,
-        m0,
-        *own_taps,
-        *col_taps,
-        scratch=[pltpu.VMEM((rows - 2 * HALF, wide), F32)],
-        flops=3 * 2 * rows * wide * 3 * LANES,
+        r0,
+        early,
+        own_taps,
+        col_taps,
+        flops=5 * 2 * rows * wide * 3 * LANES,
         name="second",
     )
     b1, moments = call(
@@ -578,14 +605,15 @@
         w_below,
         y0,
         root,
-        z,
+        r0,
+        b0,
         part,
         inner,
         sums,
-        *halo_taps,
-        *col_taps,
+        halo_taps,
+        col_taps,
         scratch=[pltpu.VMEM((2 * HALF, wide), F32)],
-        flops=3 * 2 * rows * wide * 3 * LANES,
+        flops=5 * 2 * rows * wide * 3 * LANES,
         name="third",
     )
     moments = lax.all_to_all(

time: 80.9 us -> 82 us (1.014)
  waiting for transfers between devices: 34.1 us -> 32.9 us
  Pallas kernels: 9.24 us -> 10.4 us
    pallas_call x7, Pallas kernels: 9.24 us -> 10.4 us  [call(): pl.pallas_call(kernel, out_shape=[jax.ShapeDtypeStruct(s, F32) if isinsta...]
    ppermute x1, starting transfers between devices: 0.01 us -> 1.07 us  [shards(): prior_right = lax.ppermute(prior_weight[:, :LANES], TX, neighbours(TX, -1))]
    ppermute x1, starting transfers between devices: 1.7 us -> 0.68 us  [shards(): lax.ppermute(prior_weight[:, cols - LANES:], TX, neighbours(TX, 1))]
  transfers between devices with their start and end apart: 7 -> 7, of which waited for: 3 -> 2; matrix products, arithmetic and copies ran while one was open for 0% -> 1% of each run, Pallas kernels for 4% -> 6%
where the time goes in v6:
time: 82 us; the launch traced here: 81.8 us
  waiting for transfers between devices  32.9 us (40%)
  starting transfers between devices  18.7 us (23%)
  blocking collectives  18.3 us (22%)
  Pallas kernels  10.4 us (13%)
    all_to_all x1, waiting for transfers between devices, shards(): lax.all_to_all(message.reshape(devices, 1, length * LANES), TY_TX, split_...  30.7 us
    all_to_all x1, blocking collectives, shards(): lax.all_to_all(moments.reshape(devices, 1, LANES), TY_TX, split_axis=0, c...  18.3 us
    all_to_all x1, starting transfers between devices, shards(): lax.all_to_all(message.reshape(devices, 1, length * LANES), TY_TX, split_...  11.5 us
    pallas_call x7, Pallas kernels, call(): pl.pallas_call(kernel, out_shape=[jax.ShapeDtypeStruct(s, F32) if isinsta...  10.4 us
    ppermute x1, starting transfers between devices, shards(): lax.ppermute(s_up, 'ty', upward)  2.66 us
    ppermute x1, starting transfers between devices, shards(): lax.ppermute(w_up, 'ty', upward)  2.66 us
    ppermute x1, waiting for transfers between devices, shards(): lax.ppermute(s_down, 'ty', downward)  2.18 us
  transfers between devices with their start and end apart: 7, of which 2 were waited for; matrix products, arithmetic and copies ran while one was open for 1% of the time, Pallas kernels for 6%

profile of v6, /device:TPU:1, one launch (start us, length us, event | category | flops | bytes accessed | tf_op | source)
XLA Modules:
  0.0 81.8 jit_solution(15229817671142628198)
XLA Ops:
  0.6 3.6 %pack.1 = f32[4608,128]{1,0:T(8,128)} custom-call(s32[1,128]{1,0:T(1,128)} %bitcast.17, s32[1,128]{1,0:T(1,128)} %bitcast.18, f32[1024,128]{1,0:T(8,128)} %bitcast.15, f32[1024,128]{1,0:T(8,128)} %bitcast.16), custom_call_target="tpu_custom_call" | custom-call | bytes 1049600 | tf_op jit(solution)/shard_map/pack/pallas_call | solution.py:474
  4.2 0.0 copy-start.1
  4.2 11.5 %all-to-all-start = ((f32[128,1,4608]{2,1,0:T(1,128)}), f32[128,1,4608]{2,1,0:T(1,128)S(1)}, u32[]{:S(2)}, u32[]{:S(2)}) async-start(f32[128,1,4608]{2,1,0:T(1,128)} %bitcast.14), calls=%async_computation | async-start | bytes 4718592 | tf_op jit(solution)/shard_map/all_to_all | solution.py:529
  15.7 0.0 copy-done.1
  15.8 0.7 fusion
  16.4 1.1 %collective-permute-start = (f32[128,128]{1,0:T(8,128)}, f32[128,128]{1,0:T(8,128)S(1)}, u32[]{:S(2)}, u32[]{:S(2)}) collective-permute-start(f32[128,128]{1,0:T(8,128)} %get-tuple-element.39), channel_id=1, source_target_pairs={{0,31},{1,0},{2,1},{3,2},{4,3},{5,4},{6,5},{7,6},{8,7},{9,8},{10,9... | collective-permute-start | bytes 196616 | tf_op jit(solution)/shard_map/ppermute | solution.py:502
  17.5 0.7 collective-permute-start.1
  18.2 30.7 %all-to-all-done = f32[128,1,4608]{2,1,0:T(1,128)S(1)} async-done(((f32[128,1,4608]{2,1,0:T(1,128)}), f32[128,1,4608]{2,1,0:T(1,128)S(1)}, u32[]{:S(2)}, u32[]{:S(2)}) %all-to-all-start) | async-done | bytes 2359328 | tf_op jit(solution)/shard_map/all_to_all | solution.py:529
  48.8 0.0 copy-start
  48.8 0.0 copy-start.4
  48.8 0.0 copy-start.5
  48.9 0.6 sums.1
  49.5 0.1 collective-permute-start.4
  49.6 2.7 %collective-permute-start.5 = (f32[64,1152]{1,0:T(8,128)S(1)}, f32[64,1152]{1,0:T(8,128)S(1)}, u32[]{:S(2)}, u32[]{:S(2)}) collective-permute-start(f32[64,1152]{1,0:T(8,128)S(1)} %get-tuple-element.27), channel_id=1, source_target_pairs={{0,96},{32,0},{64,32},{96,64},{1,97},{33,1},{65,33},{97,65},{2,98}... | collective-permute-start | bytes 884744 | tf_op jit(solution)/shard_map/ppermute | solution.py:559
  52.2 0.0 collective-permute-done
  52.2 0.0 collective-permute-done.1
  52.3 0.4 weights.1
  52.7 0.1 collective-permute-start.2
  52.8 2.7 %collective-permute-start.3 = (f32[32,1152]{1,0:T(8,128)S(1)}, f32[32,1152]{1,0:T(8,128)S(1)}, u32[]{:S(2)}, u32[]{:S(2)}) collective-permute-start(f32[32,1152]{1,0:T(8,128)S(1)} %get-tuple-element.23), channel_id=1, source_target_pairs={{0,96},{32,0},{64,32},{96,64},{1,97},{33,1},{65,33},{97,65},{2,98}... | collective-permute-start | bytes 442376 | tf_op jit(solution)/shard_map/ppermute | solution.py:560
  55.4 2.2 %collective-permute-done.4.above_ref = f32[64,1152]{1,0:T(8,128)S(1)} collective-permute-done((f32[64,1152]{1,0:T(8,128)S(1)}, f32[64,1152]{1,0:T(8,128)S(1)}, u32[]{:S(2)}, u32[]{:S(2)}) %collective-permute-start.4) | collective-permute-done | bytes 294944 | tf_op jit(solution)/shard_map/ppermute | solution.py:559
  57.6 0.0 collective-permute-done.5.below_ref
  57.6 0.0 copy-done
  57.6 0.0 copy-done.4
  57.6 0.0 copy-done.5
  57.6 0.0 copy-start.2
  57.7 2.3 %first.1 = (f32[192,1152]{1,0:T(8,128)S(1)}, f32[128,1024]{1,0:T(8,128)S(1)}, f32[128,1024]{1,0:T(8,128)S(1)}, f32[16,128]{1,0:T(8,128)S(1)}) custom-call(f32[128,1152]{1,0:T(8,128)S(1)} %get-tuple-element.24.s_ref, f32[128,1152]{1,0:T(8,128)S(1)} %get-tuple-element.25.w_ref, f32[64,1152]{1,0:T(8,128)S(1)} %collective-permute-done.4.above_ref, ...), custom_call_target="tpu_custom_call" | custom-call | flops 1698693120 | bytes 2686976 | tf_op jit(solution)/shard_map/first/pallas_call | solution.py:474
  60.0 0.0 copy-start.3
  60.0 0.0 copy-done.2
  60.0 1.2 %second.1 = (f32[128,1024]{1,0:T(8,128)S(1)}, f32[64,1024]{1,0:T(8,128)S(1)}, f32[128,1152]{1,0:T(8,128)S(1)}, f32[24,128]{1,0:T(8,128)S(1)}) custom-call(f32[128,1152]{1,0:T(8,128)S(1)} %get-tuple-element.25.w_ref, f32[192,1152]{1,0:T(8,128)S(1)} %get-tuple-element.28.y0_ref, f32[128,1024]{1,0:T(8,128)S(1)} %get-tuple-element.29.root_ref, ...), custom_call_target="tpu_custom_call" | custom-call | flops 566231040 | bytes 3121152 | tf_op jit(solution)/shard_map/second/pallas_call | solution.py:474
  61.2 0.0 collective-permute-done.2.above_ref
  61.2 0.0 collective-permute-done.3.below_ref
  61.2 0.0 copy-done.3
  61.2 0.9 %third.1 = (f32[128,1024]{1,0:T(8,128)S(1)}, f32[128,128]{1,0:T(8,128)S(1)}) custom-call(f32[32,1152]{1,0:T(8,128)S(1)} %collective-permute-done.2.above_ref, f32[32,1152]{1,0:T(8,128)S(1)} %collective-permute-done.3.below_ref, f32[192,1152]{1,0:T(8,128)S(1)} %get-tuple-element.28.y0_ref, f32[128,1024]{1,0:T(8,128)S(1)} %get-tuple-element.29.root_ref, ...), custom_call_target="tpu_custom_call" | custom-call | flops 566231040 | bytes 4157440 | tf_op jit(solution)/shard_map/third/pallas_call | solution.py:474
  62.1 18.3 %all_to_all.10 = f32[128,1,128]{2,1,0:T(1,128)S(1)} all-to-all(f32[128,1,128]{2,1,0:T(1,128)S(1)} %bitcast.13), channel_id=1, replica_groups=mesh['ty'=4,'tx_0'=4,'tx_1'=4,'tx_2'=2] {'ty','tx_0','tx_1','tx_2'}, dimensions={0} | all-to-all | bytes 131072 | tf_op jit(solution)/shard_map/all_to_all | solution.py:619
  80.4 1.4 %combine.1 = (f32[128,1024]{1,0:T(8,128)}, f32[128,1024]{1,0:T(8,128)}) custom-call(f32[128,128]{1,0:T(8,128)S(1)} %bitcast.12, f32[128,1024]{1,0:T(8,128)S(1)} %get-tuple-element.30.r0_ref, f32[128,1024]{1,0:T(8,128)S(1)} %get-tuple-element.32.b0_ref, f32[128,1024]{1,0:T(8,128)S(1)} %get-tuple-element.37.b1_ref), custom_call_target="tpu_custom_call" | custom-call | bytes 1638400 | tf_op jit(solution)/shard_map/combine/pallas_call | solution.py:474
  (2 shorter events, 0.0 us)
Async XLA Ops:
  4.2 11.5 %copy-start.1 = (f32[128,1024]{1,0:T(8,128)S(1)}, f32[128,1024]{1,0:T(8,128)}, u32[]{:S(2)}) copy-start(f32[128,1024]{1,0:T(8,128)} %prior_ref.1) | copy-start | bytes 1572868
  4.2 44.6 %all-to-all-start = ((f32[128,1,4608]{2,1,0:T(1,128)}), f32[128,1,4608]{2,1,0:T(1,128)S(1)}, u32[]{:S(2)}, u32[]{:S(2)}) async-start(f32[128,1,4608]{2,1,0:T(1,128)} %bitcast.14), calls=%async_computation | async-start | bytes 4718592 | tf_op jit(solution)/shard_map/all_to_all | solution.py:529
  16.4 35.8 %collective-permute-start = (f32[128,128]{1,0:T(8,128)}, f32[128,128]{1,0:T(8,128)S(1)}, u32[]{:S(2)}, u32[]{:S(2)}) collective-permute-start(f32[128,128]{1,0:T(8,128)} %get-tuple-element.39), channel_id=1, source_target_pairs={{0,31},{1,0},{2,1},{3,2},{4,3},{5,4},{6,5},{7,6},{8,7},{9,8},{10,9... | collective-permute-start | bytes 196616 | tf_op jit(solution)/shard_map/ppermute | solution.py:502
  17.5 34.8 %collective-permute-start.1 = (f32[128,128]{1,0:T(8,128)}, f32[128,128]{1,0:T(8,128)S(1)}, u32[]{:S(2)}, u32[]{:S(2)}) collective-permute-start(f32[128,128]{1,0:T(8,128)} %get-tuple-element.38), channel_id=1, source_target_pairs={{0,1},{1,2},{2,3},{3,4},{4,5},{5,6},{6,7},{7,8},{8,9},{9,10},{10,1... | collective-permute-start | bytes 196616 | tf_op jit(solution)/shard_map/ppermute | solution.py:503
  48.8 8.8 %copy-start = (bf16[1024,256]{1,0:T(8,128)(2,1)S(1)}, bf16[1024,256]{1,0:T(8,128)(2,1)}, u32[]{:S(2)}) copy-start(bf16[1024,256]{1,0:T(8,128)(2,1)} %constant.17.clone.col_ref) | copy-start | bytes 1572868
  48.8 8.8 %copy-start.4 = (bf16[384,256]{1,0:T(8,128)(2,1)S(1)}, bf16[384,256]{1,0:T(8,128)(2,1)}, u32[]{:S(2)}) copy-start(bf16[384,256]{1,0:T(8,128)(2,1)} %constant.16.clone.row_ref) | copy-start | bytes 589828
  48.8 8.8 %copy-start.5 = (bf16[768,128]{1,0:T(8,128)(2,1)S(1)}, bf16[768,128]{1,0:T(8,128)(2,1)}, u32[]{:S(2)}) copy-start(bf16[768,128]{1,0:T(8,128)(2,1)} %constant.18.clone.edge_ref) | copy-start | bytes 589828
  49.5 8.1 %collective-permute-start.4 = (f32[64,1152]{1,0:T(8,128)S(1)}, f32[64,1152]{1,0:T(8,128)S(1)}, u32[]{:S(2)}, u32[]{:S(2)}) collective-permute-start(f32[64,1152]{1,0:T(8,128)S(1)} %get-tuple-element.26), channel_id=1, source_target_pairs={{0,32},{32,64},{64,96},{96,0},{1,33},{33,65},{65,97},{97,1},{2,34}... | collective-permute-start | bytes 884744 | tf_op jit(solution)/shard_map/ppermute | solution.py:559
  49.6 8.1 %collective-permute-start.5 = (f32[64,1152]{1,0:T(8,128)S(1)}, f32[64,1152]{1,0:T(8,128)S(1)}, u32[]{:S(2)}, u32[]{:S(2)}) collective-permute-start(f32[64,1152]{1,0:T(8,128)S(1)} %get-tuple-element.27), channel_id=1, source_target_pairs={{0,96},{32,0},{64,32},{96,64},{1,97},{33,1},{65,33},{97,65},{2,98}... | collective-permute-start | bytes 884744 | tf_op jit(solution)/shard_map/ppermute | solution.py:559
  52.7 8.5 %collective-permute-start.2 = (f32[32,1152]{1,0:T(8,128)S(1)}, f32[32,1152]{1,0:T(8,128)S(1)}, u32[]{:S(2)}, u32[]{:S(2)}) collective-permute-start(f32[32,1152]{1,0:T(8,128)S(1)} %get-tuple-element.22), channel_id=1, source_target_pairs={{0,32},{32,64},{64,96},{96,0},{1,33},{33,65},{65,97},{97,1},{2,34}... | collective-permute-start | bytes 442376 | tf_op jit(solution)/shard_map/ppermute | solution.py:560
  52.8 8.4 %collective-permute-start.3 = (f32[32,1152]{1,0:T(8,128)S(1)}, f32[32,1152]{1,0:T(8,128)S(1)}, u32[]{:S(2)}, u32[]{:S(2)}) collective-permute-start(f32[32,1152]{1,0:T(8,128)S(1)} %get-tuple-element.23), channel_id=1, source_target_pairs={{0,96},{32,0},{64,32},{96,64},{1,97},{33,1},{65,33},{97,65},{2,98}... | collective-permute-start | bytes 442376 | tf_op jit(solution)/shard_map/ppermute | solution.py:560
  57.6 2.3 %copy-start.2 = (bf16[256,128]{1,0:T(8,128)(2,1)S(1)}, bf16[256,128]{1,0:T(8,128)(2,1)}, u32[]{:S(2)}) copy-start(bf16[256,128]{1,0:T(8,128)(2,1)} %constant.19.clone.own_ref) | copy-start | bytes 196612
  60.0 1.2 %copy-start.3 = (bf16[128,64]{1,0:T(8,128)(2,1)S(1)}, bf16[128,64]{1,0:T(8,128)(2,1)}, u32[]{:S(2)}) copy-start(bf16[128,64]{1,0:T(8,128)(2,1)} %constant.20.clone.halo_ref) | copy-start | bytes 49156

commit v7 on v6

--- a/solution.py
+++ b/solution.py
@@ -248,13 +248,6 @@
     down_ref[...] = w_ref[rows - HALF :, :]
 
 
-def with_halo(n_ty, above_ref, ref, below_ref, at):
-    row_at = lax.axis_index("ty")
-    above = above_ref[:, at] * jnp.where(row_at > 0, 1.0, 0.0)
-    below = below_ref[:, at] * jnp.where(row_at < n_ty - 1, 1.0, 0.0)
-    return jnp.concatenate([above, ref[:, at], below], axis=0)
-
-
 def along_columns(pieces, taps_ref):
     height, wide = pieces[0].shape
     cols = wide - LANES
@@ -274,16 +267,24 @@
     return out
 
 
-def first_kernel(
-    n_ty,
+def all_columns(mid, y0_ref, at, col_ref, edge_ref):
+    wide = mid.shape[1]
+    cols = wide - LANES
+    pieces = split3(mid)
+    for c, y in enumerate(along_columns(pieces, col_ref)):
+        y0_ref[at, 2 * c * LANES : 2 * (c + 1) * LANES] = y
+    near = [jnp.concatenate([x[:, cols - LANES :], x[:, :LANES]], axis=1) for x in pieces]
+    y0_ref[at, cols:] = times_taps(near, edge_ref)
+
+
+def early_kernel(
     s_ref,
     w_ref,
-    above_ref,
-    below_ref,
-    row_ref,
+    own_ref,
     col_ref,
     edge_ref,
-    y0_ref,
+    part_ref,
+    deep_ref,
     root_ref,
     r0_ref,
     sums_ref,
@@ -291,13 +292,12 @@
 ):
     rows, wide = s_ref.shape
     cols = wide - LANES
+    edge = 4 * HALF
     for at in spans(wide):
-        mid_ref[:, at] = taps_times(row_ref, with_halo(n_ty, above_ref, s_ref, below_ref, at))
-    pieces = split3(mid_ref[...])
-    for c, y in enumerate(along_columns(pieces, col_ref)):
-        y0_ref[:, 2 * c * LANES : 2 * (c + 1) * LANES] = y
-    near = [jnp.concatenate([x[:, cols - LANES :], x[:, :LANES]], axis=1) for x in pieces]
-    y0_ref[:, cols:] = times_taps(near, edge_ref)
+        mid = taps_times(own_ref, s_ref[:, at])
+        part_ref[:, at] = mid[:edge]
+        mid_ref[:, at] = mid[edge:]
+    all_columns(mid_ref[...], deep_ref, slice(None), col_ref, edge_ref)
     total_rr = total_rb = jnp.zeros((8, cols), F32)
     for r in range(0, rows, 8):
         at = slice(r, r + 8)
@@ -307,11 +307,45 @@
         root_ref[at, :] = root
         r0_ref[at, :] = r0
         total_rr += r0 * r0
-        total_rb += s * y0_ref[HALF + r : HALF + r + 8, :cols]
-    for i, total in enumerate((total_rr, total_rb)):
-        sums_ref[8 * i : 8 * i + 8, :] = sum(
-            total[:, c : c + LANES] for c in range(0, cols, LANES)
-        )
+        if HALF <= r < rows - HALF:
+            total_rb += s * deep_ref[r - HALF : r - HALF + 8, :cols]
+    sums_ref[0:8, :] = folded(total_rr)
+    sums_ref[8:16, :] = folded(total_rb)
+
+
+def first_kernel(
+    n_ty,
+    s_ref,
+    above_ref,
+    below_ref,
+    part_ref,
+    deep_ref,
+    early_ref,
+    halo_ref,
+    col_ref,
+    edge_ref,
+    y0_ref,
+    sums_ref,
+    mid_ref,
+    border_ref,
+):
+    rows, wide = s_ref.shape
+    cols = wide - LANES
+    row_at = lax.axis_index("ty")
+    has_above = jnp.where(row_at > 0, 1.0, 0.0)
+    has_below = jnp.where(row_at < n_ty - 1, 1.0, 0.0)
+    for at in spans(wide):
+        halo = jnp.concatenate([above_ref[:, at] * has_above, below_ref[:, at] * has_below], axis=0)
+        mid_ref[:, at] = part_ref[:, at] + taps_times(halo_ref, halo)
+    all_columns(mid_ref[...], border_ref, slice(None), col_ref, edge_ref)
+    two = 2 * HALF
+    y0_ref[:two, :] = border_ref[:two, :]
+    y0_ref[two:rows, :] = deep_ref[...]
+    y0_ref[rows:, :] = border_ref[two:, :]
+    top = s_ref[:HALF, :cols] * border_ref[HALF:two, :cols]
+    bottom = s_ref[rows - HALF :, :cols] * border_ref[two : two + HALF, :cols]
+    sums_ref[0:8, :] = early_ref[0:8, :]
+    sums_ref[8:16, :] = early_ref[8:16, :] + folded(top) + folded(bottom)
 
 
 def folded(total):
@@ -560,27 +594,47 @@
     w_above, w_below = lax.ppermute(w_down, "ty", downward), lax.ppermute(w_up, "ty", upward)
 
     tall = rows + 2 * HALF
-    row_taps = taps(np.arange(tall)[:, None] - np.arange(rows + 4 * HALF)[None, :] + HALF, 0)
     col_taps = taps(np.arange(2 * LANES)[None, :] - np.arange(4 * LANES)[:, None] + LANES, 0)
     ring = np.where(np.arange(LANES) < 64, cols, -LANES) + np.arange(LANES)
     near = np.concatenate([np.arange(cols - LANES, cols), ring, np.arange(LANES)])
     edge_taps = taps(ring[None, :] - near[:, None], 0)
     tile = (rows, cols)
-    y0, root, r0, early = call(
-        functools.partial(first_kernel, n_ty),
-        [(tall, wide), tile, tile, (16, LANES)],
+    inside = np.arange(rows)
+    border_rows = np.concatenate(
+        [np.arange(-HALF, HALF), np.arange(rows - HALF, rows + HALF)]
+    )
+    early_rows = np.concatenate([border_rows, inside[HALF : rows - HALF]])
+    far_rows = np.concatenate([np.arange(-2 * HALF, 0), np.arange(rows, rows + 2 * HALF)])
+    early_taps = taps(early_rows[:, None] - inside[None, :], 0)
+    first_taps = taps(border_rows[:, None] - far_rows[None, :], 0)
+    part, deep, root, r0, early = call(
+        early_kernel,
+        [(4 * HALF, wide), (rows - 2 * HALF, wide), tile, tile, (16, LANES)],
         s,
         w,
+        early_taps,
+        col_taps,
+        edge_taps,
+        scratch=[pltpu.VMEM((rows - 2 * HALF, wide), F32)],
+        flops=5 * 2 * tall * wide * 3 * LANES,
+        name="early",
+    )
+    y0, early = call(
+        functools.partial(first_kernel, n_ty),
+        [(tall, wide), (16, LANES)],
+        s,
         s_above,
         s_below,
-        row_taps,
+        part,
+        deep,
+        early,
+        first_taps,
         col_taps,
         edge_taps,
-        scratch=[pltpu.VMEM((tall, wide), F32)],
-        flops=5 * 2 * tall * wide * (2 * LANES + 4 * LANES),
+        scratch=[pltpu.VMEM((4 * HALF, wide), F32), pltpu.VMEM((4 * HALF, wide), F32)],
+        flops=5 * 2 * rows * wide * 6 * LANES,
         name="first",
     )
-    inside = np.arange(rows)
     own_taps = taps(inside[:, None] - inside[None, :], 0)
     border = np.concatenate([inside[:HALF], inside[rows - HALF :]])
     outside = np.concatenate([np.arange(-HALF, 0), np.arange(rows, rows + HALF)])

time: 82 us -> 81.3 us (level)
    ppermute x1, waiting for transfers between devices: 2.18 us -> 0.75 us  [shards(): lax.ppermute(s_down, 'ty', downward)]
    ppermute x1, starting transfers between devices: 1.07 us -> 0.01 us  [shards(): prior_right = lax.ppermute(prior_weight[:, :LANES], TX, neighbours(TX, -1))]
    ppermute x1, starting transfers between devices: 0.68 us -> 1.7 us  [shards(): lax.ppermute(prior_weight[:, cols - LANES:], TX, neighbours(TX, 1))]
    pallas_call x7 -> x8, Pallas kernels: 10.4 us -> 11.2 us  [call(): pl.pallas_call(kernel, out_shape=[jax.ShapeDtypeStruct(s, F32) if isinsta...]
  transfers between devices with their start and end apart: 7 -> 7, of which waited for: 2 -> 3; matrix products, arithmetic and copies ran while one was open for 1% -> 0% of each run, Pallas kernels for 6% -> 6%
where the time goes in v7:
time: 81.3 us; the launch traced here: 81.1 us
  waiting for transfers between devices  32.5 us (40%)
  starting transfers between devices  18.7 us (23%)
  blocking collectives  17.9 us (22%)
  Pallas kernels  11.2 us (14%)
    all_to_all x1, waiting for transfers between devices, shards(): lax.all_to_all(message.reshape(devices, 1, length * LANES), TY_TX, split_...  31.4 us
    all_to_all x1, blocking collectives, shards(): lax.all_to_all(moments.reshape(devices, 1, LANES), TY_TX, split_axis=0, c...  17.9 us
    all_to_all x1, starting transfers between devices, shards(): lax.all_to_all(message.reshape(devices, 1, length * LANES), TY_TX, split_...  11.5 us
    pallas_call x8, Pallas kernels, call(): pl.pallas_call(kernel, out_shape=[jax.ShapeDtypeStruct(s, F32) if isinsta...  11.2 us
    ppermute x1, starting transfers between devices, shards(): lax.ppermute(s_up, 'ty', upward)  2.66 us
    ppermute x1, starting transfers between devices, shards(): lax.ppermute(w_up, 'ty', upward)  2.66 us
    ppermute x1, starting transfers between devices, shards(): lax.ppermute(prior_weight[:, cols - LANES:], TX, neighbours(TX, 1))  1.7 us
  transfers between devices with their start and end apart: 7, of which 3 were waited for; matrix products, arithmetic and copies ran while one was open for 0% of the time, Pallas kernels for 6%

profile of v7, /device:TPU:1, one launch (start us, length us, event | category | flops | bytes accessed | tf_op | source)
XLA Modules:
  0.0 81.1 jit_solution(4365670552307498156)
XLA Ops:
  0.6 3.6 %pack.1 = f32[4608,128]{1,0:T(8,128)} custom-call(s32[1,128]{1,0:T(1,128)} %bitcast.17, s32[1,128]{1,0:T(1,128)} %bitcast.18, f32[1024,128]{1,0:T(8,128)} %bitcast.15, f32[1024,128]{1,0:T(8,128)} %bitcast.16), custom_call_target="tpu_custom_call" | custom-call | bytes 1049600 | tf_op jit(solution)/shard_map/pack/pallas_call | solution.py:508
  4.2 0.0 copy-start.1
  4.3 11.5 %all-to-all-start = ((f32[128,1,4608]{2,1,0:T(1,128)}), f32[128,1,4608]{2,1,0:T(1,128)S(1)}, u32[]{:S(2)}, u32[]{:S(2)}) async-start(f32[128,1,4608]{2,1,0:T(1,128)} %bitcast.14), calls=%async_computation | async-start | bytes 4718592 | tf_op jit(solution)/shard_map/all_to_all | solution.py:563
  15.8 0.0 copy-done.1
  15.8 1.7 %collective-permute-start.1 = (f32[128,128]{1,0:T(8,128)S(1)}, f32[128,128]{1,0:T(8,128)S(1)}, u32[]{:S(2)}, u32[]{:S(2)}) collective-permute-start(f32[128,128]{1,0:T(8,128)S(1)} %get-tuple-element.44), channel_id=1, source_target_pairs={{0,1},{1,2},{2,3},{3,4},{4,5},{5,6},{6,7},{7,8},{8,9},{9,10},{10,1... | collective-permute-start | bytes 196616 | tf_op jit(solution)/shard_map/ppermute | solution.py:537
  17.5 0.0 collective-permute-start
  17.5 31.4 %all-to-all-done = f32[128,1,4608]{2,1,0:T(1,128)S(1)} async-done(((f32[128,1,4608]{2,1,0:T(1,128)}), f32[128,1,4608]{2,1,0:T(1,128)S(1)}, u32[]{:S(2)}, u32[]{:S(2)}) %all-to-all-start) | async-done | bytes 2359328 | tf_op jit(solution)/shard_map/all_to_all | solution.py:563
  48.9 0.0 copy-start
  48.9 0.0 copy-start.4
  48.9 0.0 copy-start.5
  48.9 0.6 sums.1
  49.5 0.1 collective-permute-start.4
  49.6 2.7 %collective-permute-start.5 = (f32[64,1152]{1,0:T(8,128)S(1)}, f32[64,1152]{1,0:T(8,128)S(1)}, u32[]{:S(2)}, u32[]{:S(2)}) collective-permute-start(f32[64,1152]{1,0:T(8,128)S(1)} %get-tuple-element.29), channel_id=1, source_target_pairs={{0,96},{32,0},{64,32},{96,64},{1,97},{33,1},{65,33},{97,65},{2,98}... | collective-permute-start | bytes 884744 | tf_op jit(solution)/shard_map/ppermute | solution.py:593
  52.3 0.0 collective-permute-done.1
  52.3 0.0 collective-permute-done
  52.3 0.0 copy-start.6
  52.3 0.4 weights.1
  52.7 0.1 collective-permute-start.2
  52.8 2.7 %collective-permute-start.3 = (f32[32,1152]{1,0:T(8,128)S(1)}, f32[32,1152]{1,0:T(8,128)S(1)}, u32[]{:S(2)}, u32[]{:S(2)}) collective-permute-start(f32[32,1152]{1,0:T(8,128)S(1)} %get-tuple-element.26), channel_id=1, source_target_pairs={{0,96},{32,0},{64,32},{96,64},{1,97},{33,1},{65,33},{97,65},{2,98}... | collective-permute-start | bytes 442376 | tf_op jit(solution)/shard_map/ppermute | solution.py:594
  55.5 0.0 copy-done
  55.5 0.0 copy-done.4
  55.5 0.0 copy-done.5
  55.5 1.4 %early.1 = (f32[128,1152]{1,0:T(8,128)S(1)}, f32[64,1152]{1,0:T(8,128)S(1)}, f32[128,1024]{1,0:T(8,128)S(1)}, f32[128,1024]{1,0:T(8,128)S(1)}, f32[16,128]{1,0:T(8,128)S(1)}) custom-call(f32[128,1152]{1,0:T(8,128)S(1)} %get-tuple-element.27.s_ref, f32[128,1152]{1,0:T(8,128)S(1)} %get-tuple-element.30.w_ref, bf16[384,128]{1,0:T(8,128)(2,1)S(1)} %copy-done.5, ...), custom_call_target="tpu_custom_call" | custom-call | flops 849346560 | bytes 1998848 | tf_op jit(solution)/shard_map/early/pallas_call | solution.py:508
  56.9 0.0 copy-start.2
  56.9 0.7 collective-permute-done.4.above_ref
  57.7 0.0 collective-permute-done.5.below_ref
  57.7 0.0 copy-done.6
  57.7 1.6 %first.1 = (f32[192,1152]{1,0:T(8,128)S(1)}, f32[16,128]{1,0:T(8,128)S(1)}) custom-call(f32[128,1152]{1,0:T(8,128)S(1)} %get-tuple-element.27.s_ref, f32[64,1152]{1,0:T(8,128)S(1)} %collective-permute-done.4.above_ref, f32[64,1152]{1,0:T(8,128)S(1)} %collective-permute-done.5.below_ref, f32[128,1152]{1,0:T(8,128)S(1)} %get-tuple-element.31.part_ref, ...), custom_call_target="tpu_custom_call" | custom-call | flops 1132462080 | bytes 2859008 | tf_op jit(solution)/shard_map/first/pallas_call | solution.py:508
  59.2 0.0 copy-start.3
  59.2 0.0 copy-done.2
  59.3 1.2 %second.1 = (f32[128,1024]{1,0:T(8,128)S(1)}, f32[64,1024]{1,0:T(8,128)S(1)}, f32[128,1152]{1,0:T(8,128)S(1)}, f32[24,128]{1,0:T(8,128)S(1)}) custom-call(f32[128,1152]{1,0:T(8,128)S(1)} %get-tuple-element.30.w_ref, f32[192,1152]{1,0:T(8,128)S(1)} %get-tuple-element.34.y0_ref, f32[128,1024]{1,0:T(8,128)S(1)} %get-tuple-element.35.root_ref, ...), custom_call_target="tpu_custom_call" | custom-call | flops 566231040 | bytes 3121152 | tf_op jit(solution)/shard_map/second/pallas_call | solution.py:508
  60.4 0.4 collective-permute-done.2.above_ref
  60.8 0.0 collective-permute-done.3.below_ref
  60.8 0.0 copy-done.3
  60.8 0.9 %third.1 = (f32[128,1024]{1,0:T(8,128)S(1)}, f32[128,128]{1,0:T(8,128)S(1)}) custom-call(f32[32,1152]{1,0:T(8,128)S(1)} %collective-permute-done.2.above_ref, f32[32,1152]{1,0:T(8,128)S(1)} %collective-permute-done.3.below_ref, f32[192,1152]{1,0:T(8,128)S(1)} %get-tuple-element.34.y0_ref, f32[128,1024]{1,0:T(8,128)S(1)} %get-tuple-element.35.root_ref, ...), custom_call_target="tpu_custom_call" | custom-call | flops 566231040 | bytes 4157440 | tf_op jit(solution)/shard_map/third/pallas_call | solution.py:508
  61.8 17.9 %all_to_all.10 = f32[128,1,128]{2,1,0:T(1,128)S(1)} all-to-all(f32[128,1,128]{2,1,0:T(1,128)S(1)} %bitcast.13), channel_id=1, replica_groups=mesh['ty'=4,'tx_0'=4,'tx_1'=4,'tx_2'=2] {'ty','tx_0','tx_1','tx_2'}, dimensions={0} | all-to-all | bytes 131072 | tf_op jit(solution)/shard_map/all_to_all | solution.py:673
  79.7 1.4 %combine.1 = (f32[128,1024]{1,0:T(8,128)}, f32[128,1024]{1,0:T(8,128)}) custom-call(f32[128,128]{1,0:T(8,128)S(1)} %bitcast.12, f32[128,1024]{1,0:T(8,128)S(1)} %get-tuple-element.36.r0_ref, f32[128,1024]{1,0:T(8,128)S(1)} %get-tuple-element.38.b0_ref, f32[128,1024]{1,0:T(8,128)S(1)} %get-tuple-element.43.b1_ref), custom_call_target="tpu_custom_call" | custom-call | bytes 1638400 | tf_op jit(solution)/shard_map/combine/pallas_call | solution.py:508
  (3 shorter events, 0.0 us)
Async XLA Ops:
  4.2 11.5 %copy-start.1 = (f32[128,1024]{1,0:T(8,128)S(1)}, f32[128,1024]{1,0:T(8,128)}, u32[]{:S(2)}) copy-start(f32[128,1024]{1,0:T(8,128)} %prior_ref.1) | copy-start | bytes 1572868
  4.3 44.6 %all-to-all-start = ((f32[128,1,4608]{2,1,0:T(1,128)}), f32[128,1,4608]{2,1,0:T(1,128)S(1)}, u32[]{:S(2)}, u32[]{:S(2)}) async-start(f32[128,1,4608]{2,1,0:T(1,128)} %bitcast.14), calls=%async_computation | async-start | bytes 4718592 | tf_op jit(solution)/shard_map/all_to_all | solution.py:563
  15.8 36.5 %collective-permute-start.1 = (f32[128,128]{1,0:T(8,128)S(1)}, f32[128,128]{1,0:T(8,128)S(1)}, u32[]{:S(2)}, u32[]{:S(2)}) collective-permute-start(f32[128,128]{1,0:T(8,128)S(1)} %get-tuple-element.44), channel_id=1, source_target_pairs={{0,1},{1,2},{2,3},{3,4},{4,5},{5,6},{6,7},{7,8},{8,9},{9,10},{10,1... | collective-permute-start | bytes 196616 | tf_op jit(solution)/shard_map/ppermute | solution.py:537
  17.5 34.8 %collective-permute-start = (f32[128,128]{1,0:T(8,128)S(1)}, f32[128,128]{1,0:T(8,128)S(1)}, u32[]{:S(2)}, u32[]{:S(2)}) collective-permute-start(f32[128,128]{1,0:T(8,128)S(1)} %get-tuple-element.45), channel_id=1, source_target_pairs={{0,31},{1,0},{2,1},{3,2},{4,3},{5,4},{6,5},{7,6},{8,7},{9,8},{10,9... | collective-permute-start | bytes 196616 | tf_op jit(solution)/shard_map/ppermute | solution.py:536
  48.9 6.6 %copy-start = (bf16[1024,256]{1,0:T(8,128)(2,1)S(1)}, bf16[1024,256]{1,0:T(8,128)(2,1)}, u32[]{:S(2)}) copy-start(bf16[1024,256]{1,0:T(8,128)(2,1)} %constant.18.clone.col_ref) | copy-start | bytes 1572868
  48.9 6.6 %copy-start.4 = (bf16[768,128]{1,0:T(8,128)(2,1)S(1)}, bf16[768,128]{1,0:T(8,128)(2,1)}, u32[]{:S(2)}) copy-start(bf16[768,128]{1,0:T(8,128)(2,1)} %constant.19.clone.edge_ref) | copy-start | bytes 589828
  48.9 6.6 %copy-start.5 = (bf16[384,128]{1,0:T(8,128)(2,1)S(1)}, bf16[384,128]{1,0:T(8,128)(2,1)}, u32[]{:S(2)}) copy-start(bf16[384,128]{1,0:T(8,128)(2,1)} %constant.20.clone.own_ref) | copy-start | bytes 294916
  49.5 8.1 %collective-permute-start.4 = (f32[64,1152]{1,0:T(8,128)S(1)}, f32[64,1152]{1,0:T(8,128)S(1)}, u32[]{:S(2)}, u32[]{:S(2)}) collective-permute-start(f32[64,1152]{1,0:T(8,128)S(1)} %get-tuple-element.28), channel_id=1, source_target_pairs={{0,32},{32,64},{64,96},{96,0},{1,33},{33,65},{65,97},{97,1},{2,34}... | collective-permute-start | bytes 884744 | tf_op jit(solution)/shard_map/ppermute | solution.py:593
  49.6 8.1 %collective-permute-start.5 = (f32[64,1152]{1,0:T(8,128)S(1)}, f32[64,1152]{1,0:T(8,128)S(1)}, u32[]{:S(2)}, u32[]{:S(2)}) collective-permute-start(f32[64,1152]{1,0:T(8,128)S(1)} %get-tuple-element.29), channel_id=1, source_target_pairs={{0,96},{32,0},{64,32},{96,64},{1,97},{33,1},{65,33},{97,65},{2,98}... | collective-permute-start | bytes 884744 | tf_op jit(solution)/shard_map/ppermute | solution.py:593
  52.3 5.4 %copy-start.6 = (bf16[256,128]{1,0:T(8,128)(2,1)S(1)}, bf16[256,128]{1,0:T(8,128)(2,1)}, u32[]{:S(2)}) copy-start(bf16[256,128]{1,0:T(8,128)(2,1)} %constant.21.clone.halo_ref) | copy-start | bytes 196612
  52.7 8.1 %collective-permute-start.2 = (f32[32,1152]{1,0:T(8,128)S(1)}, f32[32,1152]{1,0:T(8,128)S(1)}, u32[]{:S(2)}, u32[]{:S(2)}) collective-permute-start(f32[32,1152]{1,0:T(8,128)S(1)} %get-tuple-element.25), channel_id=1, source_target_pairs={{0,32},{32,64},{64,96},{96,0},{1,33},{33,65},{65,97},{97,1},{2,34}... | collective-permute-start | bytes 442376 | tf_op jit(solution)/shard_map/ppermute | solution.py:594
  52.8 8.0 %collective-permute-start.3 = (f32[32,1152]{1,0:T(8,128)S(1)}, f32[32,1152]{1,0:T(8,128)S(1)}, u32[]{:S(2)}, u32[]{:S(2)}) collective-permute-start(f32[32,1152]{1,0:T(8,128)S(1)} %get-tuple-element.26), channel_id=1, source_target_pairs={{0,96},{32,0},{64,32},{96,64},{1,97},{33,1},{65,33},{97,65},{2,98}... | collective-permute-start | bytes 442376 | tf_op jit(solution)/shard_map/ppermute | solution.py:594
  56.9 2.3 %copy-start.2 = (bf16[256,128]{1,0:T(8,128)(2,1)S(1)}, bf16[256,128]{1,0:T(8,128)(2,1)}, u32[]{:S(2)}) copy-start(bf16[256,128]{1,0:T(8,128)(2,1)} %constant.22.clone.own_ref) | copy-start | bytes 196612
  59.2 1.6 %copy-start.3 = (bf16[128,64]{1,0:T(8,128)(2,1)S(1)}, bf16[128,64]{1,0:T(8,128)(2,1)}, u32[]{:S(2)}) copy-start(bf16[128,64]{1,0:T(8,128)(2,1)} %constant.23.clone.halo_ref) | copy-start | bytes 49156

commit v8 on v7

--- a/solution.py
+++ b/solution.py
@@ -177,6 +177,25 @@
     return got_ref[pl.ds(at, devices, stride=length), :]
 
 
+def odd_row():
+    return lax.rem(lax.axis_index("ty"), 2)
+
+
+def to_partners(ref, near_ref, next_ref):
+    rows, count = ref.shape[0], near_ref.shape[0]
+    bottom = (rows - count) * (1 - odd_row())
+    near_ref[...] = ref[pl.ds(pl.multiple_of(bottom, 8), count), :]
+    next_ref[...] = ref[pl.ds(pl.multiple_of(rows - count - bottom, 8), count), :]
+
+
+def from_partners(n_ty, near_ref, next_ref, at):
+    row_at, odd = lax.axis_index("ty"), odd_row() == 1
+    near, far = near_ref[:, at], next_ref[:, at]
+    above = jnp.where(odd, near, far) * jnp.where(row_at > 0, 1.0, 0.0)
+    below = jnp.where(odd, far, near) * jnp.where(row_at < n_ty - 1, 1.0, 0.0)
+    return above, below
+
+
 def gather_tile(got_ref, parts, length, which, select, dst, extra):
     devices = got_ref.shape[0] // length
     for c in range(0, parts, 2):
@@ -198,7 +217,7 @@
         dst[:, at] = y if extra is None else y + extra[:, at]
 
 
-def sums_kernel(parts, length, got_ref, s_ref, up_ref, down_ref, select_ref, strip_ref):
+def sums_kernel(parts, length, got_ref, s_ref, near_ref, next_ref, select_ref, strip_ref):
     rows, wide = s_ref.shape
     cols = wide - LANES
     devices = got_ref.shape[0] // length
@@ -222,13 +241,12 @@
     lane = iota((rows, LANES), 1)
     s_ref[:, cols:] = jnp.where(lane < 64, right, left)
     strip_ref[...] = jnp.where(lane < 64, pltpu.roll(right, 64, 1), pltpu.roll(left, 64, 1))
-    up_ref[...] = s_ref[: 2 * HALF, :]
-    down_ref[...] = s_ref[rows - 2 * HALF :, :]
+    to_partners(s_ref, near_ref, next_ref)
 
 
 def weights_kernel(
     parts, length, n_tx, got_ref, prior_ref, prior_halo_ref, select_ref, strip_ref,
-    w_ref, up_ref, down_ref
+    w_ref, near_ref, next_ref
 ):
     rows, wide = w_ref.shape
     cols = wide - LANES
@@ -244,8 +262,7 @@
         prior_halo * has_right + strip,
         jnp.where(lane >= LANES - HALF, prior_halo * has_left + strip, 0.0),
     )
-    up_ref[...] = w_ref[:HALF, :]
-    down_ref[...] = w_ref[rows - HALF :, :]
+    to_partners(w_ref, near_ref, next_ref)
 
 
 def along_columns(pieces, taps_ref):
@@ -316,8 +333,8 @@
 def first_kernel(
     n_ty,
     s_ref,
-    above_ref,
-    below_ref,
+    near_ref,
+    next_ref,
     part_ref,
     deep_ref,
     early_ref,
@@ -331,11 +348,8 @@
 ):
     rows, wide = s_ref.shape
     cols = wide - LANES
-    row_at = lax.axis_index("ty")
-    has_above = jnp.where(row_at > 0, 1.0, 0.0)
-    has_below = jnp.where(row_at < n_ty - 1, 1.0, 0.0)
     for at in spans(wide):
-        halo = jnp.concatenate([above_ref[:, at] * has_above, below_ref[:, at] * has_below], axis=0)
+        halo = jnp.concatenate(from_partners(n_ty, near_ref, next_ref, at), axis=0)
         mid_ref[:, at] = part_ref[:, at] + taps_times(halo_ref, halo)
     all_columns(mid_ref[...], border_ref, slice(None), col_ref, edge_ref)
     two = 2 * HALF
@@ -409,8 +423,8 @@
 
 def third_kernel(
     n_ty,
-    above_ref,
-    below_ref,
+    near_ref,
+    next_ref,
     y0_ref,
     root_ref,
     r0_ref,
@@ -426,9 +440,6 @@
 ):
     rows, wide = part_ref.shape
     cols = wide - LANES
-    row_at = lax.axis_index("ty")
-    has_above = jnp.where(row_at > 0, 1.0, 0.0)
-    has_below = jnp.where(row_at < n_ty - 1, 1.0, 0.0)
     top, bottom = slice(0, HALF), slice(rows - HALF, rows)
     b1_ref[HALF : rows - HALF, :] = inner_ref[...]
     known = sums_ref[0:1, :]
@@ -439,12 +450,9 @@
         return jnp.concatenate([ref[top, at], ref[bottom, at]], axis=0)
 
     for at in spans(wide):
+        above, below = from_partners(n_ty, near_ref, next_ref, at)
         z = jnp.concatenate(
-            [
-                above_ref[:, at] * has_above * y0_ref[:HALF, at],
-                below_ref[:, at] * has_below * y0_ref[rows + HALF :, at],
-            ],
-            axis=0,
+            [above * y0_ref[:HALF, at], below * y0_ref[rows + HALF :, at]], axis=0
         )
         mid_ref[:, at] = border(part_ref, at) + taps_times(halo_ref, z)
     total_vq, total_mix = sums_ref[8:16, :], sums_ref[16:24, :]
@@ -564,7 +572,7 @@
         message.reshape(devices, 1, length * LANES), TY_TX, split_axis=0, concat_axis=0, tiled=True
     ).reshape(devices * length, LANES)
     s_slab, w_slab = (2 * HALF, wide), (HALF, wide)
-    s, s_up, s_down, chosen, strip = call(
+    s, s_near, s_next, chosen, strip = call(
         functools.partial(sums_kernel, parts, length),
         [
             (rows, wide),
@@ -577,7 +585,7 @@
         flops=3 * 2 * rows * wide * SLOTS * devices,
         name="sums",
     )
-    w, w_up, w_down = call(
+    w, w_near, w_next = call(
         functools.partial(weights_kernel, parts, length, n_tx),
         [(rows, wide), w_slab, w_slab],
         got,
@@ -589,9 +597,10 @@
         name="weights",
     )
     n_ty = lax.axis_size("ty")
-    downward, upward = neighbours(("ty",), 1), neighbours(("ty",), -1)
-    s_above, s_below = lax.ppermute(s_down, "ty", downward), lax.ppermute(s_up, "ty", upward)
-    w_above, w_below = lax.ppermute(w_down, "ty", downward), lax.ppermute(w_up, "ty", upward)
+    near = [(i, i ^ 1) for i in range(n_ty)]
+    far = [((i + 1) % n_ty, ((i ^ 1) + 1) % n_ty) for i in range(n_ty)]
+    s_near, s_next = lax.ppermute(s_near, "ty", near), lax.ppermute(s_next, "ty", far)
+    w_near, w_next = lax.ppermute(w_near, "ty", near), lax.ppermute(w_next, "ty", far)
 
     tall = rows + 2 * HALF
     col_taps = taps(np.arange(2 * LANES)[None, :] - np.arange(4 * LANES)[:, None] + LANES, 0)
@@ -623,8 +632,8 @@
         functools.partial(first_kernel, n_ty),
         [(tall, wide), (16, LANES)],
         s,
-        s_above,
-        s_below,
+        s_near,
+        s_next,
         part,
         deep,
         early,
@@ -655,8 +664,8 @@
     b1, moments = call(
         functools.partial(third_kernel, n_ty),
         [tile, (devices, LANES)],
-        w_above,
-        w_below,
+        w_near,
+        w_next,
         y0,
         root,
         r0,

time: 81.3 us -> 80.4 us (0.989)
  starting transfers between devices: 18.7 us -> 16.9 us
  waiting for transfers between devices: 32.5 us -> 34.1 us
    ppermute x4, starting transfers between devices: 5.48 us -> 3.69 us  [the longest x1 1.88 us: shards(): lax.ppermute(w_next, 'ty', far)]
    ppermute x4, waiting for transfers between devices: 1.16 us -> 2.69 us  [the longest x1 1.33 us: shards(): lax.ppermute(s_near, 'ty', near)]
  transfers between devices with their start and end apart: 7 -> 7, of which waited for: 3 -> 4; matrix products, arithmetic and copies ran while one was open for 0% -> 0% of each run, Pallas kernels for 6% -> 7%
where the time goes in v8:
time: 80.4 us; the launch traced here: 80.2 us
  waiting for transfers between devices  34.1 us (42%)
  blocking collectives  17.2 us (21%)
  starting transfers between devices  16.9 us (21%)
  Pallas kernels  11.3 us (14%)
    all_to_all x1, waiting for transfers between devices, shards(): lax.all_to_all(message.reshape(devices, 1, length * LANES), TY_TX, split_...  31.4 us
    all_to_all x1, blocking collectives, shards(): lax.all_to_all(moments.reshape(devices, 1, LANES), TY_TX, split_axis=0, c...  17.2 us
    all_to_all x1, starting transfers between devices, shards(): lax.all_to_all(message.reshape(devices, 1, length * LANES), TY_TX, split_...  11.5 us
    pallas_call x8, Pallas kernels, call(): pl.pallas_call(kernel, out_shape=[jax.ShapeDtypeStruct(s, F32) if isinsta...  11.3 us
    ppermute x1, starting transfers between devices, shards(): lax.ppermute(w_next, 'ty', far)  1.88 us
    ppermute x1, starting transfers between devices, shards(): lax.ppermute(prior_weight[:, cols - LANES:], TX, neighbours(TX, 1))  1.7 us
  transfers between devices with their start and end apart: 7, of which 4 were waited for; matrix products, arithmetic and copies ran while one was open for 0% of the time, Pallas kernels for 7%

profile of v8, /device:TPU:1, one launch (start us, length us, event | category | flops | bytes accessed | tf_op | source)
XLA Modules:
  0.0 80.2 jit_solution(6668236160081707546)
XLA Ops:
  0.6 3.6 %pack.1 = f32[4608,128]{1,0:T(8,128)} custom-call(s32[1,128]{1,0:T(1,128)} %bitcast.17, s32[1,128]{1,0:T(1,128)} %bitcast.18, f32[1024,128]{1,0:T(8,128)} %bitcast.15, f32[1024,128]{1,0:T(8,128)} %bitcast.16), custom_call_target="tpu_custom_call" | custom-call | bytes 1049600 | tf_op jit(solution)/shard_map/pack/pallas_call | solution.py:516
  4.2 0.0 copy-start.1
  4.3 11.5 %all-to-all-start = ((f32[128,1,4608]{2,1,0:T(1,128)}), f32[128,1,4608]{2,1,0:T(1,128)S(1)}, u32[]{:S(2)}, u32[]{:S(2)}) async-start(f32[128,1,4608]{2,1,0:T(1,128)} %bitcast.14), calls=%async_computation | async-start | bytes 4718592 | tf_op jit(solution)/shard_map/all_to_all | solution.py:571
  15.8 0.0 copy-done.1
  15.8 1.7 %collective-permute-start.1 = (f32[128,128]{1,0:T(8,128)S(1)}, f32[128,128]{1,0:T(8,128)S(1)}, u32[]{:S(2)}, u32[]{:S(2)}) collective-permute-start(f32[128,128]{1,0:T(8,128)S(1)} %get-tuple-element.44), channel_id=1, source_target_pairs={{0,1},{1,2},{2,3},{3,4},{4,5},{5,6},{6,7},{7,8},{8,9},{9,10},{10,1... | collective-permute-start | bytes 196616 | tf_op jit(solution)/shard_map/ppermute | solution.py:545
  17.5 0.0 collective-permute-start
  17.5 31.4 %all-to-all-done = f32[128,1,4608]{2,1,0:T(1,128)S(1)} async-done(((f32[128,1,4608]{2,1,0:T(1,128)}), f32[128,1,4608]{2,1,0:T(1,128)S(1)}, u32[]{:S(2)}, u32[]{:S(2)}) %all-to-all-start) | async-done | bytes 2359328 | tf_op jit(solution)/shard_map/all_to_all | solution.py:571
  48.9 0.0 copy-start
  48.9 0.0 copy-start.4
  48.9 0.0 copy-start.5
  48.9 0.7 sums.1
  49.6 0.1 collective-permute-start.4
  49.7 1.4 %collective-permute-start.5 = (f32[64,1152]{1,0:T(8,128)S(1)}, f32[64,1152]{1,0:T(8,128)S(1)}, u32[]{:S(2)}, u32[]{:S(2)}) collective-permute-start(f32[64,1152]{1,0:T(8,128)S(1)} %get-tuple-element.29), channel_id=1, source_target_pairs={{32,64},{64,32},{96,0},{0,96},{33,65},{65,33},{97,1},{1,97},{34,66... | collective-permute-start | bytes 884744 | tf_op jit(solution)/shard_map/ppermute | solution.py:602
  51.1 0.0 collective-permute-done.1
  51.1 0.0 collective-permute-done
  51.1 0.0 copy-start.6
  51.1 0.4 weights.1
  51.6 0.3 collective-permute-start.2
  51.9 1.9 %collective-permute-start.3 = (f32[32,1152]{1,0:T(8,128)S(1)}, f32[32,1152]{1,0:T(8,128)S(1)}, u32[]{:S(2)}, u32[]{:S(2)}) collective-permute-start(f32[32,1152]{1,0:T(8,128)S(1)} %get-tuple-element.26), channel_id=1, source_target_pairs={{32,64},{64,32},{96,0},{0,96},{33,65},{65,33},{97,1},{1,97},{34,66... | collective-permute-start | bytes 442376 | tf_op jit(solution)/shard_map/ppermute | solution.py:603
  53.8 0.0 copy-done
  53.8 0.0 copy-done.4
  53.8 0.0 copy-done.5
  53.8 1.4 %early.1 = (f32[128,1152]{1,0:T(8,128)S(1)}, f32[64,1152]{1,0:T(8,128)S(1)}, f32[128,1024]{1,0:T(8,128)S(1)}, f32[128,1024]{1,0:T(8,128)S(1)}, f32[16,128]{1,0:T(8,128)S(1)}) custom-call(f32[128,1152]{1,0:T(8,128)S(1)} %get-tuple-element.27.s_ref, f32[128,1152]{1,0:T(8,128)S(1)} %get-tuple-element.30.w_ref, bf16[384,128]{1,0:T(8,128)(2,1)S(1)} %copy-done.5, ...), custom_call_target="tpu_custom_call" | custom-call | flops 849346560 | bytes 1998848 | tf_op jit(solution)/shard_map/early/pallas_call | solution.py:516
  55.2 0.0 copy-start.2
  55.2 1.3 %collective-permute-done.4.near_ref = f32[64,1152]{1,0:T(8,128)S(1)} collective-permute-done((f32[64,1152]{1,0:T(8,128)S(1)}, f32[64,1152]{1,0:T(8,128)S(1)}, u32[]{:S(2)}, u32[]{:S(2)}) %collective-permute-start.4) | collective-permute-done | bytes 294944 | tf_op jit(solution)/shard_map/ppermute | solution.py:602
  56.5 1.0 %collective-permute-done.5.next_ref = f32[64,1152]{1,0:T(8,128)S(1)} collective-permute-done((f32[64,1152]{1,0:T(8,128)S(1)}, f32[64,1152]{1,0:T(8,128)S(1)}, u32[]{:S(2)}, u32[]{:S(2)}) %collective-permute-start.5) | collective-permute-done | bytes 294944 | tf_op jit(solution)/shard_map/ppermute | solution.py:602
  57.5 0.0 copy-done.6
  57.5 1.6 %first.1 = (f32[192,1152]{1,0:T(8,128)S(1)}, f32[16,128]{1,0:T(8,128)S(1)}) custom-call(f32[128,1152]{1,0:T(8,128)S(1)} %get-tuple-element.27.s_ref, f32[64,1152]{1,0:T(8,128)S(1)} %collective-permute-done.4.near_ref, f32[64,1152]{1,0:T(8,128)S(1)} %collective-permute-done.5.next_ref, f32[128,1152]{1,0:T(8,128)S(1)} %get-tuple-element.31.part_ref, ...), custom_call_target="tpu_custom_call" | custom-call | flops 1132462080 | bytes 2859008 | tf_op jit(solution)/shard_map/first/pallas_call | solution.py:516
  59.1 0.0 copy-start.3
  59.1 0.0 copy-done.2
  59.1 1.2 %second.1 = (f32[128,1024]{1,0:T(8,128)S(1)}, f32[64,1024]{1,0:T(8,128)S(1)}, f32[128,1152]{1,0:T(8,128)S(1)}, f32[24,128]{1,0:T(8,128)S(1)}) custom-call(f32[128,1152]{1,0:T(8,128)S(1)} %get-tuple-element.30.w_ref, f32[192,1152]{1,0:T(8,128)S(1)} %get-tuple-element.34.y0_ref, f32[128,1024]{1,0:T(8,128)S(1)} %get-tuple-element.35.root_ref, ...), custom_call_target="tpu_custom_call" | custom-call | flops 566231040 | bytes 3121152 | tf_op jit(solution)/shard_map/second/pallas_call | solution.py:516
  60.3 0.0 collective-permute-done.2.near_ref
  60.3 0.4 collective-permute-done.3.next_ref
  60.7 0.0 copy-done.3
  60.7 0.9 %third.1 = (f32[128,1024]{1,0:T(8,128)S(1)}, f32[128,128]{1,0:T(8,128)S(1)}) custom-call(f32[32,1152]{1,0:T(8,128)S(1)} %collective-permute-done.2.near_ref, f32[32,1152]{1,0:T(8,128)S(1)} %collective-permute-done.3.next_ref, f32[192,1152]{1,0:T(8,128)S(1)} %get-tuple-element.34.y0_ref, f32[128,1024]{1,0:T(8,128)S(1)} %get-tuple-element.35.root_ref, ...), custom_call_target="tpu_custom_call" | custom-call | flops 566231040 | bytes 4157440 | tf_op jit(solution)/shard_map/third/pallas_call | solution.py:516
  61.6 17.2 %all_to_all.10 = f32[128,1,128]{2,1,0:T(1,128)S(1)} all-to-all(f32[128,1,128]{2,1,0:T(1,128)S(1)} %bitcast.13), channel_id=1, replica_groups=mesh['ty'=4,'tx_0'=4,'tx_1'=4,'tx_2'=2] {'ty','tx_0','tx_1','tx_2'}, dimensions={0} | all-to-all | bytes 131072 | tf_op jit(solution)/shard_map/all_to_all | solution.py:682
  78.8 1.4 %combine.1 = (f32[128,1024]{1,0:T(8,128)}, f32[128,1024]{1,0:T(8,128)}) custom-call(f32[128,128]{1,0:T(8,128)S(1)} %bitcast.12, f32[128,1024]{1,0:T(8,128)S(1)} %get-tuple-element.36.r0_ref, f32[128,1024]{1,0:T(8,128)S(1)} %get-tuple-element.38.b0_ref, f32[128,1024]{1,0:T(8,128)S(1)} %get-tuple-element.43.b1_ref), custom_call_target="tpu_custom_call" | custom-call | bytes 1638400 | tf_op jit(solution)/shard_map/combine/pallas_call | solution.py:516
  (3 shorter events, 0.0 us)
Async XLA Ops:
  4.2 11.5 %copy-start.1 = (f32[128,1024]{1,0:T(8,128)S(1)}, f32[128,1024]{1,0:T(8,128)}, u32[]{:S(2)}) copy-start(f32[128,1024]{1,0:T(8,128)} %prior_ref.1) | copy-start | bytes 1572868
  4.3 44.6 %all-to-all-start = ((f32[128,1,4608]{2,1,0:T(1,128)}), f32[128,1,4608]{2,1,0:T(1,128)S(1)}, u32[]{:S(2)}, u32[]{:S(2)}) async-start(f32[128,1,4608]{2,1,0:T(1,128)} %bitcast.14), calls=%async_computation | async-start | bytes 4718592 | tf_op jit(solution)/shard_map/all_to_all | solution.py:571
  15.8 35.3 %collective-permute-start.1 = (f32[128,128]{1,0:T(8,128)S(1)}, f32[128,128]{1,0:T(8,128)S(1)}, u32[]{:S(2)}, u32[]{:S(2)}) collective-permute-start(f32[128,128]{1,0:T(8,128)S(1)} %get-tuple-element.44), channel_id=1, source_target_pairs={{0,1},{1,2},{2,3},{3,4},{4,5},{5,6},{6,7},{7,8},{8,9},{9,10},{10,1... | collective-permute-start | bytes 196616 | tf_op jit(solution)/shard_map/ppermute | solution.py:545
  17.5 33.6 %collective-permute-start = (f32[128,128]{1,0:T(8,128)S(1)}, f32[128,128]{1,0:T(8,128)S(1)}, u32[]{:S(2)}, u32[]{:S(2)}) collective-permute-start(f32[128,128]{1,0:T(8,128)S(1)} %get-tuple-element.45), channel_id=1, source_target_pairs={{0,31},{1,0},{2,1},{3,2},{4,3},{5,4},{6,5},{7,6},{8,7},{9,8},{10,9... | collective-permute-start | bytes 196616 | tf_op jit(solution)/shard_map/ppermute | solution.py:544
  48.9 4.9 %copy-start = (bf16[1024,256]{1,0:T(8,128)(2,1)S(1)}, bf16[1024,256]{1,0:T(8,128)(2,1)}, u32[]{:S(2)}) copy-start(bf16[1024,256]{1,0:T(8,128)(2,1)} %constant.18.clone.col_ref) | copy-start | bytes 1572868
  48.9 4.9 %copy-start.4 = (bf16[768,128]{1,0:T(8,128)(2,1)S(1)}, bf16[768,128]{1,0:T(8,128)(2,1)}, u32[]{:S(2)}) copy-start(bf16[768,128]{1,0:T(8,128)(2,1)} %constant.19.clone.edge_ref) | copy-start | bytes 589828
  48.9 4.9 %copy-start.5 = (bf16[384,128]{1,0:T(8,128)(2,1)S(1)}, bf16[384,128]{1,0:T(8,128)(2,1)}, u32[]{:S(2)}) copy-start(bf16[384,128]{1,0:T(8,128)(2,1)} %constant.20.clone.own_ref) | copy-start | bytes 294916
  49.6 6.9 %collective-permute-start.4 = (f32[64,1152]{1,0:T(8,128)S(1)}, f32[64,1152]{1,0:T(8,128)S(1)}, u32[]{:S(2)}, u32[]{:S(2)}) collective-permute-start(f32[64,1152]{1,0:T(8,128)S(1)} %get-tuple-element.28), channel_id=1, source_target_pairs={{0,32},{32,0},{64,96},{96,64},{1,33},{33,1},{65,97},{97,65},{2,34}... | collective-permute-start | bytes 884744 | tf_op jit(solution)/shard_map/ppermute | solution.py:602
  49.7 7.8 %collective-permute-start.5 = (f32[64,1152]{1,0:T(8,128)S(1)}, f32[64,1152]{1,0:T(8,128)S(1)}, u32[]{:S(2)}, u32[]{:S(2)}) collective-permute-start(f32[64,1152]{1,0:T(8,128)S(1)} %get-tuple-element.29), channel_id=1, source_target_pairs={{32,64},{64,32},{96,0},{0,96},{33,65},{65,33},{97,1},{1,97},{34,66... | collective-permute-start | bytes 884744 | tf_op jit(solution)/shard_map/ppermute | solution.py:602
  51.1 6.4 %copy-start.6 = (bf16[256,128]{1,0:T(8,128)(2,1)S(1)}, bf16[256,128]{1,0:T(8,128)(2,1)}, u32[]{:S(2)}) copy-start(bf16[256,128]{1,0:T(8,128)(2,1)} %constant.21.clone.halo_ref) | copy-start | bytes 196612
  51.6 8.7 %collective-permute-start.2 = (f32[32,1152]{1,0:T(8,128)S(1)}, f32[32,1152]{1,0:T(8,128)S(1)}, u32[]{:S(2)}, u32[]{:S(2)}) collective-permute-start(f32[32,1152]{1,0:T(8,128)S(1)} %get-tuple-element.25), channel_id=1, source_target_pairs={{0,32},{32,0},{64,96},{96,64},{1,33},{33,1},{65,97},{97,65},{2,34}... | collective-permute-start | bytes 442376 | tf_op jit(solution)/shard_map/ppermute | solution.py:603
  51.9 8.8 %collective-permute-start.3 = (f32[32,1152]{1,0:T(8,128)S(1)}, f32[32,1152]{1,0:T(8,128)S(1)}, u32[]{:S(2)}, u32[]{:S(2)}) collective-permute-start(f32[32,1152]{1,0:T(8,128)S(1)} %get-tuple-element.26), channel_id=1, source_target_pairs={{32,64},{64,32},{96,0},{0,96},{33,65},{65,33},{97,1},{1,97},{34,66... | collective-permute-start | bytes 442376 | tf_op jit(solution)/shard_map/ppermute | solution.py:603
  55.2 3.9 %copy-start.2 = (bf16[256,128]{1,0:T(8,128)(2,1)S(1)}, bf16[256,128]{1,0:T(8,128)(2,1)}, u32[]{:S(2)}) copy-start(bf16[256,128]{1,0:T(8,128)(2,1)} %constant.22.clone.own_ref) | copy-start | bytes 196612
  59.1 1.6 %copy-start.3 = (bf16[128,64]{1,0:T(8,128)(2,1)S(1)}, bf16[128,64]{1,0:T(8,128)(2,1)}, u32[]{:S(2)}) copy-start(bf16[128,64]{1,0:T(8,128)(2,1)} %constant.23.clone.halo_ref) | copy-start | bytes 49156

commit v9 on v8

--- a/solution.py
+++ b/solution.py
@@ -336,15 +336,13 @@
     near_ref,
     next_ref,
     part_ref,
-    deep_ref,
     early_ref,
     halo_ref,
     col_ref,
     edge_ref,
-    y0_ref,
+    border_ref,
     sums_ref,
     mid_ref,
-    border_ref,
 ):
     rows, wide = s_ref.shape
     cols = wide - LANES
@@ -353,9 +351,6 @@
         mid_ref[:, at] = part_ref[:, at] + taps_times(halo_ref, halo)
     all_columns(mid_ref[...], border_ref, slice(None), col_ref, edge_ref)
     two = 2 * HALF
-    y0_ref[:two, :] = border_ref[:two, :]
-    y0_ref[two:rows, :] = deep_ref[...]
-    y0_ref[rows:, :] = border_ref[two:, :]
     top = s_ref[:HALF, :cols] * border_ref[HALF:two, :cols]
     bottom = s_ref[rows - HALF :, :cols] * border_ref[two : two + HALF, :cols]
     sums_ref[0:8, :] = early_ref[0:8, :]
@@ -372,100 +367,61 @@
     return jnp.sum(jnp.sum(total, axis=0, keepdims=True), axis=1, keepdims=True)
 
 
-def centred(r0, b0, b1, c):
-    v, q = b0 - c * r0, b1 - c * b0
-    return v * q, v * b0 + r0 * q
-
-
 def second_kernel(
+    n_ty,
     w_ref,
-    y0_ref,
+    near_ref,
+    next_ref,
+    deep_ref,
+    border_ref,
     root_ref,
     r0_ref,
     first_ref,
-    own_ref,
+    row_ref,
     col_ref,
     b0_ref,
-    inner_ref,
-    mid_ref,
-    sums_ref,
-):
-    rows, wide = w_ref.shape
-    cols = wide - LANES
-    tile = slice(HALF, HALF + rows)
-    deep = slice(HALF, rows - HALF)
-    m0, n1 = whole(first_ref[0:8, :]), whole(first_ref[8:16, :])
-    c0 = n1 / jnp.where(m0 > 0.0, m0, 1.0)
-    for at in spans(wide):
-        mid_ref[:, at] = taps_times(own_ref, w_ref[:, at] * y0_ref[tile, at])
-    total_vv = total_rv = total_vq = total_mix = jnp.zeros((8, LANES), F32)
-    for c, y1 in enumerate(along_columns(split3(mid_ref[deep, :]), col_ref)):
-        at = slice(2 * c * LANES, 2 * (c + 1) * LANES)
-        r0 = r0_ref[:, at]
-        b0 = root_ref[:, at] * y0_ref[tile, at]
-        b0_ref[:, at] = b0
-        v = b0 - c0 * r0
-        total_vv += folded(v * v)
-        total_rv += folded(r0 * v)
-        b1 = root_ref[deep, at] * y1
-        inner_ref[:, at] = b1
-        vq, mix = centred(r0[deep], b0[deep], b1, c0)
-        total_vq += folded(vq)
-        total_mix += folded(mix)
-    lane = iota((8, LANES), 1)
-    known = jnp.zeros((8, LANES), F32)
-    for i, value in enumerate((m0, n1, c0, whole(total_vv), whole(total_rv))):
-        known = jnp.where(lane == i, value, known)
-    sums_ref[0:8, :] = known
-    sums_ref[8:16, :] = total_vq
-    sums_ref[16:24, :] = total_mix
-
-
-def third_kernel(
-    n_ty,
-    near_ref,
-    next_ref,
-    y0_ref,
-    root_ref,
-    r0_ref,
-    b0_ref,
-    part_ref,
-    inner_ref,
-    sums_ref,
-    halo_ref,
-    col_ref,
     b1_ref,
     moments_ref,
     mid_ref,
 ):
-    rows, wide = part_ref.shape
-    cols = wide - LANES
-    top, bottom = slice(0, HALF), slice(rows - HALF, rows)
-    b1_ref[HALF : rows - HALF, :] = inner_ref[...]
-    known = sums_ref[0:1, :]
-    lane = iota(known.shape, 1)
-    c0 = jnp.sum(jnp.where(lane == 2, known, 0.0), axis=1, keepdims=True)
-
-    def border(ref, at):
-        return jnp.concatenate([ref[top, at], ref[bottom, at]], axis=0)
-
+    rows, wide = w_ref.shape
+    cols = wide - LANES
+    one, two, three = HALF, 2 * HALF, 3 * HALF
+    m0, n1 = whole(first_ref[0:8, :]), whole(first_ref[8:16, :])
+    c0 = n1 / jnp.where(m0 > 0.0, m0, 1.0)
     for at in spans(wide):
         above, below = from_partners(n_ty, near_ref, next_ref, at)
         z = jnp.concatenate(
-            [above * y0_ref[:HALF, at], below * y0_ref[rows + HALF :, at]], axis=0
+            [
+                above * border_ref[:one, at],
+                w_ref[:one, at] * border_ref[one:two, at],
+                w_ref[one : rows - one, at] * deep_ref[:, at],
+                w_ref[rows - one :, at] * border_ref[two:three, at],
+                below * border_ref[three:, at],
+            ],
+            axis=0,
         )
-        mid_ref[:, at] = border(part_ref, at) + taps_times(halo_ref, z)
-    total_vq, total_mix = sums_ref[8:16, :], sums_ref[16:24, :]
+        mid_ref[:, at] = taps_times(row_ref, z)
+    total_vv = total_rv = total_vq = total_mix = jnp.zeros((8, LANES), F32)
     for c, y1 in enumerate(along_columns(split3(mid_ref[...]), col_ref)):
         at = slice(2 * c * LANES, 2 * (c + 1) * LANES)
-        b1 = border(root_ref, at) * y1
-        b1_ref[top, at] = b1[:HALF]
-        b1_ref[bottom, at] = b1[HALF:]
-        vq, mix = centred(border(r0_ref, at), border(b0_ref, at), b1, c0)
-        total_vq += folded(vq)
-        total_mix += folded(mix)
-    known = jnp.where(lane == 5, whole(total_vq), known)
-    known = jnp.where(lane == 6, whole(total_mix), known)
+        y0 = jnp.concatenate(
+            [border_ref[one:two, at], deep_ref[:, at], border_ref[two:three, at]], axis=0
+        )
+        r0, root = r0_ref[:, at], root_ref[:, at]
+        b0, b1 = root * y0, root * y1
+        b0_ref[:, at] = b0
+        b1_ref[:, at] = b1
+        v, q = b0 - c0 * r0, b1 - c0 * b0
+        total_vv += folded(v * v)
+        total_rv += folded(r0 * v)
+        total_vq += folded(v * q)
+        total_mix += folded(v * b0 + r0 * q)
+    lane = iota((1, LANES), 1)
+    known = jnp.zeros((1, LANES), F32)
+    totals = (whole(x) for x in (total_vv, total_rv, total_vq, total_mix))
+    for i, value in enumerate((m0, n1, c0, *totals)):
+        known = jnp.where(lane == i, value, known)
     moments_ref[...] = jnp.broadcast_to(known, moments_ref.shape)
 
 
@@ -628,56 +584,38 @@
         flops=5 * 2 * tall * wide * 3 * LANES,
         name="early",
     )
-    y0, early = call(
+    border, early = call(
         functools.partial(first_kernel, n_ty),
-        [(tall, wide), (16, LANES)],
+        [(4 * HALF, wide), (16, LANES)],
         s,
         s_near,
         s_next,
         part,
-        deep,
         early,
         first_taps,
         col_taps,
         edge_taps,
-        scratch=[pltpu.VMEM((4 * HALF, wide), F32), pltpu.VMEM((4 * HALF, wide), F32)],
+        scratch=[pltpu.VMEM((4 * HALF, wide), F32)],
         flops=5 * 2 * rows * wide * 6 * LANES,
         name="first",
     )
-    own_taps = taps(inside[:, None] - inside[None, :], 0)
-    border = np.concatenate([inside[:HALF], inside[rows - HALF :]])
-    outside = np.concatenate([np.arange(-HALF, 0), np.arange(rows, rows + HALF)])
-    halo_taps = taps(border[:, None] - outside[None, :], 0)
-    b0, inner, part, sums = call(
-        second_kernel,
-        [tile, (rows - 2 * HALF, cols), (rows, wide), (24, LANES)],
+    second_taps = taps(inside[:, None] - np.arange(-HALF, rows + HALF)[None, :], 0)
+    b0, b1, moments = call(
+        functools.partial(second_kernel, n_ty),
+        [tile, tile, (devices, LANES)],
         w,
-        y0,
+        w_near,
+        w_next,
+        deep,
+        border,
         root,
         r0,
         early,
-        own_taps,
+        second_taps,
         col_taps,
-        flops=5 * 2 * rows * wide * 3 * LANES,
+        scratch=[pltpu.VMEM((rows, wide), F32)],
+        flops=5 * 2 * rows * wide * 6 * LANES,
         name="second",
-    )
-    b1, moments = call(
-        functools.partial(third_kernel, n_ty),
-        [tile, (devices, LANES)],
-        w_near,
-        w_next,
-        y0,
-        root,
-        r0,
-        b0,
-        part,
-        inner,
-        sums,
-        halo_taps,
-        col_taps,
-        scratch=[pltpu.VMEM((2 * HALF, wide), F32)],
-        flops=5 * 2 * rows * wide * 3 * LANES,
-        name="third",
     )
     moments = lax.all_to_all(
         moments.reshape(devices, 1, LANES), TY_TX, split_axis=0, concat_axis=0, tiled=True

time: 80.4 us -> 79.9 us (level)
  blocking collectives: 17.2 us -> 16.1 us
  waiting for transfers between devices: 34.1 us -> 35.1 us
    all_to_all x1, blocking collectives: 17.2 us -> 16.1 us  [shards(): lax.all_to_all(moments.reshape(devices, 1, LANES), TY_TX, split_axis=0, c...]
    ppermute x1, starting transfers between devices: 0.01 us -> 1.14 us  [shards(): prior_right = lax.ppermute(prior_weight[:, :LANES], TX, neighbours(TX, -1))]
    ppermute x1, starting transfers between devices: 1.7 us -> 0.68 us  [shards(): lax.ppermute(prior_weight[:, cols - LANES:], TX, neighbours(TX, 1))]
    pallas_call x8 -> x7, Pallas kernels: 11.3 us -> 10.8 us  [call(): pl.pallas_call(kernel, out_shape=[jax.ShapeDtypeStruct(s, F32) if isinsta...]
  transfers between devices with their start and end apart: 7 -> 7, of which waited for: 4 -> 5; matrix products, arithmetic and copies ran while one was open for 0% -> 0% of each run, Pallas kernels for 7% -> 5%
where the time goes in v9:
time: 79.9 us; the launch traced here: 79.7 us
  waiting for transfers between devices  35.1 us (44%)
  starting transfers between devices  17 us (21%)
  blocking collectives  16.1 us (20%)
  Pallas kernels  10.8 us (14%)
    all_to_all x1, waiting for transfers between devices, shards(): lax.all_to_all(message.reshape(devices, 1, length * LANES), TY_TX, split_...  31.2 us
    all_to_all x1, blocking collectives, shards(): lax.all_to_all(moments.reshape(devices, 1, LANES), TY_TX, split_axis=0, c...  16.1 us
    all_to_all x1, starting transfers between devices, shards(): lax.all_to_all(message.reshape(devices, 1, length * LANES), TY_TX, split_...  11.5 us
    pallas_call x7, Pallas kernels, call(): pl.pallas_call(kernel, out_shape=[jax.ShapeDtypeStruct(s, F32) if isinsta...  10.8 us
    ppermute x1, starting transfers between devices, shards(): lax.ppermute(w_next, 'ty', far)  1.87 us
  transfers between devices with their start and end apart: 7, of which 5 were waited for; matrix products, arithmetic and copies ran while one was open for 0% of the time, Pallas kernels for 5%

profile of v9, /device:TPU:1, one launch (start us, length us, event | category | flops | bytes accessed | tf_op | source)
XLA Modules:
  0.0 79.7 jit_solution(9348679895663625579)
XLA Ops:
  0.6 3.6 %pack.1 = f32[4608,128]{1,0:T(8,128)} custom-call(s32[1,128]{1,0:T(1,128)} %bitcast.17, s32[1,128]{1,0:T(1,128)} %bitcast.18, f32[1024,128]{1,0:T(8,128)} %bitcast.15, f32[1024,128]{1,0:T(8,128)} %bitcast.16), custom_call_target="tpu_custom_call" | custom-call | bytes 1049600 | tf_op jit(solution)/shard_map/pack/pallas_call | solution.py:472
  4.2 0.0 copy-start
  4.2 11.5 %all-to-all-start = ((f32[128,1,4608]{2,1,0:T(1,128)}), f32[128,1,4608]{2,1,0:T(1,128)S(1)}, u32[]{:S(2)}, u32[]{:S(2)}) async-start(f32[128,1,4608]{2,1,0:T(1,128)} %bitcast.14), calls=%async_computation | async-start | bytes 4718592 | tf_op jit(solution)/shard_map/all_to_all | solution.py:527
  15.7 0.0 copy-done
  15.8 1.1 %collective-permute-start = (f32[128,128]{1,0:T(8,128)S(1)}, f32[128,128]{1,0:T(8,128)S(1)}, u32[]{:S(2)}, u32[]{:S(2)}) collective-permute-start(f32[128,128]{1,0:T(8,128)S(1)} %get-tuple-element.39), channel_id=1, source_target_pairs={{0,31},{1,0},{2,1},{3,2},{4,3},{5,4},{6,5},{7,6},{8,7},{9,8},{10,9... | collective-permute-start | bytes 196616 | tf_op jit(solution)/shard_map/ppermute | solution.py:500
  16.9 0.7 collective-permute-start.1
  17.6 31.2 %all-to-all-done = f32[128,1,4608]{2,1,0:T(1,128)S(1)} async-done(((f32[128,1,4608]{2,1,0:T(1,128)}), f32[128,1,4608]{2,1,0:T(1,128)S(1)}, u32[]{:S(2)}, u32[]{:S(2)}) %all-to-all-start) | async-done | bytes 2359328 | tf_op jit(solution)/shard_map/all_to_all | solution.py:527
  48.8 0.0 copy-start.1
  48.8 0.0 copy-start.2
  48.8 0.0 copy-start.4
  48.9 0.7 sums.1
  49.6 0.1 collective-permute-start.4
  49.6 1.4 %collective-permute-start.5 = (f32[64,1152]{1,0:T(8,128)S(1)}, f32[64,1152]{1,0:T(8,128)S(1)}, u32[]{:S(2)}, u32[]{:S(2)}) collective-permute-start(f32[64,1152]{1,0:T(8,128)S(1)} %get-tuple-element.28), channel_id=1, source_target_pairs={{32,64},{64,32},{96,0},{0,96},{33,65},{65,33},{97,1},{1,97},{34,66... | collective-permute-start | bytes 884744 | tf_op jit(solution)/shard_map/ppermute | solution.py:558
  51.1 0.0 collective-permute-done
  51.1 0.0 collective-permute-done.1
  51.1 0.0 copy-start.5
  51.1 0.4 weights.1
  51.6 0.3 collective-permute-start.2
  51.9 1.9 %collective-permute-start.3 = (f32[32,1152]{1,0:T(8,128)S(1)}, f32[32,1152]{1,0:T(8,128)S(1)}, u32[]{:S(2)}, u32[]{:S(2)}) collective-permute-start(f32[32,1152]{1,0:T(8,128)S(1)} %get-tuple-element.24), channel_id=1, source_target_pairs={{32,64},{64,32},{96,0},{0,96},{33,65},{65,33},{97,1},{1,97},{34,66... | collective-permute-start | bytes 442376 | tf_op jit(solution)/shard_map/ppermute | solution.py:559
  53.7 0.0 copy-done.1
  53.7 0.0 copy-done.2
  53.7 0.0 copy-done.4
  53.7 1.4 %early.1 = (f32[128,1152]{1,0:T(8,128)S(1)}, f32[64,1152]{1,0:T(8,128)S(1)}, f32[128,1024]{1,0:T(8,128)S(1)}, f32[128,1024]{1,0:T(8,128)S(1)}, f32[16,128]{1,0:T(8,128)S(1)}) custom-call(f32[128,1152]{1,0:T(8,128)S(1)} %get-tuple-element.25.s_ref, f32[128,1152]{1,0:T(8,128)S(1)} %get-tuple-element.22.w_ref, bf16[384,128]{1,0:T(8,128)(2,1)S(1)} %copy-done.4, ...), custom_call_target="tpu_custom_call" | custom-call | flops 849346560 | bytes 1998848 | tf_op jit(solution)/shard_map/early/pallas_call | solution.py:472
  55.2 0.0 copy-start.3
  55.2 1.3 %collective-permute-done.4.near_ref = f32[64,1152]{1,0:T(8,128)S(1)} collective-permute-done((f32[64,1152]{1,0:T(8,128)S(1)}, f32[64,1152]{1,0:T(8,128)S(1)}, u32[]{:S(2)}, u32[]{:S(2)}) %collective-permute-start.4) | collective-permute-done | bytes 294944 | tf_op jit(solution)/shard_map/ppermute | solution.py:558
  56.5 1.0 %collective-permute-done.5.next_ref = f32[64,1152]{1,0:T(8,128)S(1)} collective-permute-done((f32[64,1152]{1,0:T(8,128)S(1)}, f32[64,1152]{1,0:T(8,128)S(1)}, u32[]{:S(2)}, u32[]{:S(2)}) %collective-permute-start.5) | collective-permute-done | bytes 294944 | tf_op jit(solution)/shard_map/ppermute | solution.py:558
  57.5 0.0 copy-done.5
  57.5 1.6 %first.1 = (f32[128,1152]{1,0:T(8,128)S(1)}, f32[16,128]{1,0:T(8,128)S(1)}) custom-call(f32[128,1152]{1,0:T(8,128)S(1)} %get-tuple-element.25.s_ref, f32[64,1152]{1,0:T(8,128)S(1)} %collective-permute-done.4.near_ref, f32[64,1152]{1,0:T(8,128)S(1)} %collective-permute-done.5.next_ref, f32[128,1152]{1,0:T(8,128)S(1)} %get-tuple-element.29.part_ref, ...), custom_call_target="tpu_custom_call" | custom-call | flops 1132462080 | bytes 2564096 | tf_op jit(solution)/shard_map/first/pallas_call | solution.py:472
  59.1 0.6 collective-permute-done.2.near_ref
  59.7 1.0 %collective-permute-done.3.next_ref = f32[32,1152]{1,0:T(8,128)S(1)} collective-permute-done((f32[32,1152]{1,0:T(8,128)S(1)}, f32[32,1152]{1,0:T(8,128)S(1)}, u32[]{:S(2)}, u32[]{:S(2)}) %collective-permute-start.3) | collective-permute-done | bytes 147488 | tf_op jit(solution)/shard_map/ppermute | solution.py:559
  60.6 0.0 copy-done.3
  60.6 1.6 %second.1 = (f32[128,1024]{1,0:T(8,128)S(1)}, f32[128,1024]{1,0:T(8,128)S(1)}, f32[128,128]{1,0:T(8,128)S(1)}) custom-call(f32[128,1152]{1,0:T(8,128)S(1)} %get-tuple-element.22.w_ref, f32[32,1152]{1,0:T(8,128)S(1)} %collective-permute-done.2.near_ref, f32[32,1152]{1,0:T(8,128)S(1)} %collective-permute-done.3.next_ref, ...), custom_call_target="tpu_custom_call" | custom-call | flops 1132462080 | bytes 3448832 | tf_op jit(solution)/shard_map/second/pallas_call | solution.py:472
  62.3 16.1 %all_to_all.10 = f32[128,1,128]{2,1,0:T(1,128)S(1)} all-to-all(f32[128,1,128]{2,1,0:T(1,128)S(1)} %bitcast.13), channel_id=1, replica_groups=mesh['ty'=4,'tx_0'=4,'tx_1'=4,'tx_2'=2] {'ty','tx_0','tx_1','tx_2'}, dimensions={0} | all-to-all | bytes 131072 | tf_op jit(solution)/shard_map/all_to_all | solution.py:620
  78.3 1.4 %combine.1 = (f32[128,1024]{1,0:T(8,128)}, f32[128,1024]{1,0:T(8,128)}) custom-call(f32[128,128]{1,0:T(8,128)S(1)} %bitcast.12, f32[128,1024]{1,0:T(8,128)S(1)} %get-tuple-element.33.r0_ref, f32[128,1024]{1,0:T(8,128)S(1)} %get-tuple-element.36.b0_ref, f32[128,1024]{1,0:T(8,128)S(1)} %get-tuple-element.37.b1_ref), custom_call_target="tpu_custom_call" | custom-call | bytes 1638400 | tf_op jit(solution)/shard_map/combine/pallas_call | solution.py:472
  (3 shorter events, 0.0 us)
Async XLA Ops:
  4.2 11.5 %copy-start = (f32[128,1024]{1,0:T(8,128)S(1)}, f32[128,1024]{1,0:T(8,128)}, u32[]{:S(2)}) copy-start(f32[128,1024]{1,0:T(8,128)} %prior_ref.1) | copy-start | bytes 1572868
  4.2 44.6 %all-to-all-start = ((f32[128,1,4608]{2,1,0:T(1,128)}), f32[128,1,4608]{2,1,0:T(1,128)S(1)}, u32[]{:S(2)}, u32[]{:S(2)}) async-start(f32[128,1,4608]{2,1,0:T(1,128)} %bitcast.14), calls=%async_computation | async-start | bytes 4718592 | tf_op jit(solution)/shard_map/all_to_all | solution.py:527
  15.8 35.3 %collective-permute-start = (f32[128,128]{1,0:T(8,128)S(1)}, f32[128,128]{1,0:T(8,128)S(1)}, u32[]{:S(2)}, u32[]{:S(2)}) collective-permute-start(f32[128,128]{1,0:T(8,128)S(1)} %get-tuple-element.39), channel_id=1, source_target_pairs={{0,31},{1,0},{2,1},{3,2},{4,3},{5,4},{6,5},{7,6},{8,7},{9,8},{10,9... | collective-permute-start | bytes 196616 | tf_op jit(solution)/shard_map/ppermute | solution.py:500
  16.9 34.2 %collective-permute-start.1 = (f32[128,128]{1,0:T(8,128)S(1)}, f32[128,128]{1,0:T(8,128)S(1)}, u32[]{:S(2)}, u32[]{:S(2)}) collective-permute-start(f32[128,128]{1,0:T(8,128)S(1)} %get-tuple-element.38), channel_id=1, source_target_pairs={{0,1},{1,2},{2,3},{3,4},{4,5},{5,6},{6,7},{7,8},{8,9},{9,10},{10,1... | collective-permute-start | bytes 196616 | tf_op jit(solution)/shard_map/ppermute | solution.py:501
  48.8 4.9 %copy-start.1 = (bf16[1024,256]{1,0:T(8,128)(2,1)S(1)}, bf16[1024,256]{1,0:T(8,128)(2,1)}, u32[]{:S(2)}) copy-start(bf16[1024,256]{1,0:T(8,128)(2,1)} %constant.16.clone.col_ref) | copy-start | bytes 1572868
  48.8 4.9 %copy-start.2 = (bf16[768,128]{1,0:T(8,128)(2,1)S(1)}, bf16[768,128]{1,0:T(8,128)(2,1)}, u32[]{:S(2)}) copy-start(bf16[768,128]{1,0:T(8,128)(2,1)} %constant.17.clone.edge_ref) | copy-start | bytes 589828
  48.8 4.9 %copy-start.4 = (bf16[384,128]{1,0:T(8,128)(2,1)S(1)}, bf16[384,128]{1,0:T(8,128)(2,1)}, u32[]{:S(2)}) copy-start(bf16[384,128]{1,0:T(8,128)(2,1)} %constant.18.clone.own_ref) | copy-start | bytes 294916
  49.6 6.9 %collective-permute-start.4 = (f32[64,1152]{1,0:T(8,128)S(1)}, f32[64,1152]{1,0:T(8,128)S(1)}, u32[]{:S(2)}, u32[]{:S(2)}) collective-permute-start(f32[64,1152]{1,0:T(8,128)S(1)} %get-tuple-element.27), channel_id=1, source_target_pairs={{0,32},{32,0},{64,96},{96,64},{1,33},{33,1},{65,97},{97,65},{2,34}... | collective-permute-start | bytes 884744 | tf_op jit(solution)/shard_map/ppermute | solution.py:558
  49.6 7.8 %collective-permute-start.5 = (f32[64,1152]{1,0:T(8,128)S(1)}, f32[64,1152]{1,0:T(8,128)S(1)}, u32[]{:S(2)}, u32[]{:S(2)}) collective-permute-start(f32[64,1152]{1,0:T(8,128)S(1)} %get-tuple-element.28), channel_id=1, source_target_pairs={{32,64},{64,32},{96,0},{0,96},{33,65},{65,33},{97,1},{1,97},{34,66... | collective-permute-start | bytes 884744 | tf_op jit(solution)/shard_map/ppermute | solution.py:558
  51.1 6.4 %copy-start.5 = (bf16[256,128]{1,0:T(8,128)(2,1)S(1)}, bf16[256,128]{1,0:T(8,128)(2,1)}, u32[]{:S(2)}) copy-start(bf16[256,128]{1,0:T(8,128)(2,1)} %constant.19.clone.halo_ref) | copy-start | bytes 196612
  51.6 8.1 %collective-permute-start.2 = (f32[32,1152]{1,0:T(8,128)S(1)}, f32[32,1152]{1,0:T(8,128)S(1)}, u32[]{:S(2)}, u32[]{:S(2)}) collective-permute-start(f32[32,1152]{1,0:T(8,128)S(1)} %get-tuple-element.23), channel_id=1, source_target_pairs={{0,32},{32,0},{64,96},{96,64},{1,33},{33,1},{65,97},{97,65},{2,34}... | collective-permute-start | bytes 442376 | tf_op jit(solution)/shard_map/ppermute | solution.py:559
  51.9 8.8 %collective-permute-start.3 = (f32[32,1152]{1,0:T(8,128)S(1)}, f32[32,1152]{1,0:T(8,128)S(1)}, u32[]{:S(2)}, u32[]{:S(2)}) collective-permute-start(f32[32,1152]{1,0:T(8,128)S(1)} %get-tuple-element.24), channel_id=1, source_target_pairs={{32,64},{64,32},{96,0},{0,96},{33,65},{65,33},{97,1},{1,97},{34,66... | collective-permute-start | bytes 442376 | tf_op jit(solution)/shard_map/ppermute | solution.py:559
  55.2 5.5 %copy-start.3 = (bf16[256,192]{1,0:T(8,128)(2,1)S(1)}, bf16[256,192]{1,0:T(8,128)(2,1)}, u32[]{:S(2)}) copy-start(bf16[256,192]{1,0:T(8,128)(2,1)} %constant.20.clone.row_ref) | copy-start | bytes 294916

commit v10 on v9

--- a/solution.py
+++ b/solution.py
@@ -246,7 +246,7 @@
 
 def weights_kernel(
     parts, length, n_tx, got_ref, prior_ref, prior_halo_ref, select_ref, strip_ref,
-    w_ref, near_ref, next_ref
+    w_ref
 ):
     rows, wide = w_ref.shape
     cols = wide - LANES
@@ -262,7 +262,6 @@
         prior_halo * has_right + strip,
         jnp.where(lane >= LANES - HALF, prior_halo * has_left + strip, 0.0),
     )
-    to_partners(w_ref, near_ref, next_ref)
 
 
 def along_columns(pieces, taps_ref):
@@ -305,11 +304,14 @@
     root_ref,
     r0_ref,
     sums_ref,
+    near_ref,
+    next_ref,
     mid_ref,
 ):
     rows, wide = s_ref.shape
     cols = wide - LANES
     edge = 4 * HALF
+    to_partners(w_ref, near_ref, next_ref)
     for at in spans(wide):
         mid = taps_times(own_ref, s_ref[:, at])
         part_ref[:, at] = mid[:edge]
@@ -541,9 +543,9 @@
         flops=3 * 2 * rows * wide * SLOTS * devices,
         name="sums",
     )
-    w, w_near, w_next = call(
+    (w,) = call(
         functools.partial(weights_kernel, parts, length, n_tx),
-        [(rows, wide), w_slab, w_slab],
+        [(rows, wide)],
         got,
         prior_weight,
         prior_halo,
@@ -553,10 +555,9 @@
         name="weights",
     )
     n_ty = lax.axis_size("ty")
-    near = [(i, i ^ 1) for i in range(n_ty)]
+    swaps = [(i, i ^ 1) for i in range(n_ty)]
     far = [((i + 1) % n_ty, ((i ^ 1) + 1) % n_ty) for i in range(n_ty)]
-    s_near, s_next = lax.ppermute(s_near, "ty", near), lax.ppermute(s_next, "ty", far)
-    w_near, w_next = lax.ppermute(w_near, "ty", near), lax.ppermute(w_next, "ty", far)
+    s_near, s_next = lax.ppermute(s_near, "ty", swaps), lax.ppermute(s_next, "ty", far)
 
     tall = rows + 2 * HALF
     col_taps = taps(np.arange(2 * LANES)[None, :] - np.arange(4 * LANES)[:, None] + LANES, 0)
@@ -572,9 +573,9 @@
     far_rows = np.concatenate([np.arange(-2 * HALF, 0), np.arange(rows, rows + 2 * HALF)])
     early_taps = taps(early_rows[:, None] - inside[None, :], 0)
     first_taps = taps(border_rows[:, None] - far_rows[None, :], 0)
-    part, deep, root, r0, early = call(
+    part, deep, root, r0, early, w_near, w_next = call(
         early_kernel,
-        [(4 * HALF, wide), (rows - 2 * HALF, wide), tile, tile, (16, LANES)],
+        [(4 * HALF, wide), (rows - 2 * HALF, wide), tile, tile, (16, LANES), w_slab, w_slab],
         s,
         w,
         early_taps,
@@ -584,6 +585,7 @@
         flops=5 * 2 * tall * wide * 3 * LANES,
         name="early",
     )
+    w_near, w_next = lax.ppermute(w_near, "ty", swaps), lax.ppermute(w_next, "ty", far)
     border, early = call(
         functools.partial(first_kernel, n_ty),
         [(4 * HALF, wide), (16, LANES)],

time: 79.9 us -> 80 us (level)
  no operation moved by 1% of the time
where the time goes in v10:
time: 80 us; the launch traced here: 79.8 us
  waiting for transfers between devices  35.1 us (44%)
  starting transfers between devices  17 us (21%)
  blocking collectives  16.1 us (20%)
  Pallas kernels  10.8 us (14%)
    all_to_all x1, waiting for transfers between devices, shards(): lax.all_to_all(message.reshape(devices, 1, length * LANES), TY_TX, split_...  31.2 us
    all_to_all x1, blocking collectives, shards(): lax.all_to_all(moments.reshape(devices, 1, LANES), TY_TX, split_axis=0, c...  16.1 us
    all_to_all x1, starting transfers between devices, shards(): lax.all_to_all(message.reshape(devices, 1, length * LANES), TY_TX, split_...  11.5 us
    pallas_call x7, Pallas kernels, call(): pl.pallas_call(kernel, out_shape=[jax.ShapeDtypeStruct(s, F32) if isinsta...  10.8 us
    ppermute x1, starting transfers between devices, shards(): lax.ppermute(w_next, 'ty', far)  1.88 us
  transfers between devices with their start and end apart: 7, of which 5 were waited for; matrix products, arithmetic and copies ran while one was open for 0% of the time, Pallas kernels for 5%

profile of v10, /device:TPU:1, one launch (start us, length us, event | category | flops | bytes accessed | tf_op | source)
XLA Modules:
  0.0 79.8 jit_solution(12813698240082750542)
XLA Ops:
  0.6 3.6 %pack.1 = f32[4608,128]{1,0:T(8,128)} custom-call(s32[1,128]{1,0:T(1,128)} %bitcast.17, s32[1,128]{1,0:T(1,128)} %bitcast.18, f32[1024,128]{1,0:T(8,128)} %bitcast.15, f32[1024,128]{1,0:T(8,128)} %bitcast.16), custom_call_target="tpu_custom_call" | custom-call | bytes 1049600 | tf_op jit(solution)/shard_map/pack/pallas_call | solution.py:474
  4.2 0.0 copy-start
  4.2 11.5 %all-to-all-start = ((f32[128,1,4608]{2,1,0:T(1,128)}), f32[128,1,4608]{2,1,0:T(1,128)S(1)}, u32[]{:S(2)}, u32[]{:S(2)}) async-start(f32[128,1,4608]{2,1,0:T(1,128)} %bitcast.14), calls=%async_computation | async-start | bytes 4718592 | tf_op jit(solution)/shard_map/all_to_all | solution.py:529
  15.8 0.0 copy-done
  15.8 1.1 %collective-permute-start = (f32[128,128]{1,0:T(8,128)S(1)}, f32[128,128]{1,0:T(8,128)S(1)}, u32[]{:S(2)}, u32[]{:S(2)}) collective-permute-start(f32[128,128]{1,0:T(8,128)S(1)} %get-tuple-element.37), channel_id=1, source_target_pairs={{0,31},{1,0},{2,1},{3,2},{4,3},{5,4},{6,5},{7,6},{8,7},{9,8},{10,9... | collective-permute-start | bytes 196616 | tf_op jit(solution)/shard_map/ppermute | solution.py:502
  16.9 0.7 collective-permute-start.1
  17.6 31.2 %all-to-all-done = f32[128,1,4608]{2,1,0:T(1,128)S(1)} async-done(((f32[128,1,4608]{2,1,0:T(1,128)}), f32[128,1,4608]{2,1,0:T(1,128)S(1)}, u32[]{:S(2)}, u32[]{:S(2)}) %all-to-all-start) | async-done | bytes 2359328 | tf_op jit(solution)/shard_map/all_to_all | solution.py:529
  48.8 0.7 sums.1
  49.6 0.0 copy-start.1
  49.6 0.0 copy-start.2
  49.6 0.0 copy-start.4
  49.6 0.1 collective-permute-start.4
  49.7 1.4 %collective-permute-start.5 = (f32[64,1152]{1,0:T(8,128)S(1)}, f32[64,1152]{1,0:T(8,128)S(1)}, u32[]{:S(2)}, u32[]{:S(2)}) collective-permute-start(f32[64,1152]{1,0:T(8,128)S(1)} %get-tuple-element.26), channel_id=1, source_target_pairs={{32,64},{64,32},{96,0},{0,96},{33,65},{65,33},{97,1},{1,97},{34,66... | collective-permute-start | bytes 884744 | tf_op jit(solution)/shard_map/ppermute | solution.py:560
  51.1 0.0 collective-permute-done
  51.1 0.0 collective-permute-done.1
  51.1 0.4 weights.1.w_ref
  51.6 0.0 copy-start.5
  51.6 0.0 copy-done.1
  51.6 0.0 copy-done.2
  51.6 0.0 copy-done.4
  51.6 1.4 %early.1 = (f32[128,1152]{1,0:T(8,128)S(1)}, f32[64,1152]{1,0:T(8,128)S(1)}, f32[128,1024]{1,0:T(8,128)S(1)}, f32[128,1024]{1,0:T(8,128)S(1)}, f32[16,128]{1,0:T...) custom-call(f32[128,1152]{1,0:T(8,128)S(1)} %get-tuple-element.21.s_ref, f32[128,1152]{1,0:T(8,128)S(1)} %weights.1.w_ref, ...), custom_call_target="tpu_custom_call" | custom-call | flops 849346560 | bytes 1998848 | tf_op jit(solution)/shard_map/early/pallas_call | solution.py:474
  53.0 0.0 copy-start.3
  53.0 0.3 collective-permute-start.2
  53.3 1.9 %collective-permute-start.3 = (f32[32,1152]{1,0:T(8,128)S(1)}, f32[32,1152]{1,0:T(8,128)S(1)}, u32[]{:S(2)}, u32[]{:S(2)}) collective-permute-start(f32[32,1152]{1,0:T(8,128)S(1)} %get-tuple-element.23), channel_id=1, source_target_pairs={{32,64},{64,32},{96,0},{0,96},{33,65},{65,33},{97,1},{1,97},{34,66... | collective-permute-start | bytes 442376 | tf_op jit(solution)/shard_map/ppermute | solution.py:588
  55.2 1.3 %collective-permute-done.4.near_ref = f32[64,1152]{1,0:T(8,128)S(1)} collective-permute-done((f32[64,1152]{1,0:T(8,128)S(1)}, f32[64,1152]{1,0:T(8,128)S(1)}, u32[]{:S(2)}, u32[]{:S(2)}) %collective-permute-start.4) | collective-permute-done | bytes 294944 | tf_op jit(solution)/shard_map/ppermute | solution.py:560
  56.5 1.0 %collective-permute-done.5.next_ref = f32[64,1152]{1,0:T(8,128)S(1)} collective-permute-done((f32[64,1152]{1,0:T(8,128)S(1)}, f32[64,1152]{1,0:T(8,128)S(1)}, u32[]{:S(2)}, u32[]{:S(2)}) %collective-permute-start.5) | collective-permute-done | bytes 294944 | tf_op jit(solution)/shard_map/ppermute | solution.py:560
  57.5 0.0 copy-done.5
  57.5 1.6 %first.1 = (f32[128,1152]{1,0:T(8,128)S(1)}, f32[16,128]{1,0:T(8,128)S(1)}) custom-call(f32[128,1152]{1,0:T(8,128)S(1)} %get-tuple-element.21.s_ref, f32[64,1152]{1,0:T(8,128)S(1)} %collective-permute-done.4.near_ref, f32[64,1152]{1,0:T(8,128)S(1)} %collective-permute-done.5.next_ref, f32[128,1152]{1,0:T(8,128)S(1)} %get-tuple-element.27.part_ref, ...), custom_call_target="tpu_custom_call" | custom-call | flops 1132462080 | bytes 2564096 | tf_op jit(solution)/shard_map/first/pallas_call | solution.py:474
  59.1 0.6 collective-permute-done.2.near_ref
  59.7 1.0 %collective-permute-done.3.next_ref = f32[32,1152]{1,0:T(8,128)S(1)} collective-permute-done((f32[32,1152]{1,0:T(8,128)S(1)}, f32[32,1152]{1,0:T(8,128)S(1)}, u32[]{:S(2)}, u32[]{:S(2)}) %collective-permute-start.3) | collective-permute-done | bytes 147488 | tf_op jit(solution)/shard_map/ppermute | solution.py:588
  60.7 0.0 copy-done.3
  60.7 1.7 %second.1 = (f32[128,1024]{1,0:T(8,128)S(1)}, f32[128,1024]{1,0:T(8,128)S(1)}, f32[128,128]{1,0:T(8,128)S(1)}) custom-call(f32[128,1152]{1,0:T(8,128)S(1)} %weights.1.w_ref, f32[32,1152]{1,0:T(8,128)S(1)} %collective-permute-done.2.near_ref, f32[32,1152]{1,0:T(8,128)S(1)} %collective-permute-done.3.next_ref, f32[64,1152]{1,0:T(8,128)S(1)} %get-tuple-element.24.deep_ref, ...), custom_call_target="tpu_custom_call" | custom-call | flops 1132462080 | bytes 3448832 | tf_op jit(solution)/shard_map/second/pallas_call | solution.py:474
  62.3 16.1 %all_to_all.10 = f32[128,1,128]{2,1,0:T(1,128)S(1)} all-to-all(f32[128,1,128]{2,1,0:T(1,128)S(1)} %bitcast.13), channel_id=1, replica_groups=mesh['ty'=4,'tx_0'=4,'tx_1'=4,'tx_2'=2] {'ty','tx_0','tx_1','tx_2'}, dimensions={0} | all-to-all | bytes 131072 | tf_op jit(solution)/shard_map/all_to_all | solution.py:622
  78.4 1.4 %combine.1 = (f32[128,1024]{1,0:T(8,128)}, f32[128,1024]{1,0:T(8,128)}) custom-call(f32[128,128]{1,0:T(8,128)S(1)} %bitcast.12, f32[128,1024]{1,0:T(8,128)S(1)} %get-tuple-element.31.r0_ref, f32[128,1024]{1,0:T(8,128)S(1)} %get-tuple-element.34.b0_ref, f32[128,1024]{1,0:T(8,128)S(1)} %get-tuple-element.35.b1_ref), custom_call_target="tpu_custom_call" | custom-call | bytes 1638400 | tf_op jit(solution)/shard_map/combine/pallas_call | solution.py:474
  (3 shorter events, 0.0 us)
Async XLA Ops:
  4.2 11.5 %copy-start = (f32[128,1024]{1,0:T(8,128)S(1)}, f32[128,1024]{1,0:T(8,128)}, u32[]{:S(2)}) copy-start(f32[128,1024]{1,0:T(8,128)} %prior_ref.1) | copy-start | bytes 1572868
  4.2 44.6 %all-to-all-start = ((f32[128,1,4608]{2,1,0:T(1,128)}), f32[128,1,4608]{2,1,0:T(1,128)S(1)}, u32[]{:S(2)}, u32[]{:S(2)}) async-start(f32[128,1,4608]{2,1,0:T(1,128)} %bitcast.14), calls=%async_computation | async-start | bytes 4718592 | tf_op jit(solution)/shard_map/all_to_all | solution.py:529
  15.8 35.3 %collective-permute-start = (f32[128,128]{1,0:T(8,128)S(1)}, f32[128,128]{1,0:T(8,128)S(1)}, u32[]{:S(2)}, u32[]{:S(2)}) collective-permute-start(f32[128,128]{1,0:T(8,128)S(1)} %get-tuple-element.37), channel_id=1, source_target_pairs={{0,31},{1,0},{2,1},{3,2},{4,3},{5,4},{6,5},{7,6},{8,7},{9,8},{10,9... | collective-permute-start | bytes 196616 | tf_op jit(solution)/shard_map/ppermute | solution.py:502
  16.9 34.2 %collective-permute-start.1 = (f32[128,128]{1,0:T(8,128)S(1)}, f32[128,128]{1,0:T(8,128)S(1)}, u32[]{:S(2)}, u32[]{:S(2)}) collective-permute-start(f32[128,128]{1,0:T(8,128)S(1)} %get-tuple-element.36), channel_id=1, source_target_pairs={{0,1},{1,2},{2,3},{3,4},{4,5},{5,6},{6,7},{7,8},{8,9},{9,10},{10,1... | collective-permute-start | bytes 196616 | tf_op jit(solution)/shard_map/ppermute | solution.py:503
  49.6 2.0 %copy-start.1 = (bf16[1024,256]{1,0:T(8,128)(2,1)S(1)}, bf16[1024,256]{1,0:T(8,128)(2,1)}, u32[]{:S(2)}) copy-start(bf16[1024,256]{1,0:T(8,128)(2,1)} %constant.16.clone.col_ref) | copy-start | bytes 1572868
  49.6 2.0 %copy-start.2 = (bf16[768,128]{1,0:T(8,128)(2,1)S(1)}, bf16[768,128]{1,0:T(8,128)(2,1)}, u32[]{:S(2)}) copy-start(bf16[768,128]{1,0:T(8,128)(2,1)} %constant.17.clone.edge_ref) | copy-start | bytes 589828
  49.6 2.0 %copy-start.4 = (bf16[384,128]{1,0:T(8,128)(2,1)S(1)}, bf16[384,128]{1,0:T(8,128)(2,1)}, u32[]{:S(2)}) copy-start(bf16[384,128]{1,0:T(8,128)(2,1)} %constant.18.clone.own_ref) | copy-start | bytes 294916
  49.6 6.9 %collective-permute-start.4 = (f32[64,1152]{1,0:T(8,128)S(1)}, f32[64,1152]{1,0:T(8,128)S(1)}, u32[]{:S(2)}, u32[]{:S(2)}) collective-permute-start(f32[64,1152]{1,0:T(8,128)S(1)} %get-tuple-element.25), channel_id=1, source_target_pairs={{0,32},{32,0},{64,96},{96,64},{1,33},{33,1},{65,97},{97,65},{2,34}... | collective-permute-start | bytes 884744 | tf_op jit(solution)/shard_map/ppermute | solution.py:560
  49.7 7.8 %collective-permute-start.5 = (f32[64,1152]{1,0:T(8,128)S(1)}, f32[64,1152]{1,0:T(8,128)S(1)}, u32[]{:S(2)}, u32[]{:S(2)}) collective-permute-start(f32[64,1152]{1,0:T(8,128)S(1)} %get-tuple-element.26), channel_id=1, source_target_pairs={{32,64},{64,32},{96,0},{0,96},{33,65},{65,33},{97,1},{1,97},{34,66... | collective-permute-start | bytes 884744 | tf_op jit(solution)/shard_map/ppermute | solution.py:560
  51.6 6.0 %copy-start.5 = (bf16[256,128]{1,0:T(8,128)(2,1)S(1)}, bf16[256,128]{1,0:T(8,128)(2,1)}, u32[]{:S(2)}) copy-start(bf16[256,128]{1,0:T(8,128)(2,1)} %constant.19.clone.halo_ref) | copy-start | bytes 196612
  53.0 7.6 %copy-start.3 = (bf16[256,192]{1,0:T(8,128)(2,1)S(1)}, bf16[256,192]{1,0:T(8,128)(2,1)}, u32[]{:S(2)}) copy-start(bf16[256,192]{1,0:T(8,128)(2,1)} %constant.20.clone.row_ref) | copy-start | bytes 294916
  53.0 6.7 %collective-permute-start.2 = (f32[32,1152]{1,0:T(8,128)S(1)}, f32[32,1152]{1,0:T(8,128)S(1)}, u32[]{:S(2)}, u32[]{:S(2)}) collective-permute-start(f32[32,1152]{1,0:T(8,128)S(1)} %get-tuple-element.22), channel_id=1, source_target_pairs={{0,32},{32,0},{64,96},{96,64},{1,33},{33,1},{65,97},{97,65},{2,34}... | collective-permute-start | bytes 442376 | tf_op jit(solution)/shard_map/ppermute | solution.py:588
  53.3 7.3 %collective-permute-start.3 = (f32[32,1152]{1,0:T(8,128)S(1)}, f32[32,1152]{1,0:T(8,128)S(1)}, u32[]{:S(2)}, u32[]{:S(2)}) collective-permute-start(f32[32,1152]{1,0:T(8,128)S(1)} %get-tuple-element.23), channel_id=1, source_target_pairs={{32,64},{64,32},{96,0},{0,96},{33,65},{65,33},{97,1},{1,97},{34,66... | collective-permute-start | bytes 442376 | tf_op jit(solution)/shard_map/ppermute | solution.py:588

commit v11 on v10

--- a/solution.py
+++ b/solution.py
@@ -178,7 +178,7 @@
 
 
 def odd_row():
-    return lax.rem(lax.axis_index("ty"), 2)
+    return lax.rem(lax.axis_index("ty") + 1 - lax.axis_index("tx_2"), 2)
 
 
 def to_partners(ref, near_ref, next_ref):
@@ -556,14 +556,22 @@
     )
     n_ty = lax.axis_size("ty")
     swaps = [(i, i ^ 1) for i in range(n_ty)]
-    far = [((i + 1) % n_ty, ((i ^ 1) + 1) % n_ty) for i in range(n_ty)]
-    s_near, s_next = lax.ppermute(s_near, "ty", swaps), lax.ppermute(s_next, "ty", far)
+    others = [((i + 1) % n_ty, ((i ^ 1) + 1) % n_ty) for i in range(n_ty)]
+    columns = ("ty", "tx_2")
+
+    def in_turn(first_core, second_core):
+        return [(2 * a, 2 * b) for a, b in first_core] + [
+            (2 * a + 1, 2 * b + 1) for a, b in second_core
+        ]
+
+    near, far = in_turn(others, swaps), in_turn(swaps, others)
+    s_near, s_next = lax.ppermute(s_near, columns, near), lax.ppermute(s_next, columns, far)
 
     tall = rows + 2 * HALF
     col_taps = taps(np.arange(2 * LANES)[None, :] - np.arange(4 * LANES)[:, None] + LANES, 0)
     ring = np.where(np.arange(LANES) < 64, cols, -LANES) + np.arange(LANES)
-    near = np.concatenate([np.arange(cols - LANES, cols), ring, np.arange(LANES)])
-    edge_taps = taps(ring[None, :] - near[:, None], 0)
+    beside = np.concatenate([np.arange(cols - LANES, cols), ring, np.arange(LANES)])
+    edge_taps = taps(ring[None, :] - beside[:, None], 0)
     tile = (rows, cols)
     inside = np.arange(rows)
     border_rows = np.concatenate(
@@ -585,7 +593,7 @@
         flops=5 * 2 * tall * wide * 3 * LANES,
         name="early",
     )
-    w_near, w_next = lax.ppermute(w_near, "ty", swaps), lax.ppermute(w_next, "ty", far)
+    w_near, w_next = lax.ppermute(w_near, columns, near), lax.ppermute(w_next, columns, far)
     border, early = call(
         functools.partial(first_kernel, n_ty),
         [(4 * HALF, wide), (16, LANES)],

time: 80 us -> 79.8 us (level)
  transfers between devices with their start and end apart: 7 -> 7, of which waited for: 5 -> 4; matrix products, arithmetic and copies ran while one was open for 0% -> 0% of each run, Pallas kernels for 5% -> 5%
where the time goes in v11:
time: 79.8 us; the launch traced here: 79.6 us
  waiting for transfers between devices  35.5 us (44%)
  starting transfers between devices  17 us (21%)
  blocking collectives  15.5 us (19%)
  Pallas kernels  10.8 us (14%)
    all_to_all x1, waiting for transfers between devices, shards(): lax.all_to_all(message.reshape(devices, 1, length * LANES), TY_TX, split_...  31.2 us
    all_to_all x1, blocking collectives, shards(): lax.all_to_all(moments.reshape(devices, 1, LANES), TY_TX, split_axis=0, c...  15.5 us
    all_to_all x1, starting transfers between devices, shards(): lax.all_to_all(message.reshape(devices, 1, length * LANES), TY_TX, split_...  11.5 us
    pallas_call x7, Pallas kernels, call(): pl.pallas_call(kernel, out_shape=[jax.ShapeDtypeStruct(s, F32) if isinsta...  10.8 us
    ppermute x1, waiting for transfers between devices, shards(): lax.ppermute(s_next, columns, far)  2.27 us
    ppermute x1, starting transfers between devices, shards(): lax.ppermute(w_next, columns, far)  1.88 us
  transfers between devices with their start and end apart: 7, of which 4 were waited for; matrix products, arithmetic and copies ran while one was open for 0% of the time, Pallas kernels for 5%

profile of v11, /device:TPU:1, one launch (start us, length us, event | category | flops | bytes accessed | tf_op | source)
XLA Modules:
  0.0 79.6 jit_solution(885428702729174608)
XLA Ops:
  0.6 3.6 %pack.1 = f32[4608,128]{1,0:T(8,128)} custom-call(s32[1,128]{1,0:T(1,128)} %bitcast.17, s32[1,128]{1,0:T(1,128)} %bitcast.18, f32[1024,128]{1,0:T(8,128)} %bitcast.15, f32[1024,128]{1,0:T(8,128)} %bitcast.16), custom_call_target="tpu_custom_call" | custom-call | bytes 1049600 | tf_op jit(solution)/shard_map/pack/pallas_call | solution.py:474
  4.2 0.0 copy-start
  4.2 11.5 %all-to-all-start = ((f32[128,1,4608]{2,1,0:T(1,128)}), f32[128,1,4608]{2,1,0:T(1,128)S(1)}, u32[]{:S(2)}, u32[]{:S(2)}) async-start(f32[128,1,4608]{2,1,0:T(1,128)} %bitcast.14), calls=%async_computation | async-start | bytes 4718592 | tf_op jit(solution)/shard_map/all_to_all | solution.py:529
  15.8 0.0 copy-done
  15.8 1.1 %collective-permute-start = (f32[128,128]{1,0:T(8,128)S(1)}, f32[128,128]{1,0:T(8,128)S(1)}, u32[]{:S(2)}, u32[]{:S(2)}) collective-permute-start(f32[128,128]{1,0:T(8,128)S(1)} %get-tuple-element.37), channel_id=1, source_target_pairs={{0,31},{1,0},{2,1},{3,2},{4,3},{5,4},{6,5},{7,6},{8,7},{9,8},{10,9... | collective-permute-start | bytes 196616 | tf_op jit(solution)/shard_map/ppermute | solution.py:502
  16.9 0.7 collective-permute-start.1
  17.6 31.2 %all-to-all-done = f32[128,1,4608]{2,1,0:T(1,128)S(1)} async-done(((f32[128,1,4608]{2,1,0:T(1,128)}), f32[128,1,4608]{2,1,0:T(1,128)S(1)}, u32[]{:S(2)}, u32[]{:S(2)}) %all-to-all-start) | async-done | bytes 2359328 | tf_op jit(solution)/shard_map/all_to_all | solution.py:529
  48.8 0.7 sums.1
  49.6 0.0 copy-start.1
  49.6 0.0 copy-start.2
  49.6 0.0 copy-start.4
  49.6 0.1 collective-permute-start.4
  49.7 1.4 %collective-permute-start.5 = (f32[64,1152]{1,0:T(8,128)S(1)}, f32[64,1152]{1,0:T(8,128)S(1)}, u32[]{:S(2)}, u32[]{:S(2)}) collective-permute-start(f32[64,1152]{1,0:T(8,128)S(1)} %get-tuple-element.26), channel_id=1, source_target_pairs={{0,32},{32,0},{64,96},{96,64},{33,65},{65,33},{97,1},{1,97},{2,34}... | collective-permute-start | bytes 884744 | tf_op jit(solution)/shard_map/ppermute | solution.py:568
  51.1 0.0 collective-permute-done
  51.1 0.0 collective-permute-done.1
  51.1 0.4 weights.1.w_ref
  51.6 0.0 copy-start.5
  51.6 0.0 copy-done.1
  51.6 0.0 copy-done.2
  51.6 0.0 copy-done.4
  51.6 1.4 %early.1 = (f32[128,1152]{1,0:T(8,128)S(1)}, f32[64,1152]{1,0:T(8,128)S(1)}, f32[128,1024]{1,0:T(8,128)S(1)}, f32[128,1024]{1,0:T(8,128)S(1)}, f32[16,128]{1,0:T...) custom-call(f32[128,1152]{1,0:T(8,128)S(1)} %get-tuple-element.21.s_ref, f32[128,1152]{1,0:T(8,128)S(1)} %weights.1.w_ref, ...), custom_call_target="tpu_custom_call" | custom-call | flops 849346560 | bytes 1998848 | tf_op jit(solution)/shard_map/early/pallas_call | solution.py:474
  53.0 0.0 copy-start.3
  53.0 0.3 collective-permute-start.2
  53.3 1.9 %collective-permute-start.3 = (f32[32,1152]{1,0:T(8,128)S(1)}, f32[32,1152]{1,0:T(8,128)S(1)}, u32[]{:S(2)}, u32[]{:S(2)}) collective-permute-start(f32[32,1152]{1,0:T(8,128)S(1)} %get-tuple-element.23), channel_id=1, source_target_pairs={{0,32},{32,0},{64,96},{96,64},{33,65},{65,33},{97,1},{1,97},{2,34}... | collective-permute-start | bytes 442376 | tf_op jit(solution)/shard_map/ppermute | solution.py:596
  55.2 0.4 collective-permute-done.4.near_ref
  55.7 2.3 %collective-permute-done.5.next_ref = f32[64,1152]{1,0:T(8,128)S(1)} collective-permute-done((f32[64,1152]{1,0:T(8,128)S(1)}, f32[64,1152]{1,0:T(8,128)S(1)}, u32[]{:S(2)}, u32[]{:S(2)}) %collective-permute-start.5) | collective-permute-done | bytes 294944 | tf_op jit(solution)/shard_map/ppermute | solution.py:568
  57.9 0.0 copy-done.5
  57.9 1.6 %first.1 = (f32[128,1152]{1,0:T(8,128)S(1)}, f32[16,128]{1,0:T(8,128)S(1)}) custom-call(f32[128,1152]{1,0:T(8,128)S(1)} %get-tuple-element.21.s_ref, f32[64,1152]{1,0:T(8,128)S(1)} %collective-permute-done.4.near_ref, f32[64,1152]{1,0:T(8,128)S(1)} %collective-permute-done.5.next_ref, f32[128,1152]{1,0:T(8,128)S(1)} %get-tuple-element.27.part_ref, ...), custom_call_target="tpu_custom_call" | custom-call | flops 1132462080 | bytes 2564096 | tf_op jit(solution)/shard_map/first/pallas_call | solution.py:474
  59.5 0.0 collective-permute-done.2.near_ref
  59.5 1.6 %collective-permute-done.3.next_ref = f32[32,1152]{1,0:T(8,128)S(1)} collective-permute-done((f32[32,1152]{1,0:T(8,128)S(1)}, f32[32,1152]{1,0:T(8,128)S(1)}, u32[]{:S(2)}, u32[]{:S(2)}) %collective-permute-start.3) | collective-permute-done | bytes 147488 | tf_op jit(solution)/shard_map/ppermute | solution.py:596
  61.1 0.0 copy-done.3
  61.1 1.6 %second.1 = (f32[128,1024]{1,0:T(8,128)S(1)}, f32[128,1024]{1,0:T(8,128)S(1)}, f32[128,128]{1,0:T(8,128)S(1)}) custom-call(f32[128,1152]{1,0:T(8,128)S(1)} %weights.1.w_ref, f32[32,1152]{1,0:T(8,128)S(1)} %collective-permute-done.2.near_ref, f32[32,1152]{1,0:T(8,128)S(1)} %collective-permute-done.3.next_ref, f32[64,1152]{1,0:T(8,128)S(1)} %get-tuple-element.24.deep_ref, ...), custom_call_target="tpu_custom_call" | custom-call | flops 1132462080 | bytes 3448832 | tf_op jit(solution)/shard_map/second/pallas_call | solution.py:474
  62.7 15.5 %all_to_all.10 = f32[128,1,128]{2,1,0:T(1,128)S(1)} all-to-all(f32[128,1,128]{2,1,0:T(1,128)S(1)} %bitcast.13), channel_id=1, replica_groups=mesh['ty'=4,'tx_0'=4,'tx_1'=4,'tx_2'=2] {'ty','tx_0','tx_1','tx_2'}, dimensions={0} | all-to-all | bytes 131072 | tf_op jit(solution)/shard_map/all_to_all | solution.py:630
  78.2 1.4 %combine.1 = (f32[128,1024]{1,0:T(8,128)}, f32[128,1024]{1,0:T(8,128)}) custom-call(f32[128,128]{1,0:T(8,128)S(1)} %bitcast.12, f32[128,1024]{1,0:T(8,128)S(1)} %get-tuple-element.31.r0_ref, f32[128,1024]{1,0:T(8,128)S(1)} %get-tuple-element.34.b0_ref, f32[128,1024]{1,0:T(8,128)S(1)} %get-tuple-element.35.b1_ref), custom_call_target="tpu_custom_call" | custom-call | bytes 1638400 | tf_op jit(solution)/shard_map/combine/pallas_call | solution.py:474
  (3 shorter events, 0.0 us)
Async XLA Ops:
  4.2 11.5 %copy-start = (f32[128,1024]{1,0:T(8,128)S(1)}, f32[128,1024]{1,0:T(8,128)}, u32[]{:S(2)}) copy-start(f32[128,1024]{1,0:T(8,128)} %prior_ref.1) | copy-start | bytes 1572868
  4.2 44.6 %all-to-all-start = ((f32[128,1,4608]{2,1,0:T(1,128)}), f32[128,1,4608]{2,1,0:T(1,128)S(1)}, u32[]{:S(2)}, u32[]{:S(2)}) async-start(f32[128,1,4608]{2,1,0:T(1,128)} %bitcast.14), calls=%async_computation | async-start | bytes 4718592 | tf_op jit(solution)/shard_map/all_to_all | solution.py:529
  15.8 35.3 %collective-permute-start = (f32[128,128]{1,0:T(8,128)S(1)}, f32[128,128]{1,0:T(8,128)S(1)}, u32[]{:S(2)}, u32[]{:S(2)}) collective-permute-start(f32[128,128]{1,0:T(8,128)S(1)} %get-tuple-element.37), channel_id=1, source_target_pairs={{0,31},{1,0},{2,1},{3,2},{4,3},{5,4},{6,5},{7,6},{8,7},{9,8},{10,9... | collective-permute-start | bytes 196616 | tf_op jit(solution)/shard_map/ppermute | solution.py:502
  16.9 34.2 %collective-permute-start.1 = (f32[128,128]{1,0:T(8,128)S(1)}, f32[128,128]{1,0:T(8,128)S(1)}, u32[]{:S(2)}, u32[]{:S(2)}) collective-permute-start(f32[128,128]{1,0:T(8,128)S(1)} %get-tuple-element.36), channel_id=1, source_target_pairs={{0,1},{1,2},{2,3},{3,4},{4,5},{5,6},{6,7},{7,8},{8,9},{9,10},{10,1... | collective-permute-start | bytes 196616 | tf_op jit(solution)/shard_map/ppermute | solution.py:503
  49.6 2.0 %copy-start.1 = (bf16[1024,256]{1,0:T(8,128)(2,1)S(1)}, bf16[1024,256]{1,0:T(8,128)(2,1)}, u32[]{:S(2)}) copy-start(bf16[1024,256]{1,0:T(8,128)(2,1)} %constant.16.clone.col_ref) | copy-start | bytes 1572868
  49.6 2.0 %copy-start.2 = (bf16[768,128]{1,0:T(8,128)(2,1)S(1)}, bf16[768,128]{1,0:T(8,128)(2,1)}, u32[]{:S(2)}) copy-start(bf16[768,128]{1,0:T(8,128)(2,1)} %constant.17.clone.edge_ref) | copy-start | bytes 589828
  49.6 2.0 %copy-start.4 = (bf16[384,128]{1,0:T(8,128)(2,1)S(1)}, bf16[384,128]{1,0:T(8,128)(2,1)}, u32[]{:S(2)}) copy-start(bf16[384,128]{1,0:T(8,128)(2,1)} %constant.18.clone.own_ref) | copy-start | bytes 294916
  49.6 6.1 %collective-permute-start.4 = (f32[64,1152]{1,0:T(8,128)S(1)}, f32[64,1152]{1,0:T(8,128)S(1)}, u32[]{:S(2)}, u32[]{:S(2)}) collective-permute-start(f32[64,1152]{1,0:T(8,128)S(1)} %get-tuple-element.25), channel_id=1, source_target_pairs={{32,64},{64,32},{96,0},{0,96},{1,33},{33,1},{65,97},{97,65},{34,66... | collective-permute-start | bytes 884744 | tf_op jit(solution)/shard_map/ppermute | solution.py:568
  49.7 8.3 %collective-permute-start.5 = (f32[64,1152]{1,0:T(8,128)S(1)}, f32[64,1152]{1,0:T(8,128)S(1)}, u32[]{:S(2)}, u32[]{:S(2)}) collective-permute-start(f32[64,1152]{1,0:T(8,128)S(1)} %get-tuple-element.26), channel_id=1, source_target_pairs={{0,32},{32,0},{64,96},{96,64},{33,65},{65,33},{97,1},{1,97},{2,34}... | collective-permute-start | bytes 884744 | tf_op jit(solution)/shard_map/ppermute | solution.py:568
  51.6 6.4 %copy-start.5 = (bf16[256,128]{1,0:T(8,128)(2,1)S(1)}, bf16[256,128]{1,0:T(8,128)(2,1)}, u32[]{:S(2)}) copy-start(bf16[256,128]{1,0:T(8,128)(2,1)} %constant.19.clone.halo_ref) | copy-start | bytes 196612
  53.0 8.1 %copy-start.3 = (bf16[256,192]{1,0:T(8,128)(2,1)S(1)}, bf16[256,192]{1,0:T(8,128)(2,1)}, u32[]{:S(2)}) copy-start(bf16[256,192]{1,0:T(8,128)(2,1)} %constant.20.clone.row_ref) | copy-start | bytes 294916
  53.0 6.5 %collective-permute-start.2 = (f32[32,1152]{1,0:T(8,128)S(1)}, f32[32,1152]{1,0:T(8,128)S(1)}, u32[]{:S(2)}, u32[]{:S(2)}) collective-permute-start(f32[32,1152]{1,0:T(8,128)S(1)} %get-tuple-element.22), channel_id=1, source_target_pairs={{32,64},{64,32},{96,0},{0,96},{1,33},{33,1},{65,97},{97,65},{34,66... | collective-permute-start | bytes 442376 | tf_op jit(solution)/shard_map/ppermute | solution.py:596
  53.3 7.8 %collective-permute-start.3 = (f32[32,1152]{1,0:T(8,128)S(1)}, f32[32,1152]{1,0:T(8,128)S(1)}, u32[]{:S(2)}, u32[]{:S(2)}) collective-permute-start(f32[32,1152]{1,0:T(8,128)S(1)} %get-tuple-element.23), channel_id=1, source_target_pairs={{0,32},{32,0},{64,96},{96,64},{33,65},{65,33},{97,1},{1,97},{2,34}... | collective-permute-start | bytes 442376 | tf_op jit(solution)/shard_map/ppermute | solution.py:596

commit v12 on v10

--- a/solution.py
+++ b/solution.py
@@ -224,8 +224,10 @@
     base = 2 * SLOTS * parts
     from_left = [slot_rows(got_ref, length, base + k, devices) for k in range(SLOTS)]
     from_right = [slot_rows(got_ref, length, base + SLOTS + k, devices) for k in range(SLOTS)]
-    left_t = [jnp.transpose(x) for x in from_left]
-    right_t = [jnp.transpose(x) for x in from_right]
+    first_lane = iota((devices, LANES), 1) == 0
+    numbers = [
+        jnp.transpose(jnp.where(first_lane, x, y)) for x, y in zip(from_left, from_right)
+    ]
     wanted = (iota((rows, devices), 0) + 1).astype(F32)
 
     def chooser(lists, at):
@@ -233,11 +235,11 @@
             [jnp.where(x[at : at + 1, :] == wanted, 1.0, 0.0) for x in lists], axis=1
         ).astype(BF16)
 
-    own = chooser(right_t, 97)
+    own = chooser(numbers, 97)
     select_ref[...] = own
     gather_tile(got_ref, parts, length, 0, own, s_ref, None)
-    left = pick(chooser(left_t, 0), jnp.concatenate(from_left, axis=0))
-    right = pick(chooser(right_t, 96), jnp.concatenate(from_right, axis=0))
+    left = pick(chooser(numbers, 0), jnp.concatenate(from_left, axis=0))
+    right = pick(chooser(numbers, 96), jnp.concatenate(from_right, axis=0))
     lane = iota((rows, LANES), 1)
     s_ref[:, cols:] = jnp.where(lane < 64, right, left)
     strip_ref[...] = jnp.where(lane < 64, pltpu.roll(right, 64, 1), pltpu.roll(left, 64, 1))

time: 80 us -> 80 us (level)
  no operation moved by 1% of the time
where the time goes in v12:
time: 80 us; the launch traced here: 79.8 us
  waiting for transfers between devices  35.1 us (44%)
  starting transfers between devices  17 us (21%)
  blocking collectives  16 us (20%)
  Pallas kernels  10.8 us (14%)
    all_to_all x1, waiting for transfers between devices, shards(): lax.all_to_all(message.reshape(devices, 1, length * LANES), TY_TX, split_...  31.2 us
    all_to_all x1, blocking collectives, shards(): lax.all_to_all(moments.reshape(devices, 1, LANES), TY_TX, split_axis=0, c...  16 us
    all_to_all x1, starting transfers between devices, shards(): lax.all_to_all(message.reshape(devices, 1, length * LANES), TY_TX, split_...  11.5 us
    pallas_call x7, Pallas kernels, call(): pl.pallas_call(kernel, out_shape=[jax.ShapeDtypeStruct(s, F32) if isinsta...  10.8 us
    ppermute x1, starting transfers between devices, shards(): lax.ppermute(w_next, 'ty', far)  1.88 us
  transfers between devices with their start and end apart: 7, of which 5 were waited for; matrix products, arithmetic and copies ran while one was open for 0% of the time, Pallas kernels for 5%

profile of v12, /device:TPU:1, one launch (start us, length us, event | category | flops | bytes accessed | tf_op | source)
XLA Modules:
  0.0 79.8 jit_solution(16986673226463471460)
XLA Ops:
  0.6 3.6 %pack.1 = f32[4608,128]{1,0:T(8,128)} custom-call(s32[1,128]{1,0:T(1,128)} %bitcast.17, s32[1,128]{1,0:T(1,128)} %bitcast.18, f32[1024,128]{1,0:T(8,128)} %bitcast.15, f32[1024,128]{1,0:T(8,128)} %bitcast.16), custom_call_target="tpu_custom_call" | custom-call | bytes 1049600 | tf_op jit(solution)/shard_map/pack/pallas_call | solution.py:476
  4.2 0.0 copy-start
  4.2 11.5 %all-to-all-start = ((f32[128,1,4608]{2,1,0:T(1,128)}), f32[128,1,4608]{2,1,0:T(1,128)S(1)}, u32[]{:S(2)}, u32[]{:S(2)}) async-start(f32[128,1,4608]{2,1,0:T(1,128)} %bitcast.14), calls=%async_computation | async-start | bytes 4718592 | tf_op jit(solution)/shard_map/all_to_all | solution.py:531
  15.8 0.0 copy-done
  15.8 1.1 %collective-permute-start = (f32[128,128]{1,0:T(8,128)S(1)}, f32[128,128]{1,0:T(8,128)S(1)}, u32[]{:S(2)}, u32[]{:S(2)}) collective-permute-start(f32[128,128]{1,0:T(8,128)S(1)} %get-tuple-element.37), channel_id=1, source_target_pairs={{0,31},{1,0},{2,1},{3,2},{4,3},{5,4},{6,5},{7,6},{8,7},{9,8},{10,9... | collective-permute-start | bytes 196616 | tf_op jit(solution)/shard_map/ppermute | solution.py:504
  16.9 0.7 collective-permute-start.1
  17.6 31.2 %all-to-all-done = f32[128,1,4608]{2,1,0:T(1,128)S(1)} async-done(((f32[128,1,4608]{2,1,0:T(1,128)}), f32[128,1,4608]{2,1,0:T(1,128)S(1)}, u32[]{:S(2)}, u32[]{:S(2)}) %all-to-all-start) | async-done | bytes 2359328 | tf_op jit(solution)/shard_map/all_to_all | solution.py:531
  48.8 0.7 sums.1
  49.6 0.0 copy-start.1
  49.6 0.0 copy-start.2
  49.6 0.0 copy-start.4
  49.6 0.1 collective-permute-start.4
  49.7 1.4 %collective-permute-start.5 = (f32[64,1152]{1,0:T(8,128)S(1)}, f32[64,1152]{1,0:T(8,128)S(1)}, u32[]{:S(2)}, u32[]{:S(2)}) collective-permute-start(f32[64,1152]{1,0:T(8,128)S(1)} %get-tuple-element.26), channel_id=1, source_target_pairs={{32,64},{64,32},{96,0},{0,96},{33,65},{65,33},{97,1},{1,97},{34,66... | collective-permute-start | bytes 884744 | tf_op jit(solution)/shard_map/ppermute | solution.py:562
  51.1 0.0 collective-permute-done
  51.1 0.0 collective-permute-done.1
  51.1 0.4 weights.1.w_ref
  51.6 0.0 copy-start.5
  51.6 0.0 copy-done.1
  51.6 0.0 copy-done.2
  51.6 0.0 copy-done.4
  51.6 1.4 %early.1 = (f32[128,1152]{1,0:T(8,128)S(1)}, f32[64,1152]{1,0:T(8,128)S(1)}, f32[128,1024]{1,0:T(8,128)S(1)}, f32[128,1024]{1,0:T(8,128)S(1)}, f32[16,128]{1,0:T...) custom-call(f32[128,1152]{1,0:T(8,128)S(1)} %get-tuple-element.21.s_ref, f32[128,1152]{1,0:T(8,128)S(1)} %weights.1.w_ref, ...), custom_call_target="tpu_custom_call" | custom-call | flops 849346560 | bytes 1998848 | tf_op jit(solution)/shard_map/early/pallas_call | solution.py:476
  53.0 0.0 copy-start.3
  53.0 0.3 collective-permute-start.2
  53.3 1.9 %collective-permute-start.3 = (f32[32,1152]{1,0:T(8,128)S(1)}, f32[32,1152]{1,0:T(8,128)S(1)}, u32[]{:S(2)}, u32[]{:S(2)}) collective-permute-start(f32[32,1152]{1,0:T(8,128)S(1)} %get-tuple-element.23), channel_id=1, source_target_pairs={{32,64},{64,32},{96,0},{0,96},{33,65},{65,33},{97,1},{1,97},{34,66... | collective-permute-start | bytes 442376 | tf_op jit(solution)/shard_map/ppermute | solution.py:590
  55.2 1.3 %collective-permute-done.4.near_ref = f32[64,1152]{1,0:T(8,128)S(1)} collective-permute-done((f32[64,1152]{1,0:T(8,128)S(1)}, f32[64,1152]{1,0:T(8,128)S(1)}, u32[]{:S(2)}, u32[]{:S(2)}) %collective-permute-start.4) | collective-permute-done | bytes 294944 | tf_op jit(solution)/shard_map/ppermute | solution.py:562
  56.5 1.0 %collective-permute-done.5.next_ref = f32[64,1152]{1,0:T(8,128)S(1)} collective-permute-done((f32[64,1152]{1,0:T(8,128)S(1)}, f32[64,1152]{1,0:T(8,128)S(1)}, u32[]{:S(2)}, u32[]{:S(2)}) %collective-permute-start.5) | collective-permute-done | bytes 294944 | tf_op jit(solution)/shard_map/ppermute | solution.py:562
  57.5 0.0 copy-done.5
  57.5 1.6 %first.1 = (f32[128,1152]{1,0:T(8,128)S(1)}, f32[16,128]{1,0:T(8,128)S(1)}) custom-call(f32[128,1152]{1,0:T(8,128)S(1)} %get-tuple-element.21.s_ref, f32[64,1152]{1,0:T(8,128)S(1)} %collective-permute-done.4.near_ref, f32[64,1152]{1,0:T(8,128)S(1)} %collective-permute-done.5.next_ref, f32[128,1152]{1,0:T(8,128)S(1)} %get-tuple-element.27.part_ref, ...), custom_call_target="tpu_custom_call" | custom-call | flops 1132462080 | bytes 2564096 | tf_op jit(solution)/shard_map/first/pallas_call | solution.py:476
  59.1 0.6 collective-permute-done.2.near_ref
  59.7 1.0 %collective-permute-done.3.next_ref = f32[32,1152]{1,0:T(8,128)S(1)} collective-permute-done((f32[32,1152]{1,0:T(8,128)S(1)}, f32[32,1152]{1,0:T(8,128)S(1)}, u32[]{:S(2)}, u32[]{:S(2)}) %collective-permute-start.3) | collective-permute-done | bytes 147488 | tf_op jit(solution)/shard_map/ppermute | solution.py:590
  60.7 0.0 copy-done.3
  60.7 1.6 %second.1 = (f32[128,1024]{1,0:T(8,128)S(1)}, f32[128,1024]{1,0:T(8,128)S(1)}, f32[128,128]{1,0:T(8,128)S(1)}) custom-call(f32[128,1152]{1,0:T(8,128)S(1)} %weights.1.w_ref, f32[32,1152]{1,0:T(8,128)S(1)} %collective-permute-done.2.near_ref, f32[32,1152]{1,0:T(8,128)S(1)} %collective-permute-done.3.next_ref, f32[64,1152]{1,0:T(8,128)S(1)} %get-tuple-element.24.deep_ref, ...), custom_call_target="tpu_custom_call" | custom-call | flops 1132462080 | bytes 3448832 | tf_op jit(solution)/shard_map/second/pallas_call | solution.py:476
  62.3 16.0 %all_to_all.10 = f32[128,1,128]{2,1,0:T(1,128)S(1)} all-to-all(f32[128,1,128]{2,1,0:T(1,128)S(1)} %bitcast.13), channel_id=1, replica_groups=mesh['ty'=4,'tx_0'=4,'tx_1'=4,'tx_2'=2] {'ty','tx_0','tx_1','tx_2'}, dimensions={0} | all-to-all | bytes 131072 | tf_op jit(solution)/shard_map/all_to_all | solution.py:624
  78.4 1.4 %combine.1 = (f32[128,1024]{1,0:T(8,128)}, f32[128,1024]{1,0:T(8,128)}) custom-call(f32[128,128]{1,0:T(8,128)S(1)} %bitcast.12, f32[128,1024]{1,0:T(8,128)S(1)} %get-tuple-element.31.r0_ref, f32[128,1024]{1,0:T(8,128)S(1)} %get-tuple-element.34.b0_ref, f32[128,1024]{1,0:T(8,128)S(1)} %get-tuple-element.35.b1_ref), custom_call_target="tpu_custom_call" | custom-call | bytes 1638400 | tf_op jit(solution)/shard_map/combine/pallas_call | solution.py:476
  (3 shorter events, 0.0 us)
Async XLA Ops:
  4.2 11.5 %copy-start = (f32[128,1024]{1,0:T(8,128)S(1)}, f32[128,1024]{1,0:T(8,128)}, u32[]{:S(2)}) copy-start(f32[128,1024]{1,0:T(8,128)} %prior_ref.1) | copy-start | bytes 1572868
  4.2 44.6 %all-to-all-start = ((f32[128,1,4608]{2,1,0:T(1,128)}), f32[128,1,4608]{2,1,0:T(1,128)S(1)}, u32[]{:S(2)}, u32[]{:S(2)}) async-start(f32[128,1,4608]{2,1,0:T(1,128)} %bitcast.14), calls=%async_computation | async-start | bytes 4718592 | tf_op jit(solution)/shard_map/all_to_all | solution.py:531
  15.8 35.3 %collective-permute-start = (f32[128,128]{1,0:T(8,128)S(1)}, f32[128,128]{1,0:T(8,128)S(1)}, u32[]{:S(2)}, u32[]{:S(2)}) collective-permute-start(f32[128,128]{1,0:T(8,128)S(1)} %get-tuple-element.37), channel_id=1, source_target_pairs={{0,31},{1,0},{2,1},{3,2},{4,3},{5,4},{6,5},{7,6},{8,7},{9,8},{10,9... | collective-permute-start | bytes 196616 | tf_op jit(solution)/shard_map/ppermute | solution.py:504
  16.9 34.2 %collective-permute-start.1 = (f32[128,128]{1,0:T(8,128)S(1)}, f32[128,128]{1,0:T(8,128)S(1)}, u32[]{:S(2)}, u32[]{:S(2)}) collective-permute-start(f32[128,128]{1,0:T(8,128)S(1)} %get-tuple-element.36), channel_id=1, source_target_pairs={{0,1},{1,2},{2,3},{3,4},{4,5},{5,6},{6,7},{7,8},{8,9},{9,10},{10,1... | collective-permute-start | bytes 196616 | tf_op jit(solution)/shard_map/ppermute | solution.py:505
  49.6 2.0 %copy-start.1 = (bf16[1024,256]{1,0:T(8,128)(2,1)S(1)}, bf16[1024,256]{1,0:T(8,128)(2,1)}, u32[]{:S(2)}) copy-start(bf16[1024,256]{1,0:T(8,128)(2,1)} %constant.16.clone.col_ref) | copy-start | bytes 1572868
  49.6 2.0 %copy-start.2 = (bf16[768,128]{1,0:T(8,128)(2,1)S(1)}, bf16[768,128]{1,0:T(8,128)(2,1)}, u32[]{:S(2)}) copy-start(bf16[768,128]{1,0:T(8,128)(2,1)} %constant.17.clone.edge_ref) | copy-start | bytes 589828
  49.6 2.0 %copy-start.4 = (bf16[384,128]{1,0:T(8,128)(2,1)S(1)}, bf16[384,128]{1,0:T(8,128)(2,1)}, u32[]{:S(2)}) copy-start(bf16[384,128]{1,0:T(8,128)(2,1)} %constant.18.clone.own_ref) | copy-start | bytes 294916
  49.6 6.9 %collective-permute-start.4 = (f32[64,1152]{1,0:T(8,128)S(1)}, f32[64,1152]{1,0:T(8,128)S(1)}, u32[]{:S(2)}, u32[]{:S(2)}) collective-permute-start(f32[64,1152]{1,0:T(8,128)S(1)} %get-tuple-element.25), channel_id=1, source_target_pairs={{0,32},{32,0},{64,96},{96,64},{1,33},{33,1},{65,97},{97,65},{2,34}... | collective-permute-start | bytes 884744 | tf_op jit(solution)/shard_map/ppermute | solution.py:562
  49.7 7.8 %collective-permute-start.5 = (f32[64,1152]{1,0:T(8,128)S(1)}, f32[64,1152]{1,0:T(8,128)S(1)}, u32[]{:S(2)}, u32[]{:S(2)}) collective-permute-start(f32[64,1152]{1,0:T(8,128)S(1)} %get-tuple-element.26), channel_id=1, source_target_pairs={{32,64},{64,32},{96,0},{0,96},{33,65},{65,33},{97,1},{1,97},{34,66... | collective-permute-start | bytes 884744 | tf_op jit(solution)/shard_map/ppermute | solution.py:562
  51.6 6.0 %copy-start.5 = (bf16[256,128]{1,0:T(8,128)(2,1)S(1)}, bf16[256,128]{1,0:T(8,128)(2,1)}, u32[]{:S(2)}) copy-start(bf16[256,128]{1,0:T(8,128)(2,1)} %constant.19.clone.halo_ref) | copy-start | bytes 196612
  53.0 7.7 %copy-start.3 = (bf16[256,192]{1,0:T(8,128)(2,1)S(1)}, bf16[256,192]{1,0:T(8,128)(2,1)}, u32[]{:S(2)}) copy-start(bf16[256,192]{1,0:T(8,128)(2,1)} %constant.20.clone.row_ref) | copy-start | bytes 294916
  53.0 6.7 %collective-permute-start.2 = (f32[32,1152]{1,0:T(8,128)S(1)}, f32[32,1152]{1,0:T(8,128)S(1)}, u32[]{:S(2)}, u32[]{:S(2)}) collective-permute-start(f32[32,1152]{1,0:T(8,128)S(1)} %get-tuple-element.22), channel_id=1, source_target_pairs={{0,32},{32,0},{64,96},{96,64},{1,33},{33,1},{65,97},{97,65},{2,34}... | collective-permute-start | bytes 442376 | tf_op jit(solution)/shard_map/ppermute | solution.py:590
  53.3 7.3 %collective-permute-start.3 = (f32[32,1152]{1,0:T(8,128)S(1)}, f32[32,1152]{1,0:T(8,128)S(1)}, u32[]{:S(2)}, u32[]{:S(2)}) collective-permute-start(f32[32,1152]{1,0:T(8,128)S(1)} %get-tuple-element.23), channel_id=1, source_target_pairs={{32,64},{64,32},{96,0},{0,96},{33,65},{65,33},{97,1},{1,97},{34,66... | collective-permute-start | bytes 442376 | tf_op jit(solution)/shard_map/ppermute | solution.py:590

commit v13 on v10

--- a/solution.py
+++ b/solution.py
@@ -264,7 +264,7 @@
     )
 
 
-def along_columns(pieces, taps_ref):
+def along_columns(pieces, taps_ref, together=2):
     height, wide = pieces[0].shape
     cols = wide - LANES
 
@@ -277,9 +277,9 @@
 
     half = [stacked(x) for x in pieces]
     out = []
-    for r in range(0, half[0].shape[0], 2 * height):
-        y = times_taps([x[r : r + 2 * height] for x in half], taps_ref)
-        out += [y[:height], y[height:]]
+    for r in range(0, half[0].shape[0], together * height):
+        y = times_taps([x[r : r + together * height] for x in half], taps_ref)
+        out += [y[i * height : (i + 1) * height] for i in range(together)]
     return out
 
 
@@ -405,7 +405,7 @@
         )
         mid_ref[:, at] = taps_times(row_ref, z)
     total_vv = total_rv = total_vq = total_mix = jnp.zeros((8, LANES), F32)
-    for c, y1 in enumerate(along_columns(split3(mid_ref[...]), col_ref)):
+    for c, y1 in enumerate(along_columns(split3(mid_ref[...]), col_ref, 1)):
         at = slice(2 * c * LANES, 2 * (c + 1) * LANES)
         y0 = jnp.concatenate(
             [border_ref[one:two, at], deep_ref[:, at], border_ref[two:three, at]], axis=0

time: 80 us -> 80 us (level)
  no operation moved by 1% of the time
where the time goes in v13:
time: 80 us; the launch traced here: 79.7 us
  waiting for transfers between devices  35.1 us (44%)
  starting transfers between devices  17 us (21%)
  blocking collectives  16.1 us (20%)
  Pallas kernels  10.7 us (13%)
    all_to_all x1, waiting for transfers between devices, shards(): lax.all_to_all(message.reshape(devices, 1, length * LANES), TY_TX, split_...  31.2 us
    all_to_all x1, blocking collectives, shards(): lax.all_to_all(moments.reshape(devices, 1, LANES), TY_TX, split_axis=0, c...  16.1 us
    all_to_all x1, starting transfers between devices, shards(): lax.all_to_all(message.reshape(devices, 1, length * LANES), TY_TX, split_...  11.5 us
    pallas_call x7, Pallas kernels, call(): pl.pallas_call(kernel, out_shape=[jax.ShapeDtypeStruct(s, F32) if isinsta...  10.7 us
    ppermute x1, starting transfers between devices, shards(): lax.ppermute(w_next, 'ty', far)  1.88 us
  transfers between devices with their start and end apart: 7, of which 5 were waited for; matrix products, arithmetic and copies ran while one was open for 0% of the time, Pallas kernels for 5%

profile of v13, /device:TPU:1, one launch (start us, length us, event | category | flops | bytes accessed | tf_op | source)
XLA Modules:
  0.0 79.7 jit_solution(13897690590972060661)
XLA Ops:
  0.6 3.6 %pack.1 = f32[4608,128]{1,0:T(8,128)} custom-call(s32[1,128]{1,0:T(1,128)} %bitcast.17, s32[1,128]{1,0:T(1,128)} %bitcast.18, f32[1024,128]{1,0:T(8,128)} %bitcast.15, f32[1024,128]{1,0:T(8,128)} %bitcast.16), custom_call_target="tpu_custom_call" | custom-call | bytes 1049600 | tf_op jit(solution)/shard_map/pack/pallas_call | solution.py:474
  4.2 0.0 copy-start
  4.2 11.5 %all-to-all-start = ((f32[128,1,4608]{2,1,0:T(1,128)}), f32[128,1,4608]{2,1,0:T(1,128)S(1)}, u32[]{:S(2)}, u32[]{:S(2)}) async-start(f32[128,1,4608]{2,1,0:T(1,128)} %bitcast.14), calls=%async_computation | async-start | bytes 4718592 | tf_op jit(solution)/shard_map/all_to_all | solution.py:529
  15.8 0.0 copy-done
  15.8 1.1 %collective-permute-start = (f32[128,128]{1,0:T(8,128)S(1)}, f32[128,128]{1,0:T(8,128)S(1)}, u32[]{:S(2)}, u32[]{:S(2)}) collective-permute-start(f32[128,128]{1,0:T(8,128)S(1)} %get-tuple-element.37), channel_id=1, source_target_pairs={{0,31},{1,0},{2,1},{3,2},{4,3},{5,4},{6,5},{7,6},{8,7},{9,8},{10,9... | collective-permute-start | bytes 196616 | tf_op jit(solution)/shard_map/ppermute | solution.py:502
  16.9 0.7 collective-permute-start.1
  17.6 31.2 %all-to-all-done = f32[128,1,4608]{2,1,0:T(1,128)S(1)} async-done(((f32[128,1,4608]{2,1,0:T(1,128)}), f32[128,1,4608]{2,1,0:T(1,128)S(1)}, u32[]{:S(2)}, u32[]{:S(2)}) %all-to-all-start) | async-done | bytes 2359328 | tf_op jit(solution)/shard_map/all_to_all | solution.py:529
  48.8 0.7 sums.1
  49.6 0.0 copy-start.1
  49.6 0.0 copy-start.2
  49.6 0.0 copy-start.4
  49.6 0.1 collective-permute-start.4
  49.7 1.4 %collective-permute-start.5 = (f32[64,1152]{1,0:T(8,128)S(1)}, f32[64,1152]{1,0:T(8,128)S(1)}, u32[]{:S(2)}, u32[]{:S(2)}) collective-permute-start(f32[64,1152]{1,0:T(8,128)S(1)} %get-tuple-element.26), channel_id=1, source_target_pairs={{32,64},{64,32},{96,0},{0,96},{33,65},{65,33},{97,1},{1,97},{34,66... | collective-permute-start | bytes 884744 | tf_op jit(solution)/shard_map/ppermute | solution.py:560
  51.1 0.0 collective-permute-done
  51.1 0.0 collective-permute-done.1
  51.1 0.4 weights.1.w_ref
  51.6 0.0 copy-start.5
  51.6 0.0 copy-done.1
  51.6 0.0 copy-done.2
  51.6 0.0 copy-done.4
  51.6 1.4 %early.1 = (f32[128,1152]{1,0:T(8,128)S(1)}, f32[64,1152]{1,0:T(8,128)S(1)}, f32[128,1024]{1,0:T(8,128)S(1)}, f32[128,1024]{1,0:T(8,128)S(1)}, f32[16,128]{1,0:T...) custom-call(f32[128,1152]{1,0:T(8,128)S(1)} %get-tuple-element.21.s_ref, f32[128,1152]{1,0:T(8,128)S(1)} %weights.1.w_ref, ...), custom_call_target="tpu_custom_call" | custom-call | flops 849346560 | bytes 1998848 | tf_op jit(solution)/shard_map/early/pallas_call | solution.py:474
  53.0 0.0 copy-start.3
  53.0 0.3 collective-permute-start.2
  53.3 1.9 %collective-permute-start.3 = (f32[32,1152]{1,0:T(8,128)S(1)}, f32[32,1152]{1,0:T(8,128)S(1)}, u32[]{:S(2)}, u32[]{:S(2)}) collective-permute-start(f32[32,1152]{1,0:T(8,128)S(1)} %get-tuple-element.23), channel_id=1, source_target_pairs={{32,64},{64,32},{96,0},{0,96},{33,65},{65,33},{97,1},{1,97},{34,66... | collective-permute-start | bytes 442376 | tf_op jit(solution)/shard_map/ppermute | solution.py:588
  55.2 1.3 %collective-permute-done.4.near_ref = f32[64,1152]{1,0:T(8,128)S(1)} collective-permute-done((f32[64,1152]{1,0:T(8,128)S(1)}, f32[64,1152]{1,0:T(8,128)S(1)}, u32[]{:S(2)}, u32[]{:S(2)}) %collective-permute-start.4) | collective-permute-done | bytes 294944 | tf_op jit(solution)/shard_map/ppermute | solution.py:560
  56.5 1.0 %collective-permute-done.5.next_ref = f32[64,1152]{1,0:T(8,128)S(1)} collective-permute-done((f32[64,1152]{1,0:T(8,128)S(1)}, f32[64,1152]{1,0:T(8,128)S(1)}, u32[]{:S(2)}, u32[]{:S(2)}) %collective-permute-start.5) | collective-permute-done | bytes 294944 | tf_op jit(solution)/shard_map/ppermute | solution.py:560
  57.5 0.0 copy-done.5
  57.5 1.6 %first.1 = (f32[128,1152]{1,0:T(8,128)S(1)}, f32[16,128]{1,0:T(8,128)S(1)}) custom-call(f32[128,1152]{1,0:T(8,128)S(1)} %get-tuple-element.21.s_ref, f32[64,1152]{1,0:T(8,128)S(1)} %collective-permute-done.4.near_ref, f32[64,1152]{1,0:T(8,128)S(1)} %collective-permute-done.5.next_ref, f32[128,1152]{1,0:T(8,128)S(1)} %get-tuple-element.27.part_ref, ...), custom_call_target="tpu_custom_call" | custom-call | flops 1132462080 | bytes 2564096 | tf_op jit(solution)/shard_map/first/pallas_call | solution.py:474
  59.1 0.6 collective-permute-done.2.near_ref
  59.7 1.0 %collective-permute-done.3.next_ref = f32[32,1152]{1,0:T(8,128)S(1)} collective-permute-done((f32[32,1152]{1,0:T(8,128)S(1)}, f32[32,1152]{1,0:T(8,128)S(1)}, u32[]{:S(2)}, u32[]{:S(2)}) %collective-permute-start.3) | collective-permute-done | bytes 147488 | tf_op jit(solution)/shard_map/ppermute | solution.py:588
  60.7 0.0 copy-done.3
  60.7 1.6 %second.1 = (f32[128,1024]{1,0:T(8,128)S(1)}, f32[128,1024]{1,0:T(8,128)S(1)}, f32[128,128]{1,0:T(8,128)S(1)}) custom-call(f32[128,1152]{1,0:T(8,128)S(1)} %weights.1.w_ref, f32[32,1152]{1,0:T(8,128)S(1)} %collective-permute-done.2.near_ref, f32[32,1152]{1,0:T(8,128)S(1)} %collective-permute-done.3.next_ref, f32[64,1152]{1,0:T(8,128)S(1)} %get-tuple-element.24.deep_ref, ...), custom_call_target="tpu_custom_call" | custom-call | flops 1132462080 | bytes 3448832 | tf_op jit(solution)/shard_map/second/pallas_call | solution.py:474
  62.3 16.1 %all_to_all.10 = f32[128,1,128]{2,1,0:T(1,128)S(1)} all-to-all(f32[128,1,128]{2,1,0:T(1,128)S(1)} %bitcast.13), channel_id=1, replica_groups=mesh['ty'=4,'tx_0'=4,'tx_1'=4,'tx_2'=2] {'ty','tx_0','tx_1','tx_2'}, dimensions={0} | all-to-all | bytes 131072 | tf_op jit(solution)/shard_map/all_to_all | solution.py:622
  78.4 1.4 %combine.1 = (f32[128,1024]{1,0:T(8,128)}, f32[128,1024]{1,0:T(8,128)}) custom-call(f32[128,128]{1,0:T(8,128)S(1)} %bitcast.12, f32[128,1024]{1,0:T(8,128)S(1)} %get-tuple-element.31.r0_ref, f32[128,1024]{1,0:T(8,128)S(1)} %get-tuple-element.34.b0_ref, f32[128,1024]{1,0:T(8,128)S(1)} %get-tuple-element.35.b1_ref), custom_call_target="tpu_custom_call" | custom-call | bytes 1638400 | tf_op jit(solution)/shard_map/combine/pallas_call | solution.py:474
  (3 shorter events, 0.0 us)
Async XLA Ops:
  4.2 11.5 %copy-start = (f32[128,1024]{1,0:T(8,128)S(1)}, f32[128,1024]{1,0:T(8,128)}, u32[]{:S(2)}) copy-start(f32[128,1024]{1,0:T(8,128)} %prior_ref.1) | copy-start | bytes 1572868
  4.2 44.6 %all-to-all-start = ((f32[128,1,4608]{2,1,0:T(1,128)}), f32[128,1,4608]{2,1,0:T(1,128)S(1)}, u32[]{:S(2)}, u32[]{:S(2)}) async-start(f32[128,1,4608]{2,1,0:T(1,128)} %bitcast.14), calls=%async_computation | async-start | bytes 4718592 | tf_op jit(solution)/shard_map/all_to_all | solution.py:529
  15.8 35.3 %collective-permute-start = (f32[128,128]{1,0:T(8,128)S(1)}, f32[128,128]{1,0:T(8,128)S(1)}, u32[]{:S(2)}, u32[]{:S(2)}) collective-permute-start(f32[128,128]{1,0:T(8,128)S(1)} %get-tuple-element.37), channel_id=1, source_target_pairs={{0,31},{1,0},{2,1},{3,2},{4,3},{5,4},{6,5},{7,6},{8,7},{9,8},{10,9... | collective-permute-start | bytes 196616 | tf_op jit(solution)/shard_map/ppermute | solution.py:502
  16.9 34.2 %collective-permute-start.1 = (f32[128,128]{1,0:T(8,128)S(1)}, f32[128,128]{1,0:T(8,128)S(1)}, u32[]{:S(2)}, u32[]{:S(2)}) collective-permute-start(f32[128,128]{1,0:T(8,128)S(1)} %get-tuple-element.36), channel_id=1, source_target_pairs={{0,1},{1,2},{2,3},{3,4},{4,5},{5,6},{6,7},{7,8},{8,9},{9,10},{10,1... | collective-permute-start | bytes 196616 | tf_op jit(solution)/shard_map/ppermute | solution.py:503
  49.6 2.0 %copy-start.1 = (bf16[1024,256]{1,0:T(8,128)(2,1)S(1)}, bf16[1024,256]{1,0:T(8,128)(2,1)}, u32[]{:S(2)}) copy-start(bf16[1024,256]{1,0:T(8,128)(2,1)} %constant.16.clone.col_ref) | copy-start | bytes 1572868
  49.6 2.0 %copy-start.2 = (bf16[768,128]{1,0:T(8,128)(2,1)S(1)}, bf16[768,128]{1,0:T(8,128)(2,1)}, u32[]{:S(2)}) copy-start(bf16[768,128]{1,0:T(8,128)(2,1)} %constant.17.clone.edge_ref) | copy-start | bytes 589828
  49.6 2.0 %copy-start.4 = (bf16[384,128]{1,0:T(8,128)(2,1)S(1)}, bf16[384,128]{1,0:T(8,128)(2,1)}, u32[]{:S(2)}) copy-start(bf16[384,128]{1,0:T(8,128)(2,1)} %constant.18.clone.own_ref) | copy-start | bytes 294916
  49.6 6.9 %collective-permute-start.4 = (f32[64,1152]{1,0:T(8,128)S(1)}, f32[64,1152]{1,0:T(8,128)S(1)}, u32[]{:S(2)}, u32[]{:S(2)}) collective-permute-start(f32[64,1152]{1,0:T(8,128)S(1)} %get-tuple-element.25), channel_id=1, source_target_pairs={{0,32},{32,0},{64,96},{96,64},{1,33},{33,1},{65,97},{97,65},{2,34}... | collective-permute-start | bytes 884744 | tf_op jit(solution)/shard_map/ppermute | solution.py:560
  49.7 7.8 %collective-permute-start.5 = (f32[64,1152]{1,0:T(8,128)S(1)}, f32[64,1152]{1,0:T(8,128)S(1)}, u32[]{:S(2)}, u32[]{:S(2)}) collective-permute-start(f32[64,1152]{1,0:T(8,128)S(1)} %get-tuple-element.26), channel_id=1, source_target_pairs={{32,64},{64,32},{96,0},{0,96},{33,65},{65,33},{97,1},{1,97},{34,66... | collective-permute-start | bytes 884744 | tf_op jit(solution)/shard_map/ppermute | solution.py:560
  51.6 6.0 %copy-start.5 = (bf16[256,128]{1,0:T(8,128)(2,1)S(1)}, bf16[256,128]{1,0:T(8,128)(2,1)}, u32[]{:S(2)}) copy-start(bf16[256,128]{1,0:T(8,128)(2,1)} %constant.19.clone.halo_ref) | copy-start | bytes 196612
  53.0 7.6 %copy-start.3 = (bf16[256,192]{1,0:T(8,128)(2,1)S(1)}, bf16[256,192]{1,0:T(8,128)(2,1)}, u32[]{:S(2)}) copy-start(bf16[256,192]{1,0:T(8,128)(2,1)} %constant.20.clone.row_ref) | copy-start | bytes 294916
  53.0 6.7 %collective-permute-start.2 = (f32[32,1152]{1,0:T(8,128)S(1)}, f32[32,1152]{1,0:T(8,128)S(1)}, u32[]{:S(2)}, u32[]{:S(2)}) collective-permute-start(f32[32,1152]{1,0:T(8,128)S(1)} %get-tuple-element.22), channel_id=1, source_target_pairs={{0,32},{32,0},{64,96},{96,64},{1,33},{33,1},{65,97},{97,65},{2,34}... | collective-permute-start | bytes 442376 | tf_op jit(solution)/shard_map/ppermute | solution.py:588
  53.3 7.3 %collective-permute-start.3 = (f32[32,1152]{1,0:T(8,128)S(1)}, f32[32,1152]{1,0:T(8,128)S(1)}, u32[]{:S(2)}, u32[]{:S(2)}) collective-permute-start(f32[32,1152]{1,0:T(8,128)S(1)} %get-tuple-element.23), channel_id=1, source_target_pairs={{32,64},{64,32},{96,0},{0,96},{33,65},{65,33},{97,1},{1,97},{34,66... | collective-permute-start | bytes 442376 | tf_op jit(solution)/shard_map/ppermute | solution.py:588
